TPU v7x, 32 devices: a whole 2x2x4 slice. The times are simulated.
32 devices in a mesh: seq: 8 (over z, x), tp: 4 (over y, core).
Axes of the slice: x: 2, y: 2, z: 4, core: 2. Of those that a mesh axis runs over, the one named last changes fastest.
Arguments:
- conv_in: bfloat16 [1024, 16384], P('seq', 'tp'), may hold values from -6 to 6
- conv_weight: float32 [4, 16384], P(None, 'tp'), may hold values from -3 to 3
- conv_bias: float32 [16384], P('tp'), may hold values from -0.5 to 0.5
- proj_weight: bfloat16 [16384, 544], P('tp'), may hold values from -0.046875 to 0.046875
- dt_weight: bfloat16 [512, 16384], P(None, 'tp'), may hold values from -0.25 to 0.25
- dt_bias: float32 [16384], P('tp'), may hold values from -6 to -2.5
- decay_rate: float32 [16, 16384], P(None, 'tp'), may hold values from 0.0009765625 to 4
- skip_gain: float32 [16384], P('tp'), may hold values from 0.5 to 1.5
- grad_out: bfloat16 [1024, 16384], P('seq', 'tp'), may hold values from -6 to 6
Outputs:
- mixed: bfloat16 [1024, 16384], P('seq', 'tp')
- weight_grad: float32 [4, 4096, 16], P('tp', 'seq')
All inputs are finite; a program needn't handle non-finite values.
Results may differ from a plain program's by a relative error of at most 0.006.
Values may be sent and summed in bfloat16 or wider, within the bound.
No kernel may reach another device: no remote copies, remote signals or barrier semaphores. Data moves between devices by JAX's collectives and lax.ppermute only.
A program may use at most 128 MiB of HBM per device.

v0:
```python
import jax
import jax.numpy as jnp
from jax import lax
from jax.sharding import PartitionSpec as P

block_len = 16


def shifted(shard, axis, by):
    count = lax.axis_size(axis)
    pairs = [(i, i + by) for i in range(count) if 0 <= i + by < count]
    return lax.ppermute(shard, axis, pairs)


def entering(part, axis, combine, identity):
    place = lax.axis_index(axis)
    gathered = jax.tree.map(lambda a: lax.all_gather(a, axis), part)
    state = jax.tree.map(lambda a, e: jnp.zeros_like(a) + jnp.asarray(e, a.dtype), part, identity)

    def one(turn, state):
        return combine(
            state, jax.tree.map(lambda a: lax.dynamic_index_in_dim(a, turn, 0, False), gathered)
        )

    return lax.fori_loop(0, place, one, state)


def chain_pair(earlier, later):
    return (earlier[0] * later[0], later[0] * earlier[1] + later[1])


def local_pass(initial, decay_rate, slices):

    def block_step(carried, pieces):
        step_now, drive_now, b_now, c_now, grad_now = pieces
        outputs = []
        grads = []
        for offset in range(block_len):
            carried = (
                jnp.exp(-step_now[offset][None, :] * decay_rate) * carried
                + drive_now[offset][None, :] * b_now[offset][:, None]
            )
            outputs.append(jnp.sum(carried * c_now[offset][:, None], axis=0))
            grads.append(jnp.sum(carried * grad_now[offset][None, :], axis=1))
        return (carried, (jnp.stack(outputs), jnp.stack(grads)))

    return lax.scan(block_step, initial, slices)


def local_ending(step_size, drive_in, b_matrix, decay_rate):
    after = jnp.flip(jnp.cumsum(jnp.flip(step_size, 0), axis=0), 0) - step_size
    rows = []
    for state_index in range(decay_rate.shape[0]):
        weights = jnp.exp(-decay_rate[state_index][None, :] * after)
        rows.append(
            jnp.sum(weights * drive_in * b_matrix[:, state_index : state_index + 1], axis=0)
        )
    return jnp.stack(rows)


def on_device(
    conv_in,
    conv_weight,
    conv_bias,
    proj_weight,
    dt_weight,
    dt_bias,
    decay_rate,
    skip_gain,
    grad_out,
):
    tok_rows, channels = conv_in.shape
    taps = conv_weight.shape[0]
    rank_width = dt_weight.shape[0]
    states = decay_rate.shape[0]
    tok_total = tok_rows * lax.axis_size("seq")
    rim_rows = shifted(conv_in[tok_rows - (taps - 1) :], "seq", 1)
    extended = jnp.concatenate([rim_rows, conv_in], axis=0).astype(jnp.float32)
    pre_act = conv_bias[None, :] + jnp.zeros((tok_rows, channels), jnp.float32)
    for tap_index in range(taps):
        pre_act = (
            pre_act + conv_weight[tap_index][None, :] * extended[tap_index : tap_index + tok_rows]
        )
    conv_out = jax.nn.silu(pre_act).astype(jnp.bfloat16)
    partial_proj = jnp.dot(conv_out, proj_weight, preferred_element_type=jnp.float32)
    proj_out = lax.psum(partial_proj, "tp").astype(jnp.bfloat16)
    dt_low = proj_out[:, :rank_width]
    b_matrix = proj_out[:, rank_width : rank_width + states].astype(jnp.float32)
    c_matrix = proj_out[:, rank_width + states :].astype(jnp.float32)
    step_size = jax.nn.softplus(
        jnp.dot(dt_low, dt_weight, preferred_element_type=jnp.float32) + dt_bias[None, :]
    )
    drive_in = step_size * conv_out.astype(jnp.float32)
    scaled_grad = grad_out.astype(jnp.float32) / tok_total
    blocks = tok_rows // block_len
    slices = (
        step_size.reshape(blocks, block_len, channels),
        drive_in.reshape(blocks, block_len, channels),
        b_matrix.reshape(blocks, block_len, states),
        c_matrix.reshape(blocks, block_len, states),
        scaled_grad.reshape(blocks, block_len, channels),
    )
    zero_state = jnp.zeros((states, channels), jnp.float32)
    local_end = local_ending(step_size, drive_in, b_matrix, decay_rate)
    total_decay = jnp.exp(-decay_rate * jnp.sum(step_size, axis=0)[None, :])
    identity = (jnp.ones((states, channels), jnp.float32), zero_state)
    _, incoming = entering((total_decay, local_end), "seq", chain_pair, identity)
    _, (scan_out, grad_parts) = local_pass(incoming, decay_rate, slices)
    mixed = (
        scan_out.reshape(tok_rows, channels) + skip_gain[None, :] * conv_out.astype(jnp.float32)
    ).astype(jnp.bfloat16)
    grad_c = lax.psum(grad_parts.reshape(tok_rows, states), "tp").astype(jnp.bfloat16)
    weight_grad = lax.psum_scatter(
        lax.dot_general(
            conv_out, grad_c, (((0,), (0,)), ((), ())), preferred_element_type=jnp.float32
        ),
        "seq",
        scatter_dimension=0,
        tiled=True,
    )
    return (mixed, weight_grad[None])


def solution(mesh):
    return jax.shard_map(
        on_device,
        mesh=mesh,
        in_specs=(
            P("seq", "tp"),
            P(None, "tp"),
            P("tp"),
            P("tp", None),
            P(None, "tp"),
            P("tp"),
            P(None, "tp"),
            P("tp"),
            P("seq", "tp"),
        ),
        out_specs=(P("seq", "tp"), P("tp", "seq", None)),
        check_vma=False,
    )
```

profile of v0, /device:TPU:0, one launch (start us, length us, event | category | flops | bytes accessed | tf_op | source)
XLA Modules:
  0.0 394.6 jit_solution(8271281646402718323)
XLA Ops:
  8.1 4.9 %collective-permute-start = (bf16[3,4096]{1,0:T(4,128)(2,1)S(1)}, bf16[3,4096]{1,0:T(4,128)(2,1)S(1)}, u32[]{:S(2)}, u32[]{:S(2)}) collective-permute-start(bf16[3,4096]{1,0:T(4,128)(2,1)S(1)} %slice.453), channel_id=1, source_target_pairs={{0,4},{4,8},{8,12},{12,16},{16,20},{20,24},{24,28},{1,5},{5,9},{9,... | collective-permute-start | bytes 73736 | tf_op jit(solution)/shard_map/ppermute | solution.py:12
  13.0 2.4 slice_negate_fusion.15
  15.4 1.1 fusion.57
  16.5 1.7 maximum_convert_fusion
  18.2 1.3 multiply_convert_fusion
  20.5 1.3 fusion.59
  21.9 14.5 %all-reduce.1 = bf16[128,544]{0,1:T(8,128)(2,1)S(1)} all-reduce(f32[128,544]{0,1:T(8,128)S(1)} %fusion.59), channel_id=1, replica_groups=mesh['seq'=8,'tp'=4] {'tp'}, use_global_device_ids=true, to_apply=%region_0.1 | all-reduce | flops 69632 | bytes 417792 | tf_op jit(solution)/shard_map/psum | solution.py:86
  37.0 6.0 %fusion.58 = (f32[4096]{0:T(1024)}, f32[128,4096]{1,0:T(8,128)}) fusion(f32[4096]{0:T(1024)S(1)} %copy-done.14, bf16[512,4096]{1,0:T(8,128)(2,1)} %param.17, bf16[128,544]{0,1:T(8,128)(2,1)S(1)} %all-reduce.1), kind=kOutput, calls=%fused_computation.252 | convolution fusion | flops 541061120 | bytes 6455296 | tf_op jit(solution)/shard_map/dot_general | solution.py:91
  43.0 16.6 %rev.7 = f32[128,4096]{1,0:T(8,128)} reverse(f32[128,4096]{1,0:T(8,128)} %get-tuple-element.359), dimensions={0} | reverse | bytes 4194304 | tf_op jit(solution)/shard_map/jit(_flip)/rev | solution.py:51
  59.6 4.6 %reduce_window_sum.11 = f32[128,4096]{1,0:T(8,128)} reduce-window(f32[128,4096]{1,0:T(8,128)} %rev.7, f32[]{:T(128)} %constant.51.clone.1), window={size=128x1 pad=127_0x0_0}, to_apply=%region_2.3 | reduce-window | flops 66584576 | bytes 4194308 | tf_op jit(solution)/shard_map/jit(cumsum)/reduce_window_sum | solution.py:51
  64.2 16.6 %rev.8 = f32[128,4096]{1,0:T(8,128)} reverse(f32[128,4096]{1,0:T(8,128)} %reduce_window_sum.11), dimensions={0} | reverse | bytes 4194304 | tf_op jit(solution)/shard_map/jit(_flip)/rev | solution.py:51
  80.8 7.7 %multiply_reduce_fusion.32 = (f32[4096]{0:T(1024)}, f32[4096]{0:T(1024)}, f32[4096]{0:T(1024)}, f32[4096]{0:T(1024)}, f32[4096]{0:T(1024)}, /*index=5*/f32[4096]...) fusion(f32[128]{0:T(128)S(1)} %get-tuple-element.343, ...), kind=kLoop, calls=%fused_computation.195 | loop fusion | flops 25133056 | bytes 17125376 | tf_op jit(solution)/shard_map/reduce_sum | solution.py:56
  88.5 4.6 %multiply_reduce_fusion.40 = (f32[4096]{0:T(1024)}, f32[4096]{0:T(1024)}, f32[4096]{0:T(1024)}, f32[4096]{0:T(1024)}, f32[4096]{0:T(1024)}, /*index=5*/f32[4096]{0:T(1024)}, f32[4096]{0:T(1024)}, f32[4096]{0:T(1024)}) fusion(f32[128,4096]{1,0:T(8,128)S(1)} %get-tuple-element.207, f32[128,4096]{1,0:T(8,128)S(1)} %get-tuple-element.206, ...), kind=kLoop, calls=%fused_computation.203 | loop fusion | flops 16744448 | bytes 4460544 | tf_op jit(solution)/shard_map/reduce_sum | solution.py:56
  93.1 3.4 stack.169
  96.6 1.5 multiply_exponential_fusion
  98.2 1.6 convert_multiply_fusion.2
  101.4 44.3 %all-gather.7.cloned.1.call-done = f32[128,4096]{1,0:T(8,128)} async-done(((f32[16,4096]{1,0:T(8,128)}), f32[128,4096]{1,0:T(8,128)}) %all-gather.7.cloned.1.call-update) | async-done | bytes 2097168 | tf_op jit(solution)/shard_map/all_gather | solution.py:17
  145.6 49.8 %all-gather.5.cloned.1.call-done = f32[128,4096]{1,0:T(8,128)} async-done(((f32[16,4096]{1,0:T(8,128)}), f32[128,4096]{1,0:T(8,128)}) %all-gather.5.cloned.1.call-update) | async-done | bytes 2097168 | tf_op jit(solution)/shard_map/all_gather | solution.py:17
  195.7 109.5 %while.27 = (s32[]{:T(128)}, f32[16,4096]{1,0:T(8,128)S(1)}, f32[8,16,4096]{2,1,0:T(8,128)}, f32[8,16,16]{2,1,0:T(8,128)}, f32[8,16,4096]{2,1,0:T(8,128)}, /*ind...) while((s32[]{:T(128)}, f32[16,4096]{1,0:T(8,128)S(1)}, ...), condition=%wide.region_54.55_spmd, body=%wide.region_21.54_spmd.sunk | while | flops 10485521 | bytes 10244477 | solution.py:47
  195.7 3.3 constant_dynamic-slice_fusion.81
  199.2 2.4 fusion.69
  201.7 2.0 multiply_reduce_fusion.53
  204.7 1.0 multiply_reduce_fusion.55
  209.1 3.5 constant_dynamic-slice_fusion.81
  212.8 2.5 fusion.69
  215.3 2.0 multiply_reduce_fusion.53
  222.7 3.6 constant_dynamic-slice_fusion.81
  226.6 2.5 fusion.69
  229.1 2.0 multiply_reduce_fusion.53
  236.6 3.7 constant_dynamic-slice_fusion.81
  240.5 2.5 fusion.69
  243.0 2.0 multiply_reduce_fusion.53
  250.5 3.7 constant_dynamic-slice_fusion.81
  254.3 2.5 fusion.69
  256.8 2.0 multiply_reduce_fusion.53
  264.3 3.4 constant_dynamic-slice_fusion.81
  267.9 2.5 fusion.69
  270.4 2.0 multiply_reduce_fusion.53
  277.8 3.4 constant_dynamic-slice_fusion.81
  281.4 2.5 fusion.69
  283.9 2.0 multiply_reduce_fusion.53
  291.4 3.6 constant_dynamic-slice_fusion.81
  295.2 2.5 fusion.69
  297.8 2.0 multiply_reduce_fusion.53
  305.2 11.2 %psum.15 = bf16[128,16]{1,0:T(8,128)(2,1)S(1)} all-reduce(f32[128,16]{1,0:T(8,128)} %bitcast.509), channel_id=1, replica_groups=mesh['seq'=8,'tp'=4] {'tp'}, use_global_device_ids=true, to_apply=%region_55.56 | all-reduce | flops 2048 | bytes 12288 | tf_op jit(solution)/shard_map/psum | solution.py:112
  316.4 2.2 fusion.60
  318.7 4.0 %fusion.49 = bf16[128,4096]{1,0:T(8,128)(2,1)} fusion(f32[8,16,4096]{2,1,0:T(8,128)} %get-tuple-element.100, f32[4096]{0:T(1024)} %param.20, f32[131,4096]{1,0:T(8,128)S(1)} %maximum_convert_fusion, f32[4096]{0:T(1024)S(1)} %bitcast.503, f32[4096]{0:T(1024)S(1)} %bitcast.506, f32[4096]{0:T(1024)S(1)} %bitcast.500, f32[4096]{0:T(1024)S(1)} %bitcast.497, ...), kind=kLoop, calls=%fused_computation.185 | loop fusion | flops 8912896 | bytes 11632640 | tf_op jit(solution)/shard_map/convert_element_type | solution.py:111
  322.7 65.4 %reduce-scatter.2.cloned.1.call-done = f32[512,16]{0,1:T(8,128)} async-done(((f32[4096,16]{0,1:T(8,128)}), f32[512,16]{0,1:T(8,128)}) %reduce-scatter.2.cloned.1.call-update) | async-done | bytes 32784 | tf_op jit(solution)/shard_map/reduce_scatter | solution.py:113
  (144 shorter events, 48.5 us)
Async XLA Ops:
  7.2 11.0 %copy-start.10 = (f32[4096]{0:T(1024)S(1)}, f32[4096]{0:T(1024)}, u32[]{:S(2)}) copy-start(f32[4096]{0:T(1024)} %param.15) | copy-start | bytes 49156
  7.2 138.5 %all-gather.7.cloned.1.call-start = ((), (), s32[]{:S(2)}) async-start(), calls=%async_computation.3 | async-start | bytes 2359296 | tf_op jit(solution)/shard_map/all_gather | solution.py:17
  8.1 8.4 %collective-permute-start = (bf16[3,4096]{1,0:T(4,128)(2,1)S(1)}, bf16[3,4096]{1,0:T(4,128)(2,1)S(1)}, u32[]{:S(2)}, u32[]{:S(2)}) collective-permute-start(bf16[3,4096]{1,0:T(4,128)(2,1)S(1)} %slice.453), channel_id=1, source_target_pairs={{0,4},{4,8},{8,12},{12,16},{16,20},{20,24},{24,28},{1,5},{5,9},{9,... | collective-permute-start | bytes 73736 | tf_op jit(solution)/shard_map/ppermute | solution.py:12
  16.5 64.3 %copy-start.4 = (f32[1,4096]{1,0:T(1,128)}, f32[1,4096]{1,0:T(1,128)S(1)}, u32[]{:S(2)}) copy-start(f32[1,4096]{1,0:T(1,128)S(1)} %get-tuple-element.339) | copy-start | bytes 49156
  16.5 64.3 %copy-start.6 = (f32[1,4096]{1,0:T(1,128)}, f32[1,4096]{1,0:T(1,128)S(1)}, u32[]{:S(2)}) copy-start(f32[1,4096]{1,0:T(1,128)S(1)} %get-tuple-element.340) | copy-start | bytes 49156
  16.5 64.3 %copy-start.8 = (f32[1,4096]{1,0:T(1,128)}, f32[1,4096]{1,0:T(1,128)S(1)}, u32[]{:S(2)}) copy-start(f32[1,4096]{1,0:T(1,128)S(1)} %get-tuple-element.341) | copy-start | bytes 49156
  16.5 4.0 %slice-start = ((s8[4456448]{0:T(1024)(128)(4,1)}), s8[4194304]{0:T(1024)(128)(4,1)S(1)}, s32[]{:S(2)}) async-start(s8[4456448]{0:T(1024)(128)(4,1)} %bitcast.411), calls=%async_computation.4 | async-start | bytes 8388608
  18.2 2.3 slice-start.1
  19.6 1.0 copy-start.1
  20.5 16.4 %copy-start.14 = (f32[4096]{0:T(1024)S(1)}, f32[4096]{0:T(1024)}, u32[]{:S(2)}) copy-start(f32[4096]{0:T(1024)} %param.18) | copy-start | bytes 49156
  37.0 6.0 %copy-start.12 = (f32[128,16]{0,1:T(8,128)}, f32[128,16]{0,1:T(8,128)S(1)}, u32[]{:S(2)}) copy-start(f32[128,16]{0,1:T(8,128)S(1)} %get-tuple-element.337) | copy-start | bytes 24580
  88.5 4.6 %copy-start.2 = (f32[128,4096]{1,0:T(8,128)}, f32[128,4096]{1,0:T(8,128)S(1)}, u32[]{:S(2)}) copy-start(f32[128,4096]{1,0:T(8,128)S(1)} %get-tuple-element.207) | copy-start | bytes 6291460
  88.5 8.1 %copy-start = (f32[16,4096]{1,0:T(8,128)S(1)}, f32[16,4096]{1,0:T(8,128)}, u32[]{:S(2)}) copy-start(f32[16,4096]{1,0:T(8,128)} %param.19) | copy-start | bytes 786436
  93.1 5.1 %copy-start.3 = (bf16[128,4096]{1,0:T(8,128)(2,1)S(1)}, bf16[128,4096]{1,0:T(8,128)(2,1)}, u32[]{:S(2)}) copy-start(bf16[128,4096]{1,0:T(8,128)(2,1)} %param.21) | copy-start | bytes 3145732
  96.6 98.8 %all-gather.5.cloned.1.call-start = ((), (), s32[]{:S(2)}) async-start(), calls=%async_computation.2 | async-start | bytes 2359296 | tf_op jit(solution)/shard_map/all_gather | solution.py:17
  98.1 290.0 %reduce-scatter.2.cloned.1.call-start = ((), (), s32[]{:S(2)}) async-start(), calls=%async_computation.1 | async-start | bytes 294912 | tf_op jit(solution)/shard_map/reduce_scatter | solution.py:113
  195.7 123.0 %copy-start.5 = (f32[1,4096]{1,0:T(1,128)S(1)}, f32[1,4096]{1,0:T(1,128)}, u32[]{:S(2)}) copy-start(f32[1,4096]{1,0:T(1,128)} %copy-done.4) | copy-start | bytes 49156
  195.7 123.0 %copy-start.7 = (f32[1,4096]{1,0:T(1,128)S(1)}, f32[1,4096]{1,0:T(1,128)}, u32[]{:S(2)}) copy-start(f32[1,4096]{1,0:T(1,128)} %copy-done.6) | copy-start | bytes 49156
  195.7 123.0 %copy-start.9 = (f32[1,4096]{1,0:T(1,128)S(1)}, f32[1,4096]{1,0:T(1,128)}, u32[]{:S(2)}) copy-start(f32[1,4096]{1,0:T(1,128)} %copy-done.8) | copy-start | bytes 49156
  195.7 123.0 %copy-start.11 = (f32[4096]{0:T(1024)S(1)}, f32[4096]{0:T(1024)}, u32[]{:S(2)}) copy-start(f32[4096]{0:T(1024)} %param.15) | copy-start | bytes 49156
  203.6 3.0 copy-start.13
  217.3 3.0 copy-start.13
  231.1 3.0 copy-start.13
  245.0 3.0 copy-start.13
  258.8 3.0 copy-start.13
  272.4 3.0 copy-start.13
  285.9 3.0 copy-start.13
  299.7 3.0 copy-start.13
Sparse Core Ops, SparseCore 0:
  96.7 48.8 all-gather.6
  147.8 47.6 all-gather.4
  318.8 69.2 reduce-scatter.1
where the time goes:
time: 398 us; the launch traced here: 395 us
  waiting for transfers between devices  159 us (40%)
  local copies, waits for them, and re-layouts  90.4 us (23%)
  other arithmetic  89.8 us (23%)
  blocking collectives  25.7 us (6%)
  between operations  14 us (4%)
  matrix products  9.51 us (2%)
  starting transfers between devices  4.99 us (1%)
    all_gather x2, waiting for transfers between devices, entering(): gathered = jax.tree.map(lambda a: lax.all_gather(a, axis), part)  94 us
    reduce_scatter x1, waiting for transfers between devices, on_device(): lax.psum_scatter(lax.dot_general(conv_out, grad_c, (((0,), (0,)), ((), ()...  65.4 us
    reduce_sum x40, other arithmetic, block_step(): grads.append(jnp.sum(carried * grad_now[offset][None, :], axis=1))  39.7 us
    rev x2, local copies, waits for them, and re-layouts, local_ending(): after = jnp.flip(jnp.cumsum(jnp.flip(step_size, 0), axis=0), 0) - step_size  33.2 us
    slice x8, local copies, waits for them, and re-layouts, block_step(): grads.append(jnp.sum(carried * grad_now[offset][None, :], axis=1))  28.2 us
    neg x8, other arithmetic, block_step(): -step_now[offset][None, :] * decay_rate  20 us
    psum x1, blocking collectives, on_device(): proj_out = lax.psum(partial_proj, 'tp').astype(jnp.bfloat16)  14.5 us
    reduce_sum x2, other arithmetic, local_ending(): jnp.sum(weights * drive_in * b_matrix[:, state_index:state_index + 1], ax...  12.3 us
  transfers between devices with their start and end apart: 4, of which 3 were waited for; matrix products, arithmetic and copies ran while one was open for 3% of the time, Pallas kernels for 0%

commit v1 on v0

v1 whole, which is shorter than its diff:
```python
import math

import jax
import jax.numpy as jnp
from jax import lax
from jax.experimental import pallas as pl
from jax.experimental.pallas import tpu as pltpu
from jax.sharding import PartitionSpec as P

LOG2E = math.log2(math.e)
BLOCK = 16
WIDTH = 512
BF = jnp.bfloat16
F4 = jnp.float32
NT = (((1,), (1,)), ((), ()))
TN = (((0,), (0,)), ((), ()))


def swap(a, axis, bit):
    count = lax.axis_size(axis)
    return lax.ppermute(a, axis, [(i, i ^ bit) for i in range(count)])


def params(limit=48 << 20):
    return pltpu.CompilerParams(
        dimension_semantics=("arbitrary",), vmem_limit_bytes=limit
    )


def conv_kernel(x_ref, rim_ref, w_ref, bias_ref, proj_ref, out_ref, part_ref, ext):
    rows = x_ref.shape[0]
    taps = w_ref.shape[0]
    base = 8 - (taps - 1)

    @pl.when(pl.program_id(0) == 0)
    def _():
        part_ref[...] = jnp.zeros_like(part_ref)

    ext[base:8, :] = rim_ref[...].astype(F4)
    ext[8 : 8 + rows, :] = x_ref[...].astype(F4)
    for top in range(0, rows, BLOCK):
        acc = bias_ref[...] + w_ref[0:1, :] * ext[base + top : base + top + BLOCK, :]
        for tap in range(1, taps):
            at = base + top + tap
            acc = acc + w_ref[tap : tap + 1, :] * ext[at : at + BLOCK, :]
        half = 0.5 * acc
        out_ref[top : top + BLOCK, :] = (half + half * jnp.tanh(half)).astype(BF)
    part_ref[...] += jnp.dot(out_ref[...], proj_ref[...], preferred_element_type=F4)


def conv_project(conv_in, rim, conv_weight, conv_bias, proj_weight):
    rows, channels = conv_in.shape
    taps = conv_weight.shape[0]
    wide = proj_weight.shape[1]
    cols = lambda n: pl.BlockSpec((n, WIDTH), lambda i: (0, i))
    return pl.pallas_call(
        conv_kernel,
        grid=(channels // WIDTH,),
        in_specs=[
            cols(rows),
            cols(taps - 1),
            cols(taps),
            cols(1),
            pl.BlockSpec((WIDTH, wide), lambda i: (i, 0)),
        ],
        out_specs=[cols(rows), pl.BlockSpec((rows, wide), lambda i: (0, 0))],
        out_shape=[
            jax.ShapeDtypeStruct((rows, channels), BF),
            jax.ShapeDtypeStruct((rows, wide), F4),
        ],
        scratch_shapes=[pltpu.VMEM((rows + 8, WIDTH), F4)],
        compiler_params=params(),
        name="conv_project",
    )(conv_in, rim, conv_weight, conv_bias[None], proj_weight)


def spread(rows, states):
    wide = BLOCK * states
    lane = lax.broadcasted_iota(jnp.int32, (states, wide), 1)
    pick = (lane % states == lax.broadcasted_iota(jnp.int32, (states, wide), 0)).astype(BF)
    tiled = jnp.dot(rows, pick, preferred_element_type=F4)
    lane = lax.broadcasted_iota(jnp.int32, (BLOCK, wide), 1)
    own = lane // states == lax.broadcasted_iota(jnp.int32, (BLOCK, wide), 0)
    return jnp.where(own, tiled, 0.0).astype(BF)


def softplus(x):
    u = jnp.exp(-jnp.abs(x))
    small = u * (1.0 - u * (0.5 - u * (1.0 / 3.0)))
    return jnp.maximum(x, 0.0) + jnp.where(u < 0.0078125, small, jnp.log(1.0 + u))


def scan_kernel(
    proj_ref, b_ref, c_ref, dtw_ref, dtb_ref, decay_ref, skip_ref, conv_ref, grad_ref,
    mixed_ref, cum_ref, end_ref, total_ref, pairs_ref,
    step, drive, b_wide, c_wide, hist,
):
    rows = conv_ref.shape[0]
    states = decay_ref.shape[0]
    first = pl.program_id(0) == 0

    @pl.when(first)
    def _():
        pairs_ref[...] = jnp.zeros_like(pairs_ref)
        for top in range(0, rows, BLOCK):
            at = slice(top, top + BLOCK)
            c_wide[at, :] = spread(c_ref[at, :], states)
            b_diag = spread(b_ref[at, :], states)
            ones = jnp.ones((BLOCK, 128), BF)
            b_wide[top * states : (top + BLOCK) * states, :] = lax.dot_general(
                b_diag, ones, TN, preferred_element_type=F4
            )

    tri = (
        lax.broadcasted_iota(jnp.int32, (rows, rows), 0)
        >= lax.broadcasted_iota(jnp.int32, (rows, rows), 1)
    ).astype(BF)
    raw = jnp.dot(proj_ref[...], dtw_ref[...], preferred_element_type=F4)
    step[...] = raw + dtb_ref[...]
    for top in range(0, rows, BLOCK):
        at = slice(top, top + BLOCK)
        now = softplus(step[at, :])
        step[at, :] = now
        conv = conv_ref[at, :].astype(F4)
        drive[at, :] = now * conv
        mixed_ref[at, :] = skip_ref[...] * conv
    high = step[...].astype(BF)
    low = (step[...] - high.astype(F4)).astype(BF)
    cum = jnp.dot(tri, high, preferred_element_type=F4)
    cum_ref[...] = cum + jnp.dot(tri, low, preferred_element_type=F4)
    total_ref[...] = cum_ref[rows - 1 : rows, :]

    rate = decay_ref[...] * (-LOG2E)
    state = jnp.zeros((states, WIDTH), F4)
    for top in range(0, rows, BLOCK):
        slot = (top // BLOCK) % 2
        for t in range(BLOCK):
            r = top + t
            decay = jnp.exp2(step[r : r + 1, :] * rate)
            b_now = b_wide[r * states : (r + 1) * states, :]
            b_now = jnp.concatenate([b_now] * (WIDTH // 128), axis=1)
            state = decay * state + drive[r : r + 1, :] * b_now
            hist[slot, t * states : (t + 1) * states, :] = state.astype(BF)
        at = slice(top, top + BLOCK)
        block = hist[slot]
        mixed_ref[at, :] += jnp.dot(c_wide[at, :], block, preferred_element_type=F4)
        pairs_ref[at, :] += lax.dot_general(
            grad_ref[at, :], block, NT, preferred_element_type=F4
        )
    end_ref[...] = state


def local_scan(proj, b_mat, c_mat, dt_weight, dt_bias, decay_rate, skip, conv_out, grad_out):
    rows, channels = conv_out.shape
    rank = dt_weight.shape[0]
    states = decay_rate.shape[0]
    cols = lambda n: pl.BlockSpec((n, WIDTH), lambda i: (0, i))
    whole = lambda a, b: pl.BlockSpec((a, b), lambda i: (0, 0))
    return pl.pallas_call(
        scan_kernel,
        grid=(channels // WIDTH,),
        in_specs=[
            whole(rows, rank),
            whole(rows, states),
            whole(rows, states),
            cols(rank),
            cols(1),
            cols(states),
            cols(1),
            cols(rows),
            cols(rows),
        ],
        out_specs=[
            cols(rows),
            cols(rows),
            cols(states),
            cols(1),
            whole(rows, BLOCK * states),
        ],
        out_shape=[
            jax.ShapeDtypeStruct((rows, channels), F4),
            jax.ShapeDtypeStruct((rows, channels), F4),
            jax.ShapeDtypeStruct((states, channels), F4),
            jax.ShapeDtypeStruct((1, channels), F4),
            jax.ShapeDtypeStruct((rows, BLOCK * states), F4),
        ],
        scratch_shapes=[
            pltpu.VMEM((rows, WIDTH), F4),
            pltpu.VMEM((rows, WIDTH), F4),
            pltpu.VMEM((rows * states, 128), F4),
            pltpu.VMEM((rows, BLOCK * states), BF),
            pltpu.VMEM((2, BLOCK * states, WIDTH), BF),
        ],
        compiler_params=params(),
        name="local_scan",
    )(proj, b_mat, c_mat, dt_weight, dt_bias[None], decay_rate, skip[None], conv_out, grad_out)


def carry_kernel(
    scale, c_ref, decay_ref, state_ref, cum_ref, mixed_ref, grad_ref, pairs_in,
    out_ref, gradc_ref,
    c_wide, pairs, hist,
):
    rows = cum_ref.shape[0]
    states = decay_ref.shape[0]

    @pl.when(pl.program_id(0) == 0)
    def _():
        pairs[...] = pairs_in[...]
        for top in range(0, rows, BLOCK):
            at = slice(top, top + BLOCK)
            c_wide[at, :] = spread(c_ref[at, :], states)

    rate = decay_ref[...] * (-LOG2E)
    state = state_ref[...]
    for top in range(0, rows, BLOCK):
        slot = (top // BLOCK) % 2
        for t in range(BLOCK):
            r = top + t
            now = jnp.exp2(cum_ref[r : r + 1, :] * rate) * state
            hist[slot, t * states : (t + 1) * states, :] = now.astype(BF)
        at = slice(top, top + BLOCK)
        block = hist[slot]
        more = jnp.dot(c_wide[at, :], block, preferred_element_type=F4)
        out_ref[at, :] = (mixed_ref[at, :] + more).astype(BF)
        pairs[at, :] += lax.dot_general(
            grad_ref[at, :], block, NT, preferred_element_type=F4
        )

    @pl.when(pl.program_id(0) == pl.num_programs(0) - 1)
    def _():
        wide = BLOCK * states
        shape = (rows, wide)
        lane = lax.broadcasted_iota(jnp.int32, shape, 1)
        row = lax.broadcasted_iota(jnp.int32, shape, 0)
        kept = jnp.where(lane // states == row % BLOCK, pairs[...], 0.0) * scale
        pick = (
            lax.broadcasted_iota(jnp.int32, (states, wide), 1) % states
            == lax.broadcasted_iota(jnp.int32, (states, wide), 0)
        ).astype(F4)
        gradc_ref[...] = lax.dot_general(
            pick, kept, NT, preferred_element_type=F4, precision=lax.Precision.HIGHEST
        )


def add_carry(scale, c_mat, decay_rate, incoming, cum, mixed, grad_out, pairs):
    rows, channels = cum.shape
    states = decay_rate.shape[0]
    cols = lambda n: pl.BlockSpec((n, WIDTH), lambda i: (0, i))
    whole = lambda a, b: pl.BlockSpec((a, b), lambda i: (0, 0))

    def body(*refs):
        carry_kernel(scale, *refs)

    return pl.pallas_call(
        body,
        grid=(channels // WIDTH,),
        in_specs=[
            whole(rows, states),
            cols(states),
            cols(states),
            cols(rows),
            cols(rows),
            cols(rows),
            whole(rows, BLOCK * states),
        ],
        out_specs=[cols(rows), whole(states, rows)],
        out_shape=[
            jax.ShapeDtypeStruct((rows, channels), BF),
            jax.ShapeDtypeStruct((states, rows), F4),
        ],
        scratch_shapes=[
            pltpu.VMEM((rows, BLOCK * states), BF),
            pltpu.VMEM((rows, BLOCK * states), F4),
            pltpu.VMEM((2, BLOCK * states, WIDTH), BF),
        ],
        compiler_params=params(),
        name="add_carry",
    )(c_mat, decay_rate, incoming, cum, mixed, grad_out, pairs)


def incoming_state(end, total, decay_rate):
    count = lax.axis_size("seq")
    place = lax.axis_index("seq")
    prefix = jnp.zeros_like(end)
    prefix_sum = jnp.zeros_like(total)
    fade = lambda s: jnp.exp(-decay_rate * s)
    bit = 1
    while bit < count:
        other = swap(end.astype(BF), "seq", bit).astype(F4)
        other_sum = swap(total, "seq", bit)
        later = (place & bit) != 0
        prefix = jnp.where(later, prefix + fade(prefix_sum) * other, prefix)
        prefix_sum = jnp.where(later, prefix_sum + other_sum, prefix_sum)
        end = jnp.where(later, end + fade(total) * other, other + fade(other_sum) * end)
        total = total + other_sum
        bit *= 2
    return prefix


def on_device(
    conv_in,
    conv_weight,
    conv_bias,
    proj_weight,
    dt_weight,
    dt_bias,
    decay_rate,
    skip_gain,
    grad_out,
):
    rows, channels = conv_in.shape
    taps = conv_weight.shape[0]
    rank = dt_weight.shape[0]
    states = decay_rate.shape[0]
    count = lax.axis_size("seq")
    tp = lax.axis_size("tp")
    rim = lax.ppermute(
        conv_in[rows - (taps - 1) :], "seq", [(i, i + 1) for i in range(count - 1)]
    )
    conv_out, part = conv_project(conv_in, rim, conv_weight, conv_bias, proj_weight)
    bit = 1
    while bit < tp:
        mine = part if bit == 1 else part.astype(BF)
        part = mine.astype(F4) + swap(mine, "tp", bit).astype(F4)
        bit *= 2
    proj = part.astype(BF)
    dt_low = proj[:, :rank]
    b_mat = proj[:, rank : rank + states]
    c_mat = proj[:, rank + states :]
    mixed, cum, end, total, pairs = local_scan(
        dt_low, b_mat, c_mat, dt_weight, dt_bias, decay_rate, skip_gain, conv_out, grad_out
    )
    incoming = incoming_state(end, total, decay_rate)
    scale = 1.0 / (rows * count)
    mixed, grad_c = add_carry(
        scale, c_mat, decay_rate, incoming, cum, mixed, grad_out, pairs
    )
    parts = [grad_c] + [swap(grad_c, "tp", k) for k in range(1, tp)]
    grad_c = sum(parts[1:], parts[0]).astype(BF)
    weight = jnp.dot(grad_c, conv_out, preferred_element_type=F4).astype(BF)
    share = channels // count
    weight = weight.reshape(states, count, share).transpose(1, 0, 2)
    weight = lax.all_to_all(weight, "seq", 0, 0)
    weight_grad = jnp.sum(weight.astype(F4), axis=0).T
    return (mixed, weight_grad[None])


def solution(mesh):
    return jax.shard_map(
        on_device,
        mesh=mesh,
        in_specs=(
            P("seq", "tp"),
            P(None, "tp"),
            P("tp"),
            P("tp", None),
            P(None, "tp"),
            P("tp"),
            P(None, "tp"),
            P("tp"),
            P("seq", "tp"),
        ),
        out_specs=(P("seq", "tp"), P("tp", "seq", None)),
        check_vma=False,
    )
```

time: 398 us -> 96.6 us (0.24)
  waiting for transfers between devices: 159 us -> 19.2 us
  other arithmetic: 89.8 us -> 1.32 us
  local copies, waits for them, and re-layouts: 90.4 us -> 13 us
  Pallas kernels: 0 us -> 33.8 us
  blocking collectives: 25.7 us -> 12 us
  between operations: 14 us -> 0.81 us
  starting transfers between devices: 4.99 us -> 15.5 us
  matrix products: 9.51 us -> 0.25 us
    all_gather x2 -> x0, waiting for transfers between devices: 94 us -> none  [entering(): gathered = jax.tree.map(lambda a: lax.all_gather(a, axis), part)]
    reduce_scatter x1 -> x0, waiting for transfers between devices: 65.4 us -> none  [on_device(): lax.psum_scatter(lax.dot_general(conv_out, grad_c, (((0,), (0,)), ((), ()...]
    reduce_sum x42 -> x1, other arithmetic: 52.1 us -> 0.63 us  [on_device(): weight_grad = jnp.sum(weight.astype(F4), axis=0).T]
    pallas_call x0 -> x3, Pallas kernels: none -> 33.8 us  [the longest x1 16.1 us: local_scan(): pl.pallas_call(scan_kernel, grid=(channels // WIDTH,), in_specs=[whole(ro...]
    rev x2 -> x0, local copies, waits for them, and re-layouts: 33.2 us -> none  [local_ending(): after = jnp.flip(jnp.cumsum(jnp.flip(step_size, 0), axis=0), 0) - step_size]
    slice x10 -> x3, local copies, waits for them, and re-layouts: 30.1 us -> 0.95 us  [the longest x1 0.86 us: on_device(): conv_in[rows - (taps - 1):]]
    psum x2 -> x0, blocking collectives: 25.7 us -> none  [the longest x1 14.5 us: on_device(): proj_out = lax.psum(partial_proj, 'tp').astype(jnp.bfloat16)]
    neg x9 -> x0, other arithmetic: 22.4 us -> none  [the longest x8 20 us: block_step(): -step_now[offset][None, :] * decay_rate]
  transfers between devices with their start and end apart: 4 -> 11, of which waited for: 3 -> 7; matrix products, arithmetic and copies ran while one was open for 3% -> 8% of each run, Pallas kernels for 0% -> 0%
where the time goes in v1:
time: 96.6 us; the launch traced here: 96 us
  Pallas kernels  33.8 us (35%)
  waiting for transfers between devices  19.2 us (20%)
  starting transfers between devices  15.5 us (16%)
  local copies, waits for them, and re-layouts  13 us (13%)
  blocking collectives  12 us (12%)
  other arithmetic  1.32 us (1%)
    ppermute x10, waiting for transfers between devices, swap(): return lax.ppermute(a, axis, [(i, i ^ bit) for i in range(count)])  19.2 us
    pallas_call x1, Pallas kernels, local_scan(): pl.pallas_call(scan_kernel, grid=(channels // WIDTH,), in_specs=[whole(ro...  16.1 us
    unnamed x21, local copies, waits for them, and re-layouts  12.1 us
    all_to_all x1, blocking collectives, on_device(): weight = lax.all_to_all(weight, 'seq', 0, 0)  12 us
    ppermute x10, starting transfers between devices, swap(): return lax.ppermute(a, axis, [(i, i ^ bit) for i in range(count)])  10.5 us
    pallas_call x1, Pallas kernels, add_carry(): pl.pallas_call(body, grid=(channels // WIDTH,), in_specs=[whole(rows, sta...  10.5 us
    pallas_call x1, Pallas kernels, conv_project(): pl.pallas_call(conv_kernel, grid=(channels // WIDTH,), in_specs=[cols(row...  7.22 us
    ppermute x1, starting transfers between devices, on_device(): lax.ppermute(conv_in[rows - (taps - 1):], 'seq', [(i, i + 1) for i in ran...  5 us
  transfers between devices with their start and end apart: 11, of which 7 were waited for; matrix products, arithmetic and copies ran while one was open for 8% of the time, Pallas kernels for 0%

profile of v1, /device:TPU:0, one launch (start us, length us, event | category | flops | bytes accessed | tf_op | source)
XLA Modules:
  0.0 96.0 jit_solution(18352133995197946189)
XLA Ops:
  0.6 0.9 slice.12
  1.5 0.0 copy-start.5
  1.5 0.0 copy-start.6
  1.5 0.0 copy-start.7
  1.5 5.0 %collective-permute-start = (bf16[3,4096]{1,0:T(4,128)(2,1)S(1)}, bf16[3,4096]{1,0:T(4,128)(2,1)S(1)}, u32[]{:S(2)}, u32[]{:S(2)}) collective-permute-start(bf16[3,4096]{1,0:T(4,128)(2,1)S(1)} %slice.12), channel_id=1, source_target_pairs={{0,4},{4,8},{8,12},{12,16},{16,20},{20,24},{24,28},{1,5},{5,9},{9,... | collective-permute-start | bytes 73736 | tf_op jit(solution)/shard_map/ppermute | solution.py:318
  6.5 7.6 %copy.12.proj_ref = bf16[4096,544]{1,0:T(8,128)(2,1)} copy(bf16[4096,544]{0,1:T(8,128)(2,1)} %param.12) | data formatting | bytes 8912896 | tf_op args[3]
  14.1 0.0 collective-permute-done.rim_ref
  14.1 0.0 copy-done.5
  14.1 0.0 copy-done.6
  14.1 0.0 copy-done.7
  14.1 7.2 %conv_project.1 = (bf16[128,4096]{1,0:T(8,128)(2,1)S(1)}, f32[128,544]{1,0:T(8,128)S(1)}) custom-call(bf16[128,4096]{1,0:T(8,128)(2,1)S(1)} %copy-done.5, bf16[3,4096]{1,0:T(4,128)(2,1)S(1)} %collective-permute-done.rim_ref, f32[4,4096]{1,0:T(4,128)S(1)} %copy-done.6, f32[1,4096]{1,0:T(1,128)S(1)} %bitcast.22, bf16[4096,544]{1,0:T(8,128)(2,1)} %copy.12.proj_ref), custom_call_target="tpu_custom_call" | custom-call | tf_op jit(solution)/shard_map/conv_project/pallas_call | solution.py:56
  21.4 0.1 collective-permute-start.1
  21.5 1.6 %collective-permute-done.1 = f32[128,544]{1,0:T(8,128)S(1)} collective-permute-done((f32[128,544]{1,0:T(8,128)S(1)}, f32[128,544]{1,0:T(8,128)S(1)}, u32[]{:S(2)}, u32[]{:S(2)}) %collective-permute-start.1) | collective-permute-done | bytes 278560 | tf_op jit(solution)/shard_map/ppermute | solution.py:21
  23.1 1.6 %collective-permute-start.2 = (bf16[128,544]{1,0:T(8,128)(2,1)S(1)}, bf16[128,544]{1,0:T(8,128)(2,1)S(1)}, u32[]{:S(2)}, u32[]{:S(2)}) collective-permute-start(bf16[128,544]{1,0:T(8,128)(2,1)S(1)} %add_convert_fusion.1), channel_id=1, source_target_pairs={{0,2},{1,3},{2,0},{3,1},{4,6},{5,7},{6,4},{7,5},{8,10},{9,11},{10,... | collective-permute-start | bytes 417800 | tf_op jit(solution)/shard_map/ppermute | solution.py:21
  24.7 4.7 %collective-permute-done.2 = bf16[128,544]{1,0:T(8,128)(2,1)S(1)} collective-permute-done((bf16[128,544]{1,0:T(8,128)(2,1)S(1)}, bf16[128,544]{1,0:T(8,128)(2,1)S(1)}, u32[]{:S(2)}, u32[]{:S(2)}) %collective-permute-start.2) | collective-permute-done | bytes 139296 | tf_op jit(solution)/shard_map/ppermute | solution.py:21
  29.5 0.1 fusion.7
  29.6 0.0 copy-done
  29.6 0.0 copy-done.1
  29.6 0.0 copy-done.8
  29.6 0.0 copy-done.9
  29.6 16.1 %local_scan.1 = (f32[128,4096]{1,0:T(8,128)S(1)}, f32[128,4096]{1,0:T(8,128)}, f32[16,4096]{1,0:T(8,128)S(1)}, f32[1,4096]{1,0:T(1,128)S(1)}, f32[128,256]{1,0:T(8,128)S(1)}) custom-call(bf16[128,512]{1,0:T(8,128)(2,1)S(1)} %slice.17.proj_ref, bf16[128,16]{1,0:T(8,128)(2,1)S(1)} %get-tuple-element.22.b_ref, ...), custom_call_target="tpu_custom_call" | custom-call | tf_op jit(solution)/shard_map/local_scan/pallas_call | solution.py:159
  45.7 1.3 %copy-done.2 = f32[128,4096]{1,0:T(8,128)} copy-done((f32[128,4096]{1,0:T(8,128)}, f32[128,4096]{1,0:T(8,128)S(1)}, u32[]{:S(2)}) %copy-start.2) | copy-done | bytes 2097176
  47.0 1.6 %collective-permute-start.3 = (bf16[16,4096]{1,0:T(8,128)(2,1)S(1)}, bf16[16,4096]{1,0:T(8,128)(2,1)S(1)}, u32[]{:S(2)}, u32[]{:S(2)}) collective-permute-start(bf16[16,4096]{1,0:T(8,128)(2,1)S(1)} %convert_element_type.43), channel_id=1, source_target_pairs={{0,4},{4,0},{8,12},{12,8},{16,20},{20,16},{24,28},{28,24},{1,5},{5... | collective-permute-start | bytes 393224 | tf_op jit(solution)/shard_map/ppermute | solution.py:21
  48.6 0.5 collective-permute-start.4
  49.1 3.3 %collective-permute-done.4 = f32[1,4096]{1,0:T(1,128)S(1)} collective-permute-done((f32[1,4096]{1,0:T(1,128)S(1)}, f32[1,4096]{1,0:T(1,128)S(1)}, u32[]{:S(2)}, u32[]{:S(2)}) %collective-permute-start.4) | collective-permute-done | bytes 16416 | tf_op jit(solution)/shard_map/ppermute | solution.py:21
  52.4 0.0 collective-permute-done.3
  52.4 0.1 fusion.6
  52.5 1.6 %collective-permute-start.5 = (bf16[16,4096]{1,0:T(8,128)(2,1)S(1)}, bf16[16,4096]{1,0:T(8,128)(2,1)S(1)}, u32[]{:S(2)}, u32[]{:S(2)}) collective-permute-start(bf16[16,4096]{1,0:T(8,128)(2,1)S(1)} %fusion.6), channel_id=1, source_target_pairs={{0,8},{4,12},{8,0},{12,4},{16,24},{20,28},{24,16},{28,20},{1,9},{5... | collective-permute-start | bytes 393224 | tf_op jit(solution)/shard_map/ppermute | solution.py:21
  54.2 0.5 collective-permute-start.6
  54.7 3.3 %collective-permute-done.6 = f32[1,4096]{1,0:T(1,128)S(1)} collective-permute-done((f32[1,4096]{1,0:T(1,128)S(1)}, f32[1,4096]{1,0:T(1,128)S(1)}, u32[]{:S(2)}, u32[]{:S(2)}) %collective-permute-start.6) | collective-permute-done | bytes 16416 | tf_op jit(solution)/shard_map/ppermute | solution.py:21
  58.0 0.0 collective-permute-done.5
  58.0 0.2 fusion.5
  58.2 2.8 %collective-permute-start.7 = (bf16[16,4096]{1,0:T(8,128)(2,1)S(1)}, bf16[16,4096]{1,0:T(8,128)(2,1)S(1)}, u32[]{:S(2)}, u32[]{:S(2)}) collective-permute-start(bf16[16,4096]{1,0:T(8,128)(2,1)S(1)} %fusion.5), channel_id=1, source_target_pairs={{0,16},{4,20},{8,24},{12,28},{16,0},{20,4},{24,8},{28,12},{1,17},{... | collective-permute-start | bytes 393224 | tf_op jit(solution)/shard_map/ppermute | solution.py:21
  61.0 4.5 %collective-permute-done.7 = bf16[16,4096]{1,0:T(8,128)(2,1)S(1)} collective-permute-done((bf16[16,4096]{1,0:T(8,128)(2,1)S(1)}, bf16[16,4096]{1,0:T(8,128)(2,1)S(1)}, u32[]{:S(2)}, u32[]{:S(2)}) %collective-permute-start.7) | collective-permute-done | bytes 131104 | tf_op jit(solution)/shard_map/ppermute | solution.py:21
  65.5 0.2 add_select_fusion.refs_2_
  65.7 0.0 copy-start.3
  65.7 1.6 %copy-done.3 = f32[128,4096]{1,0:T(8,128)S(1)} copy-done((f32[128,4096]{1,0:T(8,128)S(1)}, f32[128,4096]{1,0:T(8,128)}, u32[]{:S(2)}) %copy-start.3) | copy-done | bytes 2097176
  67.3 1.6 %copy-done.4 = f32[128,4096]{1,0:T(8,128)S(1)} copy-done((f32[128,4096]{1,0:T(8,128)S(1)}, f32[128,4096]{1,0:T(8,128)}, u32[]{:S(2)}) %copy-start.4) | copy-done | bytes 2097176
  68.9 10.5 %add_carry.1 = (bf16[128,4096]{1,0:T(8,128)(2,1)}, f32[16,128]{1,0:T(8,128)S(1)}) custom-call(bf16[128,16]{1,0:T(8,128)(2,1)S(1)} %get-tuple-element.23.c_ref.refs_0_, f32[16,4096]{1,0:T(8,128)S(1)} %copy-done, f32[16,4096]{1,0:T(8,128)S(1)} %add_select_fusion.refs_2_, f32[128,4096]{1,0:T(8,128)S(1)} %copy-done.4, f32[128,4096]{1,0:T(8,128)S(1)} %copy-done.3, ...), custom_call_target="tpu_custom_call" | custom-call | tf_op jit(solution)/shard_map/add_carry/pallas_call | solution.py:255
  79.4 0.0 collective-permute-start.10
  79.4 1.5 %collective-permute-start.9 = (f32[16,128]{1,0:T(8,128)S(1)}, f32[16,128]{1,0:T(8,128)S(1)}, u32[]{:S(2)}, u32[]{:S(2)}) collective-permute-start(f32[16,128]{1,0:T(8,128)S(1)} %get-tuple-element.19), channel_id=1, source_target_pairs={{0,2},{1,3},{2,0},{3,1},{4,6},{5,7},{6,4},{7,5},{8,10},{9,11},{10,... | collective-permute-start | bytes 24584 | tf_op jit(solution)/shard_map/ppermute | solution.py:21
  81.0 0.3 collective-permute-start.8
  81.3 1.2 %collective-permute-done.10 = f32[16,128]{1,0:T(8,128)S(1)} collective-permute-done((f32[16,128]{1,0:T(8,128)S(1)}, f32[16,128]{1,0:T(8,128)S(1)}, u32[]{:S(2)}, u32[]{:S(2)}) %collective-permute-start.10) | collective-permute-done | bytes 8224 | tf_op jit(solution)/shard_map/ppermute | solution.py:21
  82.5 0.6 collective-permute-done.9
  83.1 0.0 collective-permute-done.8
  83.1 0.2 convolution_convert_fusion
  83.4 12.0 %all_to_all.5 = bf16[8,16,512]{2,1,0:T(8,128)(2,1)S(1)} all-to-all(bf16[8,16,512]{2,1,0:T(8,128)(2,1)S(1)} %bitcast.26), channel_id=1, replica_groups=mesh['seq'=8,'tp'=4] {'seq'}, dimensions={0} | all-to-all | bytes 262144 | tf_op jit(solution)/shard_map/all_to_all | solution.py:344
  95.4 0.6 convert_reduce_fusion
  (13 shorter events, 0.2 us)
Async XLA Ops:
  1.5 12.6 %copy-start.5 = (bf16[128,4096]{1,0:T(8,128)(2,1)S(1)}, bf16[128,4096]{1,0:T(8,128)(2,1)}, u32[]{:S(2)}) copy-start(bf16[128,4096]{1,0:T(8,128)(2,1)} %x_ref.1) | copy-start | bytes 3145732
  1.5 12.6 %copy-start.6 = (f32[4,4096]{1,0:T(4,128)S(1)}, f32[4,4096]{1,0:T(4,128)}, u32[]{:S(2)}) copy-start(f32[4,4096]{1,0:T(4,128)} %w_ref.1) | copy-start | bytes 196612
  1.5 12.6 %copy-start.7 = (f32[4096]{0:T(1024)S(1)}, f32[4096]{0:T(1024)}, u32[]{:S(2)}) copy-start(f32[4096]{0:T(1024)} %param.11) | copy-start | bytes 49156
  1.5 12.6 %collective-permute-start = (bf16[3,4096]{1,0:T(4,128)(2,1)S(1)}, bf16[3,4096]{1,0:T(4,128)(2,1)S(1)}, u32[]{:S(2)}, u32[]{:S(2)}) collective-permute-start(bf16[3,4096]{1,0:T(4,128)(2,1)S(1)} %slice.12), channel_id=1, source_target_pairs={{0,4},{4,8},{8,12},{12,16},{16,20},{20,24},{24,28},{1,5},{5,9},{9,... | collective-permute-start | bytes 73736 | tf_op jit(solution)/shard_map/ppermute | solution.py:318
  14.1 15.5 %copy-start = (f32[16,4096]{1,0:T(8,128)S(1)}, f32[16,4096]{1,0:T(8,128)}, u32[]{:S(2)}) copy-start(f32[16,4096]{1,0:T(8,128)} %refs_1_.1) | copy-start | bytes 786436
  14.1 15.5 %copy-start.1 = (bf16[128,4096]{1,0:T(8,128)(2,1)S(1)}, bf16[128,4096]{1,0:T(8,128)(2,1)}, u32[]{:S(2)}) copy-start(bf16[128,4096]{1,0:T(8,128)(2,1)} %refs_5_.1) | copy-start | bytes 3145732
  14.1 15.5 %copy-start.8 = (f32[4096]{0:T(1024)S(1)}, f32[4096]{0:T(1024)}, u32[]{:S(2)}) copy-start(f32[4096]{0:T(1024)} %param.14) | copy-start | bytes 49156
  14.1 15.5 %copy-start.9 = (f32[4096]{0:T(1024)S(1)}, f32[4096]{0:T(1024)}, u32[]{:S(2)}) copy-start(f32[4096]{0:T(1024)} %param.16) | copy-start | bytes 49156
  21.4 1.7 %collective-permute-start.1 = (f32[128,544]{1,0:T(8,128)S(1)}, f32[128,544]{1,0:T(8,128)S(1)}, u32[]{:S(2)}, u32[]{:S(2)}) collective-permute-start(f32[128,544]{1,0:T(8,128)S(1)} %get-tuple-element.11), channel_id=1, source_target_pairs={{0,1},{1,0},{2,3},{3,2},{4,5},{5,4},{6,7},{7,6},{8,9},{9,8},{10,11... | collective-permute-start | bytes 835592 | tf_op jit(solution)/shard_map/ppermute | solution.py:21
  23.1 6.3 %collective-permute-start.2 = (bf16[128,544]{1,0:T(8,128)(2,1)S(1)}, bf16[128,544]{1,0:T(8,128)(2,1)S(1)}, u32[]{:S(2)}, u32[]{:S(2)}) collective-permute-start(bf16[128,544]{1,0:T(8,128)(2,1)S(1)} %add_convert_fusion.1), channel_id=1, source_target_pairs={{0,2},{1,3},{2,0},{3,1},{4,6},{5,7},{6,4},{7,5},{8,10},{9,11},{10,... | collective-permute-start | bytes 417800 | tf_op jit(solution)/shard_map/ppermute | solution.py:21
  45.7 1.3 %copy-start.2 = (f32[128,4096]{1,0:T(8,128)}, f32[128,4096]{1,0:T(8,128)S(1)}, u32[]{:S(2)}) copy-start(f32[128,4096]{1,0:T(8,128)S(1)} %get-tuple-element.16.refs_4_) | copy-start | bytes 6291460
  47.0 5.4 %collective-permute-start.3 = (bf16[16,4096]{1,0:T(8,128)(2,1)S(1)}, bf16[16,4096]{1,0:T(8,128)(2,1)S(1)}, u32[]{:S(2)}, u32[]{:S(2)}) collective-permute-start(bf16[16,4096]{1,0:T(8,128)(2,1)S(1)} %convert_element_type.43), channel_id=1, source_target_pairs={{0,4},{4,0},{8,12},{12,8},{16,20},{20,16},{24,28},{28,24},{1,5},{5... | collective-permute-start | bytes 393224 | tf_op jit(solution)/shard_map/ppermute | solution.py:21
  48.6 3.7 %collective-permute-start.4 = (f32[1,4096]{1,0:T(1,128)S(1)}, f32[1,4096]{1,0:T(1,128)S(1)}, u32[]{:S(2)}, u32[]{:S(2)}) collective-permute-start(f32[1,4096]{1,0:T(1,128)S(1)} %get-tuple-element.14), channel_id=1, source_target_pairs={{0,4},{4,0},{8,12},{12,8},{16,20},{20,16},{24,28},{28,24},{1,5},{5... | collective-permute-start | bytes 49160 | tf_op jit(solution)/shard_map/ppermute | solution.py:21
  52.5 5.5 %collective-permute-start.5 = (bf16[16,4096]{1,0:T(8,128)(2,1)S(1)}, bf16[16,4096]{1,0:T(8,128)(2,1)S(1)}, u32[]{:S(2)}, u32[]{:S(2)}) collective-permute-start(bf16[16,4096]{1,0:T(8,128)(2,1)S(1)} %fusion.6), channel_id=1, source_target_pairs={{0,8},{4,12},{8,0},{12,4},{16,24},{20,28},{24,16},{28,20},{1,9},{5... | collective-permute-start | bytes 393224 | tf_op jit(solution)/shard_map/ppermute | solution.py:21
  54.2 3.8 %collective-permute-start.6 = (f32[1,4096]{1,0:T(1,128)S(1)}, f32[1,4096]{1,0:T(1,128)S(1)}, u32[]{:S(2)}, u32[]{:S(2)}) collective-permute-start(f32[1,4096]{1,0:T(1,128)S(1)} %add.44), channel_id=1, source_target_pairs={{0,8},{4,12},{8,0},{12,4},{16,24},{20,28},{24,16},{28,20},{1,9},{5... | collective-permute-start | bytes 49160 | tf_op jit(solution)/shard_map/ppermute | solution.py:21
  58.2 7.3 %collective-permute-start.7 = (bf16[16,4096]{1,0:T(8,128)(2,1)S(1)}, bf16[16,4096]{1,0:T(8,128)(2,1)S(1)}, u32[]{:S(2)}, u32[]{:S(2)}) collective-permute-start(bf16[16,4096]{1,0:T(8,128)(2,1)S(1)} %fusion.5), channel_id=1, source_target_pairs={{0,16},{4,20},{8,24},{12,28},{16,0},{20,4},{24,8},{28,12},{1,17},{... | collective-permute-start | bytes 393224 | tf_op jit(solution)/shard_map/ppermute | solution.py:21
  65.7 1.6 %copy-start.3 = (f32[128,4096]{1,0:T(8,128)S(1)}, f32[128,4096]{1,0:T(8,128)}, u32[]{:S(2)}) copy-start(f32[128,4096]{1,0:T(8,128)} %copy-done.2) | copy-start | bytes 6291460
  67.3 1.6 %copy-start.4 = (f32[128,4096]{1,0:T(8,128)S(1)}, f32[128,4096]{1,0:T(8,128)}, u32[]{:S(2)}) copy-start(f32[128,4096]{1,0:T(8,128)} %get-tuple-element.15.refs_3_) | copy-start | bytes 6291460
  79.4 3.1 %collective-permute-start.10 = (f32[16,128]{1,0:T(8,128)S(1)}, f32[16,128]{1,0:T(8,128)S(1)}, u32[]{:S(2)}, u32[]{:S(2)}) collective-permute-start(f32[16,128]{1,0:T(8,128)S(1)} %get-tuple-element.19), channel_id=1, source_target_pairs={{0,3},{1,2},{2,1},{3,0},{4,7},{5,6},{6,5},{7,4},{8,11},{9,10},{10,... | collective-permute-start | bytes 24584 | tf_op jit(solution)/shard_map/ppermute | solution.py:21
  79.4 3.7 %collective-permute-start.9 = (f32[16,128]{1,0:T(8,128)S(1)}, f32[16,128]{1,0:T(8,128)S(1)}, u32[]{:S(2)}, u32[]{:S(2)}) collective-permute-start(f32[16,128]{1,0:T(8,128)S(1)} %get-tuple-element.19), channel_id=1, source_target_pairs={{0,2},{1,3},{2,0},{3,1},{4,6},{5,7},{6,4},{7,5},{8,10},{9,11},{10,... | collective-permute-start | bytes 24584 | tf_op jit(solution)/shard_map/ppermute | solution.py:21
  81.0 2.1 %collective-permute-start.8 = (f32[16,128]{1,0:T(8,128)S(1)}, f32[16,128]{1,0:T(8,128)S(1)}, u32[]{:S(2)}, u32[]{:S(2)}) collective-permute-start(f32[16,128]{1,0:T(8,128)S(1)} %get-tuple-element.19), channel_id=1, source_target_pairs={{0,1},{1,0},{2,3},{3,2},{4,5},{5,4},{6,7},{7,6},{8,9},{9,8},{10,11... | collective-permute-start | bytes 24584 | tf_op jit(solution)/shard_map/ppermute | solution.py:21

commit v2 on v0

v2 whole, which is shorter than its diff:
```python
import math

import jax
import jax.numpy as jnp
from jax import lax
from jax.experimental import pallas as pl
from jax.experimental.pallas import tpu as pltpu
from jax.sharding import PartitionSpec as P

LOG2E = math.log2(math.e)
BLOCK = 16
WIDTH = 512
BF = jnp.bfloat16
F4 = jnp.float32
NT = (((1,), (1,)), ((), ()))
TN = (((0,), (0,)), ((), ()))


def swap(a, axis, bit):
    count = lax.axis_size(axis)
    return lax.ppermute(a, axis, [(i, i ^ bit) for i in range(count)])


def params(limit=12 << 20):
    return pltpu.CompilerParams(vmem_limit_bytes=limit)


def cols(rows):
    return pl.BlockSpec((rows, WIDTH), lambda i: (0, i))


def whole(rows, lanes):
    return pl.BlockSpec((rows, lanes), lambda i: (0, 0))


def fetch(*arrays):
    count = len(arrays)

    def body(*refs):
        sems = refs[-1]
        copies = [
            pltpu.make_async_copy(refs[i], refs[count + i], sems.at[i]) for i in range(count)
        ]
        for copy in copies:
            copy.start()
        for copy in copies:
            copy.wait()

    moved = 2 * sum(a.size * a.dtype.itemsize for a in arrays)
    return pl.pallas_call(
        body,
        in_specs=[pl.BlockSpec(memory_space=pltpu.HBM)] * count,
        out_specs=in_vmem(count),
        out_shape=[pltpu.VMEM(a.shape, a.dtype) for a in arrays],
        scratch_shapes=[pltpu.SemaphoreType.DMA((count,))],
        compiler_params=params(1 << 20),
        cost_estimate=pl.CostEstimate(flops=0, bytes_accessed=moved, transcendentals=0),
        name="fetch",
    )(*[in_hbm(a) for a in arrays])


def chunk_at(i, base=0):
    return pl.ds(pl.multiple_of((base + i) * WIDTH, WIDTH), WIDTH)


def conv_kernel(x_ref, odd_ref, even_ref, w_ref, bias_ref, proj_ref, out_ref, part_ref, ext):
    rows, channels = x_ref.shape
    rim = odd_ref.shape[0]
    taps = w_ref.shape[0]
    base = rim - (taps - 1)
    odd = (lax.axis_index("seq") & 1) != 0
    part_ref[...] = jnp.zeros_like(part_ref)

    @pl.loop(0, channels // WIDTH)
    def _(i):
        for j in range(WIDTH // 128):
            lanes = pl.ds(pl.multiple_of(i * WIDTH + j * 128, 128), 128)
            ext[j, 0:rim, :] = jnp.where(
                odd, odd_ref[:, lanes].astype(F4), even_ref[:, lanes].astype(F4)
            )
            ext[j, rim : rim + rows, :] = x_ref[:, lanes].astype(F4)
            weights = w_ref[:, lanes]
            bias = bias_ref[:, lanes]
            for top in range(0, rows, BLOCK):
                acc = bias
                for tap in range(taps):
                    at = base + top + tap
                    acc = acc + weights[tap : tap + 1, :] * ext[j, at : at + BLOCK, :]
                half = 0.5 * acc
                out_ref[top : top + BLOCK, lanes] = (half + half * jnp.tanh(half)).astype(BF)
        at = chunk_at(i)
        part_ref[...] += lax.dot_general(
            out_ref[:, at], proj_ref[:, at], NT, preferred_element_type=F4
        )


def conv_project(conv_in, rims, conv_weight, conv_bias, proj_weight_t):
    rows, channels = conv_in.shape
    wide = proj_weight_t.shape[0]
    rim = rims[0].shape[0]
    return pl.pallas_call(
        conv_kernel,
        in_specs=in_vmem(6),
        out_specs=in_vmem(2),
        out_shape=[
            jax.ShapeDtypeStruct((rows, channels), BF),
            jax.ShapeDtypeStruct((rows, wide), F4),
        ],
        scratch_shapes=[pltpu.VMEM((WIDTH // 128, rows + rim, 128), F4)],
        compiler_params=params(),
        name="conv_project",
    )(conv_in, *rims, conv_weight, conv_bias, proj_weight_t)


def in_hbm(a):
    return pltpu.with_memory_space_constraint(a, pltpu.HBM)


def in_vmem(count):
    return [pl.BlockSpec(memory_space=pltpu.VMEM)] * count


def split_sum(total, rank, out_ref):
    wide = total.shape[1]
    high = total.astype(BF)
    out_ref[:, :wide] = high
    out_ref[:, wide:] = (total[:, rank:] - high[:, rank:].astype(F4)).astype(BF)


def joined(ref, wide, rank):
    high = ref[:, :wide].astype(F4)
    return high[:, :rank], high[:, rank:] + ref[:, wide:].astype(F4)


def add_first(part, other, rank):
    rows, wide = part.shape

    def body(a_ref, b_ref, out_ref):
        split_sum(a_ref[...] + b_ref[...], rank, out_ref)

    return pl.pallas_call(
        body,
        in_specs=in_vmem(2),
        out_specs=pl.BlockSpec(memory_space=pltpu.VMEM),
        out_shape=jax.ShapeDtypeStruct((rows, 2 * wide - rank), BF),
        compiler_params=params(),
        name="add_first",
    )(part, other)


def add_later(mine, other, wide, rank):
    def body(a_ref, b_ref, out_ref):
        a_low, a_high = joined(a_ref, wide, rank)
        b_low, b_high = joined(b_ref, wide, rank)
        total = jnp.concatenate([a_low + b_low, a_high + b_high], axis=1)
        split_sum(total, rank, out_ref)

    return pl.pallas_call(
        body,
        in_specs=in_vmem(2),
        out_specs=pl.BlockSpec(memory_space=pltpu.VMEM),
        out_shape=jax.ShapeDtypeStruct(mine.shape, BF),
        compiler_params=params(),
        name="add_later",
    )(mine, other)


def softplus(x):
    u = jnp.exp(-jnp.abs(x))
    small = u * (1.0 - u * (0.5 - u * (1.0 / 3.0)))
    return jnp.maximum(x, 0.0) + jnp.where(u < 0.0078125, small, jnp.log(1.0 + u))


def wide_iota(shape, axis):
    return lax.broadcasted_iota(jnp.int32, shape, axis)


def contract(block, c_now, grad_now):
    mixed = jnp.dot(c_now, block, preferred_element_type=F4)
    pairs = lax.dot_general(grad_now, block, NT, preferred_element_type=F4)
    return mixed, pairs


def prepare_kernel(mine_ref, other_ref, proj_ref, b_ref, c_ref, alt_ref):
    rows, rank = proj_ref.shape
    wide = c_ref.shape[1]
    states = wide // BLOCK
    a_low, a_high = joined(mine_ref, rank + 2 * states, rank)
    b_low, b_high = joined(other_ref, rank + 2 * states, rank)
    proj_ref[...] = (a_low + b_low).astype(BF)
    ends = (a_high + b_high).astype(BF)
    lane = wide_iota((states, wide), 1)
    row = wide_iota((states, wide), 0)
    by_token = (lane % states == row).astype(BF)
    by_state = (lane // BLOCK == row).astype(BF)
    lane = wide_iota((rows, wide), 1)
    row = wide_iota((rows, wide), 0) % BLOCK
    c_mat = ends[:, states:]
    tiled = jnp.dot(c_mat, by_token, preferred_element_type=F4)
    c_ref[...] = jnp.where(lane // states == row, tiled, 0.0).astype(BF)
    tiled = jnp.dot(c_mat, by_state, preferred_element_type=F4)
    alt_ref[...] = jnp.where(lane % BLOCK == row, tiled, 0.0).astype(BF)
    tiled = jnp.dot(ends[:, :states], by_token, preferred_element_type=F4)
    b_diag = jnp.where(lane // states == row, tiled, 0.0).astype(BF)
    ones = jnp.ones((BLOCK, 128), BF)
    for top in range(0, rows, BLOCK):
        b_ref[top * states : (top + BLOCK) * states, :] = lax.dot_general(
            b_diag[top : top + BLOCK, :], ones, TN, preferred_element_type=F4
        )


def prepare(mine, other, rank, states):
    rows = mine.shape[0]
    wide = BLOCK * states
    return pl.pallas_call(
        prepare_kernel,
        in_specs=in_vmem(2),
        out_specs=in_vmem(4),
        out_shape=[
            jax.ShapeDtypeStruct((rows, rank), BF),
            jax.ShapeDtypeStruct((rows * states, 128), F4),
            jax.ShapeDtypeStruct((rows, wide), BF),
            jax.ShapeDtypeStruct((rows, wide), BF),
        ],
        compiler_params=params(),
        name="prepare",
    )(mine, other)


def scan_kernel(
    base, fresh,
    proj_ref, b_ref, c_ref, dtw_ref, dtb_ref, rate_ref, skip_ref, conv_ref, grad_ref, pairs_in,
    mixed_ref, cum_ref, end_ref, send_ref, total_ref, pairs_ref,
    raw, step, drive, even, odd,
):
    rows = conv_ref.shape[0]
    states = rate_ref.shape[0]
    chunks = mixed_ref.shape[1] // WIDTH
    pairs_ref[...] = jnp.zeros_like(pairs_ref) if fresh else pairs_in[...]
    tri = (
        wide_iota((rows, 2 * rows), 0) >= wide_iota((rows, 2 * rows), 1) % rows
    ).astype(BF)

    def project(i):
        raw[...] = jnp.dot(proj_ref[...], dtw_ref[:, chunk_at(i, base)], preferred_element_type=F4)

    project(0)

    @pl.loop(0, chunks)
    def _(i):
        here = chunk_at(i)
        at_in = chunk_at(i, base)
        bias = dtb_ref[:, at_in]
        skip = skip_ref[:, at_in]
        highs = []
        lows = []
        for top in range(0, rows, BLOCK):
            at = slice(top, top + BLOCK)
            now = softplus(raw[at, :] + bias)
            step[at, :] = now
            conv = conv_ref[at, at_in].astype(F4)
            drive[at, :] = now * conv
            mixed_ref[at, here] = skip * conv
            high = now.astype(BF)
            highs.append(high)
            lows.append((now - high.astype(F4)).astype(BF))
        cum_ref[:, here] = jnp.dot(
            tri, jnp.concatenate(highs + lows, axis=0), preferred_element_type=F4
        )
        total_ref[:, here] = cum_ref[rows - 1 : rows, here]
        project(jnp.minimum(i + 1, chunks - 1))

        rate = rate_ref[:, at_in]
        state = jnp.zeros((states, WIDTH), F4)
        for top in range(0, rows, BLOCK):
            hist = odd if (top // BLOCK) % 2 else even
            for t in range(BLOCK):
                r = top + t
                b_now = b_ref[r * states : (r + 1) * states, :]
                b_now = jnp.concatenate([b_now] * (WIDTH // 128), axis=1)
                state = (
                    jnp.exp2(step[r : r + 1, :] * rate) * state + drive[r : r + 1, :] * b_now
                )
                hist[t * states : (t + 1) * states, :] = state.astype(BF)
            at = slice(top, top + BLOCK)
            mixed, pairs = contract(hist[...], c_ref[at, :], grad_ref[at, at_in])
            mixed_ref[at, here] += mixed
            pairs_ref[at, :] += pairs
        end_ref[:, here] = state
        send_ref[:, here] = state.astype(BF)


def local_scan(base, width, prepared, dt_weight, dt_bias, rate, skip, conv_out, grad_out, pairs):
    rows = conv_out.shape[0]
    states = rate.shape[0]
    wide = BLOCK * states
    fresh = pairs is None
    proj, b_wide, c_wide, _ = prepared

    def body(*refs):
        refs = list(refs)
        if fresh:
            refs.insert(9, None)
        scan_kernel(base, fresh, *refs)

    ops = [proj, b_wide, c_wide, dt_weight, dt_bias, rate, skip, conv_out, grad_out]
    ops += [] if fresh else [pairs]
    work = rows * width * states
    return pl.pallas_call(
        body,
        in_specs=in_vmem(len(ops)),
        out_specs=in_vmem(6),
        out_shape=[
            jax.ShapeDtypeStruct((rows, width), F4),
            jax.ShapeDtypeStruct((rows, width), F4),
            jax.ShapeDtypeStruct((states, width), F4),
            jax.ShapeDtypeStruct((states, width), BF),
            jax.ShapeDtypeStruct((1, width), F4),
            jax.ShapeDtypeStruct((rows, wide), F4),
        ],
        scratch_shapes=[
            pltpu.VMEM((rows, WIDTH), F4),
            pltpu.VMEM((rows, WIDTH), F4),
            pltpu.VMEM((rows, WIDTH), F4),
            pltpu.VMEM((wide, WIDTH), BF),
            pltpu.VMEM((wide, WIDTH), BF),
        ],
        compiler_params=params(),
        cost_estimate=pl.CostEstimate(
            flops=600 * work, bytes_accessed=work, transcendentals=work
        ),
        name="local_scan",
    )(*ops)


def carry_kernel(
    base, scale, fresh, final,
    alt_ref, rate_ref, state_ref, cum_ref, mixed_ref, grad_ref, pairs_in, local_ref, prev_ref,
    out_ref, result_ref,
    pairs, rates, inits, even, odd,
):
    rows = cum_ref.shape[0]
    states = rate_ref.shape[0]
    wide = BLOCK * states
    i = pl.program_id(0)

    @pl.when(i == 0)
    def _():
        pairs[...] = jnp.zeros_like(pairs) if fresh else pairs_in[...]

    here = chunk_at(i)
    at_in = chunk_at(i, base)
    for n in range(states):
        at = slice(n * BLOCK, (n + 1) * BLOCK)
        shape = (BLOCK, WIDTH)
        rates[at, :] = jnp.broadcast_to(rate_ref[n : n + 1, at_in], shape).astype(BF)
        inits[at, :] = jnp.broadcast_to(state_ref[n : n + 1, here], shape).astype(BF)
    for top in range(0, rows, BLOCK):
        hist = odd if (top // BLOCK) % 2 else even
        tokens = slice(top, top + BLOCK)
        cum = cum_ref[tokens, here].astype(BF)
        for n in range(states):
            at = slice(n * BLOCK, (n + 1) * BLOCK)
            hist[at, :] = jnp.exp2(cum * rates[at, :]) * inits[at, :]
        mixed, more = contract(hist[...], alt_ref[tokens, :], grad_ref[tokens, at_in])
        out_ref[tokens, :] = (mixed_ref[tokens, here] + mixed).astype(BF)
        pairs[tokens, :] += more

    @pl.when(i == pl.num_programs(0) - 1)
    def _():
        if not final:
            result_ref[...] = pairs[...]
            return
        lane = wide_iota((rows, wide), 1)
        row = wide_iota((rows, wide), 0) % BLOCK
        by_state = jnp.where(lane % BLOCK == row, pairs[...], 0.0) * scale
        by_token = jnp.where(lane // states == row, local_ref[...], 0.0) * scale
        lane = wide_iota((states, wide), 1)
        row = wide_iota((states, wide), 0)
        exact = dict(preferred_element_type=F4, precision=lax.Precision.HIGHEST)
        result_ref[...] = lax.dot_general(
            (lane // BLOCK == row).astype(F4), by_state, NT, **exact
        ) + lax.dot_general((lane % states == row).astype(F4), by_token, NT, **exact)


def add_carry(base, scale, alt, rate, incoming, cum, mixed, grad_out, pairs, local, prev):
    rows, width = cum.shape
    states, channels = rate.shape
    wide = BLOCK * states
    fresh, final = pairs is None, local is not None
    ops = [alt, rate, incoming, cum, mixed, grad_out]
    extra = [pairs, local, prev]
    specs = in_vmem(6)
    for a in extra:
        if a is not None:
            ops.append(a)
            specs += [pl.BlockSpec(memory_space=pl.ANY)] if a is prev else in_vmem(1)

    def body(*refs):
        refs = list(refs)
        for k, a in enumerate(extra):
            if a is None:
                refs.insert(6 + k, None)
        carry_kernel(base, scale, fresh, final, *refs)

    work = rows * width * states
    return pl.pallas_call(
        body,
        grid=(width // WIDTH,),
        in_specs=specs,
        out_specs=[
            pl.BlockSpec((rows, WIDTH), lambda i: (0, i + base)),
            whole(states, rows) if final else whole(rows, wide),
        ],
        out_shape=[
            jax.ShapeDtypeStruct((rows, channels), BF),
            jax.ShapeDtypeStruct((states, rows) if final else (rows, wide), F4),
        ],
        scratch_shapes=[
            pltpu.VMEM((rows, wide), F4),
            pltpu.VMEM((wide, WIDTH), BF),
            pltpu.VMEM((wide, WIDTH), BF),
            pltpu.VMEM((wide, WIDTH), BF),
            pltpu.VMEM((wide, WIDTH), BF),
        ],
        input_output_aliases={} if prev is None else {len(ops) - 1: 0},
        compiler_params=params(),
        cost_estimate=pl.CostEstimate(
            flops=300 * work, bytes_accessed=work, transcendentals=work
        ),
        name="add_carry",
    )(*ops)


def merge_kernel(bit, last, rate_ref, end_ref, total_ref, other_ref, osum_ref, pre_ref, psum_ref, *outs):
    later = (lax.axis_index("seq") & bit) != 0
    rate = rate_ref[...]
    fade = lambda s: jnp.exp2(rate * s)
    other = other_ref[...].astype(F4)
    prefix = pre_ref[...]
    outs[0][...] = jnp.where(later, prefix + fade(psum_ref[...]) * other, prefix)
    if not last:
        total, osum, end = total_ref[...], osum_ref[...], end_ref[...]
        outs[1][...] = jnp.where(later, psum_ref[...] + osum, psum_ref[...])
        first = jnp.where(later, other, end)
        second = jnp.where(later, end, other)
        end = second + fade(jnp.where(later, total, osum)) * first
        outs[2][...] = end
        outs[3][...] = end.astype(BF)
        outs[4][...] = total + osum


def merge(base, bit, last, rate, end, total, other, other_sum, prefix, prefix_sum):
    states, channels = end.shape
    many = jax.ShapeDtypeStruct((states, channels), F4)
    one = jax.ShapeDtypeStruct((1, channels), F4)
    outs = [many] if last else [many, one, many, jax.ShapeDtypeStruct((states, channels), BF), one]
    wide, narrow = cols(states), cols(1)

    def body(*refs):
        merge_kernel(bit, last, *refs)

    return pl.pallas_call(
        body,
        grid=(channels // WIDTH,),
        in_specs=[
            pl.BlockSpec((states, WIDTH), lambda i: (0, i + base)),
            wide, narrow, wide, narrow, wide, narrow,
        ],
        out_specs=[wide] if last else [wide, narrow, wide, wide, narrow],
        out_shape=outs,
        compiler_params=params(),
        name="merge",
    )(rate, end, total, other, other_sum, prefix, prefix_sum)


def weight_first(parts, conv_out, count):
    states, rows = parts[0].shape
    share = conv_out.shape[1] // count
    many = len(parts)

    def body(*refs):
        conv_ref, out_ref = refs[many:]
        grad_c = refs[0][...]
        for r in refs[1:many]:
            grad_c = grad_c + r[...]
        grad_c = grad_c.astype(BF)
        for j in range(count):
            block = conv_ref[:, j * share : (j + 1) * share]
            out_ref[j] = jnp.dot(grad_c, block, preferred_element_type=F4).astype(BF)

    return pl.pallas_call(
        body,
        in_specs=in_vmem(many + 1),
        out_specs=pl.BlockSpec(memory_space=pltpu.VMEM),
        out_shape=jax.ShapeDtypeStruct((count, states, share), BF),
        compiler_params=params(),
        name="weight_first",
    )(*parts, conv_out)


def weight_gradient(parts, conv_out):
    count = lax.axis_size("seq")
    states = parts[0].shape[0]
    share = conv_out.shape[1] // count
    if share % 128 == 0:
        weight = weight_first(parts, conv_out, count)
    else:
        grad_c = sum(parts[1:], parts[0]).astype(BF)
        weight = jnp.dot(grad_c, conv_out, preferred_element_type=F4).astype(BF)
        weight = weight.reshape(states, count, share).transpose(1, 0, 2)
    weight = lax.all_to_all(weight, "seq", 0, 0)
    return jnp.sum(weight.astype(F4), axis=0).T


def exchange(base, bit, rate, held):
    end, send, total, prefix, prefix_sum = held
    last = 2 * bit >= lax.axis_size("seq")
    other = swap(send, "seq", bit)
    other_sum = total if last else swap(total, "seq", bit)
    outs = merge(base, bit, last, rate, end, total, other, other_sum, prefix, prefix_sum)
    if last:
        return outs[0]
    prefix, prefix_sum, end, send, total = outs
    return end, send, total, prefix, prefix_sum


def on_device(
    conv_in,
    conv_weight,
    conv_bias,
    proj_weight,
    dt_weight,
    dt_bias,
    decay_rate,
    skip_gain,
    grad_out,
):
    rows, channels = conv_in.shape
    taps = conv_weight.shape[0]
    rank = dt_weight.shape[0]
    states = decay_rate.shape[0]
    count = lax.axis_size("seq")
    tp = lax.axis_size("tp")
    rim_rows = 8 * -(-(taps - 1) // 8)
    edge = conv_in[rows - rim_rows :]
    rims = [
        lax.ppermute(edge, "seq", [p for i in range(k, count - 1, 2) for p in ((i, i + 1), (i + 1, i))])
        for k in range(2)
    ]
    x, w, bias, weight_t = fetch(conv_in, conv_weight, conv_bias[None], proj_weight.T)
    rate = decay_rate * (-LOG2E)
    conv_out, part = conv_project(x, rims, w, bias, weight_t)
    mine = add_first(part, swap(part, "tp", 1), rank)
    other = swap(mine, "tp", 2)
    bit = 4
    while bit < tp:
        mine = add_later(mine, other, part.shape[1], rank)
        other = swap(mine, "tp", bit)
        bit *= 2
    prepared = prepare(mine, other, rank, states)

    width = channels // 2
    bases = (0, width // WIDTH)
    pairs = None
    local, held = [], []
    for base in bases:
        mixed, cum, end, send, total, pairs = local_scan(
            base, width, prepared, dt_weight, dt_bias[None], rate, skip_gain[None],
            conv_out, grad_out, pairs,
        )
        local.append((cum, mixed))
        held.append((end, send, total, jnp.zeros_like(end), jnp.zeros_like(total)))
    bit = 1
    while bit < count:
        held = [exchange(base, bit, rate, h) for base, h in zip(bases, held)]
        bit *= 2

    scale = 1.0 / (rows * count)
    shared = (scale, prepared[3], rate)
    mixed, more = add_carry(bases[0], *shared, held[0], *local[0], grad_out, None, None, None)
    mixed, grad_c = add_carry(bases[1], *shared, held[1], *local[1], grad_out, more, pairs, mixed)
    parts = [grad_c] + [swap(grad_c, "tp", k) for k in range(1, tp)]
    weight_grad = weight_gradient(parts, conv_out)
    return (mixed, weight_grad[None])


def solution(mesh):
    return jax.shard_map(
        on_device,
        mesh=mesh,
        in_specs=(
            P("seq", "tp"),
            P(None, "tp"),
            P("tp"),
            P("tp", None),
            P(None, "tp"),
            P("tp"),
            P(None, "tp"),
            P("tp"),
            P("seq", "tp"),
        ),
        out_specs=(P("seq", "tp"), P("tp", "seq", None)),
        check_vma=False,
    )
```

time: 398 us -> 83.1 us (0.21)
  waiting for transfers between devices: 159 us -> 15 us
  local copies, waits for them, and re-layouts: 90.4 us -> 0.89 us
  other arithmetic: 89.8 us -> 0.66 us
  Pallas kernels: 0 us -> 32.5 us
  starting transfers between devices: 4.99 us -> 20.6 us
  blocking collectives: 25.7 us -> 12.3 us
  between operations: 14 us -> 0.84 us
  matrix products: 9.51 us -> 0 us
    all_gather x2 -> x0, waiting for transfers between devices: 94 us -> none  [entering(): gathered = jax.tree.map(lambda a: lax.all_gather(a, axis), part)]
    reduce_scatter x1 -> x0, waiting for transfers between devices: 65.4 us -> none  [on_device(): lax.psum_scatter(lax.dot_general(conv_out, grad_c, (((0,), (0,)), ((), ()...]
    reduce_sum x42 -> x1, other arithmetic: 52.1 us -> 0.63 us  [weight_gradient(): return jnp.sum(weight.astype(F4), axis=0).T]
    rev x2 -> x0, local copies, waits for them, and re-layouts: 33.2 us -> none  [local_ending(): after = jnp.flip(jnp.cumsum(jnp.flip(step_size, 0), axis=0), 0) - step_size]
    pallas_call x0 -> x15, Pallas kernels: none -> 32.5 us  [the longest x2 12 us: local_scan(): pl.pallas_call(body, in_specs=in_vmem(len(ops)), out_specs=in_vmem(6), ou...]
    slice x10 -> x1, local copies, waits for them, and re-layouts: 30.1 us -> 0.85 us  [on_device(): edge = conv_in[rows - rim_rows:]]
    psum x2 -> x0, blocking collectives: 25.7 us -> none  [the longest x1 14.5 us: on_device(): proj_out = lax.psum(partial_proj, 'tp').astype(jnp.bfloat16)]
    neg x9 -> x0, other arithmetic: 22.4 us -> none  [the longest x8 20 us: block_step(): -step_now[offset][None, :] * decay_rate]
  transfers between devices with their start and end apart: 4 -> 17, of which waited for: 3 -> 7; matrix products, arithmetic and copies ran while one was open for 3% -> 0% of each run, Pallas kernels for 0% -> 19%
where the time goes in v2:
time: 83.1 us; the launch traced here: 82.8 us
  Pallas kernels  32.5 us (39%)
  starting transfers between devices  20.6 us (25%)
  waiting for transfers between devices  15 us (18%)
  blocking collectives  12.3 us (15%)
  local copies, waits for them, and re-layouts  0.89 us (1%)
  between operations  0.84 us (1%)
    ppermute x15, starting transfers between devices, swap(): return lax.ppermute(a, axis, [(i, i ^ bit) for i in range(count)])  16.9 us
    ppermute x15, waiting for transfers between devices, swap(): return lax.ppermute(a, axis, [(i, i ^ bit) for i in range(count)])  15 us
    all_to_all x1, blocking collectives, weight_gradient(): weight = lax.all_to_all(weight, 'seq', 0, 0)  12.3 us
    pallas_call x2, Pallas kernels, local_scan(): pl.pallas_call(body, in_specs=in_vmem(len(ops)), out_specs=in_vmem(6), ou...  12 us
    pallas_call x2, Pallas kernels, add_carry(): pl.pallas_call(body, grid=(width // WIDTH,), in_specs=specs, out_specs=[p...  11.4 us
    pallas_call x1, Pallas kernels, conv_project(): pl.pallas_call(conv_kernel, in_specs=in_vmem(6), out_specs=in_vmem(2), ou...  3.8 us
    ppermute x2, starting transfers between devices, on_device(): lax.ppermute(edge, 'seq', [p for i in range(k, count - 1, 2) for p in ((i...  3.62 us
    pallas_call x1, Pallas kernels, fetch(): pl.pallas_call(body, in_specs=[pl.BlockSpec(memory_space=pltpu.HBM)] * co...  2.66 us
  transfers between devices with their start and end apart: 17, of which 7 were waited for; matrix products, arithmetic and copies ran while one was open for 0% of the time, Pallas kernels for 19%

profile of v2, /device:TPU:0, one launch (start us, length us, event | category | flops | bytes accessed | tf_op | source)
XLA Modules:
  0.0 82.8 jit_solution(8189372894188957580)
XLA Ops:
  0.6 0.8 %slice.3 = bf16[8,4096]{1,0:T(8,128)(2,1)S(1)} slice(bf16[128,4096]{1,0:T(8,128)(2,1)} %refs_0_.1), slice={[120:128], [0:4096]} | slice | bytes 131072 | tf_op jit(solution)/shard_map/slice | solution.py:546
  1.5 3.0 %collective-permute-start = (bf16[8,4096]{1,0:T(8,128)(2,1)S(1)}, bf16[8,4096]{1,0:T(8,128)(2,1)S(1)}, u32[]{:S(2)}, u32[]{:S(2)}) collective-permute-start(bf16[8,4096]{1,0:T(8,128)(2,1)S(1)} %slice.3), channel_id=1, source_target_pairs={{0,4},{4,0},{8,12},{12,8},{16,20},{20,16},{24,28},{28,24},{1,5},{5... | collective-permute-start | bytes 196616 | tf_op jit(solution)/shard_map/ppermute | solution.py:548
  4.4 0.7 collective-permute-start.1
  5.1 2.7 %fetch.1 = (bf16[128,4096]{1,0:T(8,128)(2,1)S(1)}, f32[4,4096]{1,0:T(4,128)S(1)}, f32[1,4096]{1,0:T(1,128)S(1)}, bf16[544,4096]{1,0:T(8,128)(2,1)S(1)}) custom-call(bf16[128,4096]{1,0:T(8,128)(2,1)} %refs_0_.1, f32[4,4096]{1,0:T(4,128)} %refs_1_.1, f32[1,4096]{1,0:T(1,128)} %bitcast.13, bf16[544,4096]{1,0:T(8,128)(2,1)} %bitcast.11), custom_call_target="tpu_custom_call" | custom-call | bytes 11173888 | tf_op jit(solution)/shard_map/fetch/pallas_call | solution.py:50
  7.8 0.0 copy-start.4
  7.8 0.0 copy-start
  7.8 0.0 copy-start.1
  7.8 0.0 copy-start.2
  7.8 0.0 copy-start.3
  7.8 0.0 collective-permute-done.odd_ref
  7.9 3.8 %conv_project.1 = (bf16[128,4096]{1,0:T(8,128)(2,1)S(1)}, f32[128,544]{1,0:T(8,128)S(1)}) custom-call(bf16[128,4096]{1,0:T(8,128)(2,1)S(1)} %get-tuple-element.48.x_ref, bf16[8,4096]{1,0:T(8,128)(2,1)S(1)} %collective-permute-done.odd_ref, bf16[8,4096]{1,0:T(8,128)(2,1)S(1)} %collective-permute-done.1.even_ref, f32[4,4096]{1,0:T(4,128)S(1)} %get-tuple-element.49.w_ref, ...), custom_call_target="tpu_custom_call" | custom-call | tf_op jit(solution)/shard_map/conv_project/pallas_call | solution.py:101
  11.7 0.1 collective-permute-start.2
  11.7 1.6 %collective-permute-done.2.b_ref = f32[128,544]{1,0:T(8,128)S(1)} collective-permute-done((f32[128,544]{1,0:T(8,128)S(1)}, f32[128,544]{1,0:T(8,128)S(1)}, u32[]{:S(2)}, u32[]{:S(2)}) %collective-permute-start.2) | collective-permute-done | bytes 278560 | tf_op jit(solution)/shard_map/ppermute | solution.py:21
  13.4 0.1 add_first.1.mine_ref
  13.5 1.6 %collective-permute-start.3 = (bf16[128,576]{1,0:T(8,128)(2,1)S(1)}, bf16[128,576]{1,0:T(8,128)(2,1)S(1)}, u32[]{:S(2)}, u32[]{:S(2)}) collective-permute-start(bf16[128,576]{1,0:T(8,128)(2,1)S(1)} %add_first.1.mine_ref), channel_id=1, source_target_pairs={{0,2},{1,3},{2,0},{3,1},{4,6},{5,7},{6,4},{7,5},{8,10},{9,11},{10,... | collective-permute-start | bytes 442376 | tf_op jit(solution)/shard_map/ppermute | solution.py:21
  15.1 4.7 %collective-permute-done.3.other_ref = bf16[128,576]{1,0:T(8,128)(2,1)S(1)} collective-permute-done((bf16[128,576]{1,0:T(8,128)(2,1)S(1)}, bf16[128,576]{1,0:T(8,128)(2,1)S(1)}, u32[]{:S(2)}, u32[]{:S(2)}) %collective-permute-start.3) | collective-permute-done | bytes 147488 | tf_op jit(solution)/shard_map/ppermute | solution.py:21
  19.8 0.6 prepare.1
  20.5 6.0 %local_scan.2 = (f32[128,2048]{1,0:T(8,128)S(1)}, f32[128,2048]{1,0:T(8,128)S(1)}, f32[16,2048]{1,0:T(8,128)S(1)}, bf16[16,2048]{1,0:T(8,128)(2,1)S(1)}, f32[1,2048]{1,0:T(1,128)S(1)}, /*index=5*/f32[128,256]{1,0:T(8,128)S(1)}) custom-call(bf16[128,512]{1,0:T(8,128)(2,1)S(1)} %get-tuple-element.54.refs_0_, f32[2048,128]{1,0:T(8,128)S(1)} %get-tuple-element.55.refs_1_, ...), custom_call_target="tpu_custom_call" | custom-call | flops 2516582400 | bytes 4194304 | tf_op jit(solution)/shard_map/local_scan/pallas_call | solution.py:309
  26.5 4.3 %collective-permute-start.9 = (bf16[16,2048]{1,0:T(8,128)(2,1)S(1)}, bf16[16,2048]{1,0:T(8,128)(2,1)S(1)}, u32[]{:S(2)}, u32[]{:S(2)}) collective-permute-start(bf16[16,2048]{1,0:T(8,128)(2,1)S(1)} %get-tuple-element.76), channel_id=1, source_target_pairs={{0,4},{4,0},{8,12},{12,8},{16,20},{20,16},{24,28},{28,24},{1,5},{5... | collective-permute-start | bytes 196616 | tf_op jit(solution)/shard_map/ppermute | solution.py:21
  30.8 0.1 collective-permute-start.10
  30.8 6.0 %local_scan.3 = (f32[128,2048]{1,0:T(8,128)S(1)}, f32[128,2048]{1,0:T(8,128)S(1)}, f32[16,2048]{1,0:T(8,128)S(1)}, bf16[16,2048]{1,0:T(8,128)(2,1)S(1)}, f32[1,2048]{1,0:T(1,128)S(1)}, /*index=5*/f32[128,256]{1,0:T(8,128)S(1)}) custom-call(bf16[128,512]{1,0:T(8,128)(2,1)S(1)} %get-tuple-element.54.refs_0_, f32[2048,128]{1,0:T(8,128)S(1)} %get-tuple-element.55.refs_1_, ...), custom_call_target="tpu_custom_call" | custom-call | flops 2516582400 | bytes 4194304 | tf_op jit(solution)/shard_map/local_scan/pallas_call | solution.py:309
  36.8 2.0 %collective-permute-start.4 = (bf16[16,2048]{1,0:T(8,128)(2,1)S(1)}, bf16[16,2048]{1,0:T(8,128)(2,1)S(1)}, u32[]{:S(2)}, u32[]{:S(2)}) collective-permute-start(bf16[16,2048]{1,0:T(8,128)(2,1)S(1)} %get-tuple-element.61), channel_id=1, source_target_pairs={{0,4},{4,0},{8,12},{12,8},{16,20},{20,16},{24,28},{28,24},{1,5},{5... | collective-permute-start | bytes 196616 | tf_op jit(solution)/shard_map/ppermute | solution.py:21
  38.8 0.3 merge.9
  39.2 1.6 %collective-permute-start.11 = (bf16[16,2048]{1,0:T(8,128)(2,1)S(1)}, bf16[16,2048]{1,0:T(8,128)(2,1)S(1)}, u32[]{:S(2)}, u32[]{:S(2)}) collective-permute-start(bf16[16,2048]{1,0:T(8,128)(2,1)S(1)} %get-tuple-element.79), channel_id=1, source_target_pairs={{0,8},{4,12},{8,0},{12,4},{16,24},{20,28},{24,16},{28,20},{1,9},{5... | collective-permute-start | bytes 196616 | tf_op jit(solution)/shard_map/ppermute | solution.py:21
  40.8 1.4 %collective-permute-start.5 = (f32[1,2048]{1,0:T(1,128)S(1)}, f32[1,2048]{1,0:T(1,128)S(1)}, u32[]{:S(2)}, u32[]{:S(2)}) collective-permute-start(f32[1,2048]{1,0:T(1,128)S(1)} %get-tuple-element.60.refs_2_), channel_id=1, source_target_pairs={{0,4},{4,0},{8,12},{12,8},{16,20},{20,16},{24,28},{28,24},{1,5},{5... | collective-permute-start | bytes 24584 | tf_op jit(solution)/shard_map/ppermute | solution.py:21
  42.2 0.1 collective-permute-start.12
  42.3 2.2 %collective-permute-done.5.refs_4_ = f32[1,2048]{1,0:T(1,128)S(1)} collective-permute-done((f32[1,2048]{1,0:T(1,128)S(1)}, f32[1,2048]{1,0:T(1,128)S(1)}, u32[]{:S(2)}, u32[]{:S(2)}) %collective-permute-start.5) | collective-permute-done | bytes 8224 | tf_op jit(solution)/shard_map/ppermute | solution.py:21
  44.5 0.0 collective-permute-done.4.refs_3_
  44.5 0.3 merge.6
  44.8 0.5 collective-permute-start.6
  45.3 0.5 collective-permute-done.12.refs_4_
  45.8 0.3 merge.10
  46.2 2.6 %collective-permute-start.13 = (bf16[16,2048]{1,0:T(8,128)(2,1)S(1)}, bf16[16,2048]{1,0:T(8,128)(2,1)S(1)}, u32[]{:S(2)}, u32[]{:S(2)}) collective-permute-start(bf16[16,2048]{1,0:T(8,128)(2,1)S(1)} %get-tuple-element.84), channel_id=1, source_target_pairs={{0,16},{4,20},{8,24},{12,28},{16,0},{20,4},{24,8},{28,12},{1,17},{... | collective-permute-start | bytes 196616 | tf_op jit(solution)/shard_map/ppermute | solution.py:21
  48.8 0.5 collective-permute-start.7
  49.3 3.2 %collective-permute-done.7.refs_4_ = f32[1,2048]{1,0:T(1,128)S(1)} collective-permute-done((f32[1,2048]{1,0:T(1,128)S(1)}, f32[1,2048]{1,0:T(1,128)S(1)}, u32[]{:S(2)}, u32[]{:S(2)}) %collective-permute-start.7) | collective-permute-done | bytes 8224 | tf_op jit(solution)/shard_map/ppermute | solution.py:21
  52.5 0.3 merge.7
  52.8 0.4 collective-permute-start.8
  53.2 0.2 merge.11.refs_2_
  53.4 5.5 %add_carry.2 = (bf16[128,4096]{1,0:T(8,128)(2,1)}, f32[128,256]{1,0:T(8,128)S(1)}) custom-call(bf16[128,256]{1,0:T(8,128)(2,1)S(1)} %get-tuple-element.53.refs_0_, f32[16,4096]{1,0:T(8,128)S(1)} %broadcast_multiply_fusion.refs_5_.refs_0_.refs_1_, f32[16,2048]{1,0:T(8,128)S(1)} %merge.11.refs_2_, f32[128,2048]{1,0:T(8,128)S(1)} %get-tuple-element.87.refs_3_, ...), custom_call_target="tpu_custom_call" | custom-call | flops 1258291200 | bytes 4194304 | tf_op jit(solution)/shard_map/add_carry/pallas_call | solution.py:407
  58.9 0.2 merge.8.refs_2_
  59.2 5.8 %add_carry.3 = (bf16[128,4096]{1,0:T(8,128)(2,1)}, f32[16,128]{1,0:T(8,128)S(1)}) custom-call(bf16[128,256]{1,0:T(8,128)(2,1)S(1)} %get-tuple-element.53.refs_0_, f32[16,4096]{1,0:T(8,128)S(1)} %broadcast_multiply_fusion.refs_5_.refs_0_.refs_1_, f32[16,2048]{1,0:T(8,128)S(1)} %merge.8.refs_2_, ...), custom_call_target="tpu_custom_call", output_to_operand_aliasing={{0}: (8, {})} | custom-call | flops 1258291200 | bytes 4194304 | tf_op jit(solution)/shard_map/add_carry/pallas_call | solution.py:407
  65.0 1.5 %collective-permute-start.15 = (f32[16,128]{1,0:T(8,128)S(1)}, f32[16,128]{1,0:T(8,128)S(1)}, u32[]{:S(2)}, u32[]{:S(2)}) collective-permute-start(f32[16,128]{1,0:T(8,128)S(1)} %get-tuple-element.93.refs_0_), channel_id=1, source_target_pairs={{0,2},{1,3},{2,0},{3,1},{4,6},{5,7},{6,4},{7,5},{8,10},{9,11},{10,... | collective-permute-start | bytes 24584 | tf_op jit(solution)/shard_map/ppermute | solution.py:21
  66.5 0.3 collective-permute-start.16
  66.9 1.8 %collective-permute-done.15.refs_2_ = f32[16,128]{1,0:T(8,128)S(1)} collective-permute-done((f32[16,128]{1,0:T(8,128)S(1)}, f32[16,128]{1,0:T(8,128)S(1)}, u32[]{:S(2)}, u32[]{:S(2)}) %collective-permute-start.15) | collective-permute-done | bytes 8224 | tf_op jit(solution)/shard_map/ppermute | solution.py:21
  68.7 0.9 %collective-permute-done.16.refs_3_ = f32[16,128]{1,0:T(8,128)S(1)} collective-permute-done((f32[16,128]{1,0:T(8,128)S(1)}, f32[16,128]{1,0:T(8,128)S(1)}, u32[]{:S(2)}, u32[]{:S(2)}) %collective-permute-start.16) | collective-permute-done | bytes 8224 | tf_op jit(solution)/shard_map/ppermute | solution.py:21
  69.6 0.2 weight_first.1
  69.9 12.3 %all_to_all.5 = bf16[8,16,512]{2,1,0:T(8,128)(2,1)S(1)} all-to-all(bf16[8,16,512]{2,1,0:T(8,128)(2,1)S(1)} %weight_first.1), channel_id=1, replica_groups=mesh['seq'=8,'tp'=4] {'seq'}, dimensions={0} | all-to-all | bytes 262144 | tf_op jit(solution)/shard_map/all_to_all | solution.py:512
  82.2 0.6 convert_reduce_fusion
  (17 shorter events, 0.1 us)
Async XLA Ops:
  1.5 6.4 %collective-permute-start = (bf16[8,4096]{1,0:T(8,128)(2,1)S(1)}, bf16[8,4096]{1,0:T(8,128)(2,1)S(1)}, u32[]{:S(2)}, u32[]{:S(2)}) collective-permute-start(bf16[8,4096]{1,0:T(8,128)(2,1)S(1)} %slice.3), channel_id=1, source_target_pairs={{0,4},{4,0},{8,12},{12,8},{16,20},{20,16},{24,28},{28,24},{1,5},{5... | collective-permute-start | bytes 196616 | tf_op jit(solution)/shard_map/ppermute | solution.py:548
  4.4 3.4 %collective-permute-start.1 = (bf16[8,4096]{1,0:T(8,128)(2,1)S(1)}, bf16[8,4096]{1,0:T(8,128)(2,1)S(1)}, u32[]{:S(2)}, u32[]{:S(2)}) collective-permute-start(bf16[8,4096]{1,0:T(8,128)(2,1)S(1)} %slice.3), channel_id=1, source_target_pairs={{4,8},{8,4},{12,16},{16,12},{20,24},{24,20},{5,9},{9,5},{13,17},{1... | collective-permute-start | bytes 196616 | tf_op jit(solution)/shard_map/ppermute | solution.py:548
  7.8 7.3 %copy-start.4 = (f32[16,4096]{1,0:T(8,128)S(1)}, f32[16,4096]{1,0:T(8,128)}, u32[]{:S(2)}) copy-start(f32[16,4096]{1,0:T(8,128)} %param.15) | copy-start | bytes 786436
  7.8 12.6 %copy-start = (bf16[512,4096]{1,0:T(8,128)(2,1)S(1)}, bf16[512,4096]{1,0:T(8,128)(2,1)}, u32[]{:S(2)}) copy-start(bf16[512,4096]{1,0:T(8,128)(2,1)} %refs_3_.3) | copy-start | bytes 12582916
  7.8 12.6 %copy-start.1 = (bf16[128,4096]{1,0:T(8,128)(2,1)S(1)}, bf16[128,4096]{1,0:T(8,128)(2,1)}, u32[]{:S(2)}) copy-start(bf16[128,4096]{1,0:T(8,128)(2,1)} %refs_5_.3) | copy-start | bytes 3145732
  7.8 12.6 %copy-start.2 = (f32[4096]{0:T(1024)S(1)}, f32[4096]{0:T(1024)}, u32[]{:S(2)}) copy-start(f32[4096]{0:T(1024)} %param.14) | copy-start | bytes 49156
  7.8 12.6 %copy-start.3 = (f32[4096]{0:T(1024)S(1)}, f32[4096]{0:T(1024)}, u32[]{:S(2)}) copy-start(f32[4096]{0:T(1024)} %param.16) | copy-start | bytes 49156
  11.7 1.7 %collective-permute-start.2 = (f32[128,544]{1,0:T(8,128)S(1)}, f32[128,544]{1,0:T(8,128)S(1)}, u32[]{:S(2)}, u32[]{:S(2)}) collective-permute-start(f32[128,544]{1,0:T(8,128)S(1)} %get-tuple-element.52.a_ref), channel_id=1, source_target_pairs={{0,1},{1,0},{2,3},{3,2},{4,5},{5,4},{6,7},{7,6},{8,9},{9,8},{10,11... | collective-permute-start | bytes 835592 | tf_op jit(solution)/shard_map/ppermute | solution.py:21
  13.5 6.3 %collective-permute-start.3 = (bf16[128,576]{1,0:T(8,128)(2,1)S(1)}, bf16[128,576]{1,0:T(8,128)(2,1)S(1)}, u32[]{:S(2)}, u32[]{:S(2)}) collective-permute-start(bf16[128,576]{1,0:T(8,128)(2,1)S(1)} %add_first.1.mine_ref), channel_id=1, source_target_pairs={{0,2},{1,3},{2,0},{3,1},{4,6},{5,7},{6,4},{7,5},{8,10},{9,11},{10,... | collective-permute-start | bytes 442376 | tf_op jit(solution)/shard_map/ppermute | solution.py:21
  26.5 12.4 %collective-permute-start.9 = (bf16[16,2048]{1,0:T(8,128)(2,1)S(1)}, bf16[16,2048]{1,0:T(8,128)(2,1)S(1)}, u32[]{:S(2)}, u32[]{:S(2)}) collective-permute-start(bf16[16,2048]{1,0:T(8,128)(2,1)S(1)} %get-tuple-element.76), channel_id=1, source_target_pairs={{0,4},{4,0},{8,12},{12,8},{16,20},{20,16},{24,28},{28,24},{1,5},{5... | collective-permute-start | bytes 196616 | tf_op jit(solution)/shard_map/ppermute | solution.py:21
  30.8 8.0 %collective-permute-start.10 = (f32[1,2048]{1,0:T(1,128)S(1)}, f32[1,2048]{1,0:T(1,128)S(1)}, u32[]{:S(2)}, u32[]{:S(2)}) collective-permute-start(f32[1,2048]{1,0:T(1,128)S(1)} %get-tuple-element.75.refs_2_), channel_id=1, source_target_pairs={{0,4},{4,0},{8,12},{12,8},{16,20},{20,16},{24,28},{28,24},{1,5},{5... | collective-permute-start | bytes 24584 | tf_op jit(solution)/shard_map/ppermute | solution.py:21
  36.8 7.7 %collective-permute-start.4 = (bf16[16,2048]{1,0:T(8,128)(2,1)S(1)}, bf16[16,2048]{1,0:T(8,128)(2,1)S(1)}, u32[]{:S(2)}, u32[]{:S(2)}) collective-permute-start(bf16[16,2048]{1,0:T(8,128)(2,1)S(1)} %get-tuple-element.61), channel_id=1, source_target_pairs={{0,4},{4,0},{8,12},{12,8},{16,20},{20,16},{24,28},{28,24},{1,5},{5... | collective-permute-start | bytes 196616 | tf_op jit(solution)/shard_map/ppermute | solution.py:21
  39.2 6.7 %collective-permute-start.11 = (bf16[16,2048]{1,0:T(8,128)(2,1)S(1)}, bf16[16,2048]{1,0:T(8,128)(2,1)S(1)}, u32[]{:S(2)}, u32[]{:S(2)}) collective-permute-start(bf16[16,2048]{1,0:T(8,128)(2,1)S(1)} %get-tuple-element.79), channel_id=1, source_target_pairs={{0,8},{4,12},{8,0},{12,4},{16,24},{20,28},{24,16},{28,20},{1,9},{5... | collective-permute-start | bytes 196616 | tf_op jit(solution)/shard_map/ppermute | solution.py:21
  40.8 3.7 %collective-permute-start.5 = (f32[1,2048]{1,0:T(1,128)S(1)}, f32[1,2048]{1,0:T(1,128)S(1)}, u32[]{:S(2)}, u32[]{:S(2)}) collective-permute-start(f32[1,2048]{1,0:T(1,128)S(1)} %get-tuple-element.60.refs_2_), channel_id=1, source_target_pairs={{0,4},{4,0},{8,12},{12,8},{16,20},{20,16},{24,28},{28,24},{1,5},{5... | collective-permute-start | bytes 24584 | tf_op jit(solution)/shard_map/ppermute | solution.py:21
  42.2 3.7 %collective-permute-start.12 = (f32[1,2048]{1,0:T(1,128)S(1)}, f32[1,2048]{1,0:T(1,128)S(1)}, u32[]{:S(2)}, u32[]{:S(2)}) collective-permute-start(f32[1,2048]{1,0:T(1,128)S(1)} %get-tuple-element.78.refs_2_), channel_id=1, source_target_pairs={{0,8},{4,12},{8,0},{12,4},{16,24},{20,28},{24,16},{28,20},{1,9},{5... | collective-permute-start | bytes 24584 | tf_op jit(solution)/shard_map/ppermute | solution.py:21
  44.8 7.7 %collective-permute-start.6 = (bf16[16,2048]{1,0:T(8,128)(2,1)S(1)}, bf16[16,2048]{1,0:T(8,128)(2,1)S(1)}, u32[]{:S(2)}, u32[]{:S(2)}) collective-permute-start(bf16[16,2048]{1,0:T(8,128)(2,1)S(1)} %get-tuple-element.64), channel_id=1, source_target_pairs={{0,8},{4,12},{8,0},{12,4},{16,24},{20,28},{24,16},{28,20},{1,9},{5... | collective-permute-start | bytes 196616 | tf_op jit(solution)/shard_map/ppermute | solution.py:21
  46.2 7.0 %collective-permute-start.13 = (bf16[16,2048]{1,0:T(8,128)(2,1)S(1)}, bf16[16,2048]{1,0:T(8,128)(2,1)S(1)}, u32[]{:S(2)}, u32[]{:S(2)}) collective-permute-start(bf16[16,2048]{1,0:T(8,128)(2,1)S(1)} %get-tuple-element.84), channel_id=1, source_target_pairs={{0,16},{4,20},{8,24},{12,28},{16,0},{20,4},{24,8},{28,12},{1,17},{... | collective-permute-start | bytes 196616 | tf_op jit(solution)/shard_map/ppermute | solution.py:21
  48.8 3.7 %collective-permute-start.7 = (f32[1,2048]{1,0:T(1,128)S(1)}, f32[1,2048]{1,0:T(1,128)S(1)}, u32[]{:S(2)}, u32[]{:S(2)}) collective-permute-start(f32[1,2048]{1,0:T(1,128)S(1)} %get-tuple-element.63.refs_2_), channel_id=1, source_target_pairs={{0,8},{4,12},{8,0},{12,4},{16,24},{20,28},{24,16},{28,20},{1,9},{5... | collective-permute-start | bytes 24584 | tf_op jit(solution)/shard_map/ppermute | solution.py:21
  52.8 6.1 %collective-permute-start.8 = (bf16[16,2048]{1,0:T(8,128)(2,1)S(1)}, bf16[16,2048]{1,0:T(8,128)(2,1)S(1)}, u32[]{:S(2)}, u32[]{:S(2)}) collective-permute-start(bf16[16,2048]{1,0:T(8,128)(2,1)S(1)} %get-tuple-element.69), channel_id=1, source_target_pairs={{0,16},{4,20},{8,24},{12,28},{16,0},{20,4},{24,8},{28,12},{1,17},{... | collective-permute-start | bytes 196616 | tf_op jit(solution)/shard_map/ppermute | solution.py:21
  65.0 1.9 %collective-permute-start.14 = (f32[16,128]{1,0:T(8,128)S(1)}, f32[16,128]{1,0:T(8,128)S(1)}, u32[]{:S(2)}, u32[]{:S(2)}) collective-permute-start(f32[16,128]{1,0:T(8,128)S(1)} %get-tuple-element.93.refs_0_), channel_id=1, source_target_pairs={{0,1},{1,0},{2,3},{3,2},{4,5},{5,4},{6,7},{7,6},{8,9},{9,8},{10,11... | collective-permute-start | bytes 24584 | tf_op jit(solution)/shard_map/ppermute | solution.py:21
  65.0 3.7 %collective-permute-start.15 = (f32[16,128]{1,0:T(8,128)S(1)}, f32[16,128]{1,0:T(8,128)S(1)}, u32[]{:S(2)}, u32[]{:S(2)}) collective-permute-start(f32[16,128]{1,0:T(8,128)S(1)} %get-tuple-element.93.refs_0_), channel_id=1, source_target_pairs={{0,2},{1,3},{2,0},{3,1},{4,6},{5,7},{6,4},{7,5},{8,10},{9,11},{10,... | collective-permute-start | bytes 24584 | tf_op jit(solution)/shard_map/ppermute | solution.py:21
  66.5 3.1 %collective-permute-start.16 = (f32[16,128]{1,0:T(8,128)S(1)}, f32[16,128]{1,0:T(8,128)S(1)}, u32[]{:S(2)}, u32[]{:S(2)}) collective-permute-start(f32[16,128]{1,0:T(8,128)S(1)} %get-tuple-element.93.refs_0_), channel_id=1, source_target_pairs={{0,3},{1,2},{2,1},{3,0},{4,7},{5,6},{6,5},{7,4},{8,11},{9,10},{10,... | collective-permute-start | bytes 24584 | tf_op jit(solution)/shard_map/ppermute | solution.py:21

commit v3 on v2

--- a/solution.py
+++ b/solution.py
@@ -227,19 +227,39 @@
     )(mine, other)
 
 
+def pack_sums(total_ref, send_ref, folded):
+    states, per = folded.shape
+    width = states * per
+    for n in range(states):
+        folded[n : n + 1, :] = total_ref[:, n * per : (n + 1) * per]
+    high = folded[...].astype(BF)
+    send_ref[:, width : width + per] = high
+    send_ref[:, width + per :] = (folded[...] - high.astype(F4)).astype(BF)
+
+
+def unpack_sums(got_ref, sum_ref, folded):
+    states, per = folded.shape
+    width = states * per
+    folded[...] = got_ref[:, width : width + per].astype(F4) + got_ref[:, width + per :].astype(F4)
+    for n in range(states):
+        sum_ref[:, n * per : (n + 1) * per] = folded[n : n + 1, :]
+
+
+def message_width(width, states):
+    return width + 2 * (width // states)
+
+
 def scan_kernel(
     base, fresh,
     proj_ref, b_ref, c_ref, dtw_ref, dtb_ref, rate_ref, skip_ref, conv_ref, grad_ref, pairs_in,
     mixed_ref, cum_ref, end_ref, send_ref, total_ref, pairs_ref,
-    raw, step, drive, even, odd,
+    raw, step, drive, folded, even, odd,
 ):
     rows = conv_ref.shape[0]
     states = rate_ref.shape[0]
     chunks = mixed_ref.shape[1] // WIDTH
     pairs_ref[...] = jnp.zeros_like(pairs_ref) if fresh else pairs_in[...]
-    tri = (
-        wide_iota((rows, 2 * rows), 0) >= wide_iota((rows, 2 * rows), 1) % rows
-    ).astype(BF)
+    tri = (wide_iota((rows, rows), 0) >= wide_iota((rows, rows), 1)).astype(BF)
 
     def project(i):
         raw[...] = jnp.dot(proj_ref[...], dtw_ref[:, chunk_at(i, base)], preferred_element_type=F4)
@@ -252,8 +272,7 @@
         at_in = chunk_at(i, base)
         bias = dtb_ref[:, at_in]
         skip = skip_ref[:, at_in]
-        highs = []
-        lows = []
+        rounded = []
         for top in range(0, rows, BLOCK):
             at = slice(top, top + BLOCK)
             now = softplus(raw[at, :] + bias)
@@ -261,11 +280,9 @@
             conv = conv_ref[at, at_in].astype(F4)
             drive[at, :] = now * conv
             mixed_ref[at, here] = skip * conv
-            high = now.astype(BF)
-            highs.append(high)
-            lows.append((now - high.astype(F4)).astype(BF))
+            rounded.append(now.astype(BF))
         cum_ref[:, here] = jnp.dot(
-            tri, jnp.concatenate(highs + lows, axis=0), preferred_element_type=F4
+            tri, jnp.concatenate(rounded, axis=0), preferred_element_type=F4
         )
         total_ref[:, here] = cum_ref[rows - 1 : rows, here]
         project(jnp.minimum(i + 1, chunks - 1))
@@ -289,6 +306,8 @@
         end_ref[:, here] = state
         send_ref[:, here] = state.astype(BF)
 
+    pack_sums(total_ref, send_ref, folded)
+
 
 def local_scan(base, width, prepared, dt_weight, dt_bias, rate, skip, conv_out, grad_out, pairs):
     rows = conv_out.shape[0]
@@ -314,7 +333,7 @@
             jax.ShapeDtypeStruct((rows, width), F4),
             jax.ShapeDtypeStruct((rows, width), F4),
             jax.ShapeDtypeStruct((states, width), F4),
-            jax.ShapeDtypeStruct((states, width), BF),
+            jax.ShapeDtypeStruct((states, message_width(width, states)), BF),
             jax.ShapeDtypeStruct((1, width), F4),
             jax.ShapeDtypeStruct((rows, wide), F4),
         ],
@@ -322,6 +341,7 @@
             pltpu.VMEM((rows, WIDTH), F4),
             pltpu.VMEM((rows, WIDTH), F4),
             pltpu.VMEM((rows, WIDTH), F4),
+            pltpu.VMEM((states, width // states), F4),
             pltpu.VMEM((wide, WIDTH), BF),
             pltpu.VMEM((wide, WIDTH), BF),
         ],
@@ -334,10 +354,10 @@
 
 
 def carry_kernel(
-    base, scale, fresh, final,
-    alt_ref, rate_ref, state_ref, cum_ref, mixed_ref, grad_ref, pairs_in, local_ref, prev_ref,
+    base, scale, final,
+    alt_ref, rate_ref, state_ref, cum_ref, mixed_ref, grad_ref, before_ref, local_ref, prev_ref,
     out_ref, result_ref,
-    pairs, rates, inits, even, odd,
+    sums, rates, inits, even, odd,
 ):
     rows = cum_ref.shape[0]
     states = rate_ref.shape[0]
@@ -346,7 +366,7 @@
 
     @pl.when(i == 0)
     def _():
-        pairs[...] = jnp.zeros_like(pairs) if fresh else pairs_in[...]
+        sums[...] = jnp.zeros_like(sums)
 
     here = chunk_at(i)
     at_in = chunk_at(i, base)
@@ -359,49 +379,59 @@
         hist = odd if (top // BLOCK) % 2 else even
         tokens = slice(top, top + BLOCK)
         cum = cum_ref[tokens, here].astype(BF)
+        grad = grad_ref[tokens, at_in]
         for n in range(states):
             at = slice(n * BLOCK, (n + 1) * BLOCK)
-            hist[at, :] = jnp.exp2(cum * rates[at, :]) * inits[at, :]
-        mixed, more = contract(hist[...], alt_ref[tokens, :], grad_ref[tokens, at_in])
+            now = jnp.exp2(cum * rates[at, :]) * inits[at, :]
+            hist[at, :] = now
+            pairs = now * grad
+            parts = [pairs[:, k : k + 128] for k in range(0, WIDTH, 128)]
+            while len(parts) > 1:
+                parts = [a + b for a, b in zip(parts[::2], parts[1::2])]
+            sums[n, tokens, :] += parts[0].astype(F4)
+        mixed = jnp.dot(alt_ref[tokens, :], hist[...], preferred_element_type=F4)
         out_ref[tokens, :] = (mixed_ref[tokens, here] + mixed).astype(BF)
-        pairs[tokens, :] += more
 
     @pl.when(i == pl.num_programs(0) - 1)
     def _():
-        if not final:
-            result_ref[...] = pairs[...]
-            return
-        lane = wide_iota((rows, wide), 1)
-        row = wide_iota((rows, wide), 0) % BLOCK
-        by_state = jnp.where(lane % BLOCK == row, pairs[...], 0.0) * scale
-        by_token = jnp.where(lane // states == row, local_ref[...], 0.0) * scale
-        lane = wide_iota((states, wide), 1)
-        row = wide_iota((states, wide), 0)
-        exact = dict(preferred_element_type=F4, precision=lax.Precision.HIGHEST)
-        result_ref[...] = lax.dot_general(
-            (lane // BLOCK == row).astype(F4), by_state, NT, **exact
-        ) + lax.dot_general((lane % states == row).astype(F4), by_token, NT, **exact)
-
-
-def add_carry(base, scale, alt, rate, incoming, cum, mixed, grad_out, pairs, local, prev):
+        ones = jnp.ones((8, 256), BF)
+        if final:
+            lane = wide_iota((rows, wide), 1)
+            row = wide_iota((rows, wide), 0) % BLOCK
+            by_token = jnp.where(lane // states == row, local_ref[...], 0.0)
+            pick = wide_iota((states, wide), 1) % states == wide_iota((states, wide), 0)
+            result_ref[...] = before_ref[...] + lax.dot_general(
+                pick.astype(F4), by_token, NT,
+                preferred_element_type=F4, precision=lax.Precision.HIGHEST,
+            )
+        else:
+            result_ref[...] = jnp.zeros_like(result_ref)
+        for n in range(states):
+            high = sums[n].astype(BF)
+            low = (sums[n] - high.astype(F4)).astype(BF)
+            both = jnp.concatenate([high, low], axis=1)
+            line = lax.dot_general(ones, both, NT, preferred_element_type=F4)
+            result_ref[n : n + 1, :] += line[0:1, :]
+        if final:
+            result_ref[...] = result_ref[...] * scale
+
+
+def add_carry(base, scale, alt, rate, incoming, cum, mixed, grad_out, before, local, prev):
     rows, width = cum.shape
     states, channels = rate.shape
     wide = BLOCK * states
-    fresh, final = pairs is None, local is not None
+    final = local is not None
     ops = [alt, rate, incoming, cum, mixed, grad_out]
-    extra = [pairs, local, prev]
     specs = in_vmem(6)
-    for a in extra:
-        if a is not None:
-            ops.append(a)
-            specs += [pl.BlockSpec(memory_space=pl.ANY)] if a is prev else in_vmem(1)
+    if final:
+        ops += [before, local, prev]
+        specs += in_vmem(2) + [pl.BlockSpec(memory_space=pl.ANY)]
 
     def body(*refs):
         refs = list(refs)
-        for k, a in enumerate(extra):
-            if a is None:
-                refs.insert(6 + k, None)
-        carry_kernel(base, scale, fresh, final, *refs)
+        if not final:
+            refs[6:6] = [None] * 3
+        carry_kernel(base, scale, final, *refs)
 
     work = rows * width * states
     return pl.pallas_call(
@@ -410,20 +440,20 @@
         in_specs=specs,
         out_specs=[
             pl.BlockSpec((rows, WIDTH), lambda i: (0, i + base)),
-            whole(states, rows) if final else whole(rows, wide),
+            whole(states, rows),
         ],
         out_shape=[
             jax.ShapeDtypeStruct((rows, channels), BF),
-            jax.ShapeDtypeStruct((states, rows) if final else (rows, wide), F4),
+            jax.ShapeDtypeStruct((states, rows), F4),
         ],
         scratch_shapes=[
-            pltpu.VMEM((rows, wide), F4),
+            pltpu.VMEM((states, rows, 128), F4),
             pltpu.VMEM((wide, WIDTH), BF),
             pltpu.VMEM((wide, WIDTH), BF),
             pltpu.VMEM((wide, WIDTH), BF),
             pltpu.VMEM((wide, WIDTH), BF),
         ],
-        input_output_aliases={} if prev is None else {len(ops) - 1: 0},
+        input_output_aliases={len(ops) - 1: 0} if final else {},
         compiler_params=params(),
         cost_estimate=pl.CostEstimate(
             flops=300 * work, bytes_accessed=work, transcendentals=work
@@ -432,46 +462,58 @@
     )(*ops)
 
 
-def merge_kernel(bit, last, rate_ref, end_ref, total_ref, other_ref, osum_ref, pre_ref, psum_ref, *outs):
+def merge_kernel(
+    base, bit, last, rate_ref, end_ref, total_ref, got_ref, pre_ref, psum_ref, *refs
+):
+    *outs, osum_ref, folded = refs
     later = (lax.axis_index("seq") & bit) != 0
-    rate = rate_ref[...]
-    fade = lambda s: jnp.exp2(rate * s)
-    other = other_ref[...].astype(F4)
-    prefix = pre_ref[...]
-    outs[0][...] = jnp.where(later, prefix + fade(psum_ref[...]) * other, prefix)
+    unpack_sums(got_ref, osum_ref, folded)
+    for i in range(end_ref.shape[1] // WIDTH):
+        at = slice(i * WIDTH, (i + 1) * WIDTH)
+        rate = rate_ref[:, (base + i) * WIDTH : (base + i + 1) * WIDTH]
+        fade = lambda s: jnp.exp2(rate * s)
+        other = got_ref[:, at].astype(F4)
+        prefix, before = pre_ref[:, at], psum_ref[:, at]
+        outs[0][:, at] = jnp.where(later, prefix + fade(before) * other, prefix)
+        if not last:
+            total, osum, end = total_ref[:, at], osum_ref[:, at], end_ref[:, at]
+            outs[1][:, at] = jnp.where(later, before + osum, before)
+            first = jnp.where(later, other, end)
+            second = jnp.where(later, end, other)
+            end = second + fade(jnp.where(later, total, osum)) * first
+            outs[2][:, at] = end
+            outs[3][:, at] = end.astype(BF)
+            outs[4][:, at] = total + osum
     if not last:
-        total, osum, end = total_ref[...], osum_ref[...], end_ref[...]
-        outs[1][...] = jnp.where(later, psum_ref[...] + osum, psum_ref[...])
-        first = jnp.where(later, other, end)
-        second = jnp.where(later, end, other)
-        end = second + fade(jnp.where(later, total, osum)) * first
-        outs[2][...] = end
-        outs[3][...] = end.astype(BF)
-        outs[4][...] = total + osum
-
-
-def merge(base, bit, last, rate, end, total, other, other_sum, prefix, prefix_sum):
-    states, channels = end.shape
-    many = jax.ShapeDtypeStruct((states, channels), F4)
-    one = jax.ShapeDtypeStruct((1, channels), F4)
-    outs = [many] if last else [many, one, many, jax.ShapeDtypeStruct((states, channels), BF), one]
-    wide, narrow = cols(states), cols(1)
+        pack_sums(outs[4], outs[3], folded)
+
+
+def merge(base, bit, last, rate, end, total, got, prefix, prefix_sum):
+    states, width = end.shape
+    outs = [jax.ShapeDtypeStruct((states, width), F4)]
+    if not last:
+        outs += [
+            jax.ShapeDtypeStruct((1, width), F4),
+            jax.ShapeDtypeStruct((states, width), F4),
+            jax.ShapeDtypeStruct(got.shape, BF),
+            jax.ShapeDtypeStruct((1, width), F4),
+        ]
 
     def body(*refs):
-        merge_kernel(bit, last, *refs)
+        merge_kernel(base, bit, last, *refs)
 
     return pl.pallas_call(
         body,
-        grid=(channels // WIDTH,),
-        in_specs=[
-            pl.BlockSpec((states, WIDTH), lambda i: (0, i + base)),
-            wide, narrow, wide, narrow, wide, narrow,
-        ],
-        out_specs=[wide] if last else [wide, narrow, wide, wide, narrow],
+        in_specs=in_vmem(6),
+        out_specs=in_vmem(len(outs)),
         out_shape=outs,
+        scratch_shapes=[
+            pltpu.VMEM((1, width), F4),
+            pltpu.VMEM((states, width // states), F4),
+        ],
         compiler_params=params(),
         name="merge",
-    )(rate, end, total, other, other_sum, prefix, prefix_sum)
+    )(rate, end, total, got, prefix, prefix_sum)
 
 
 def weight_first(parts, conv_out, count):
@@ -516,9 +558,8 @@
 def exchange(base, bit, rate, held):
     end, send, total, prefix, prefix_sum = held
     last = 2 * bit >= lax.axis_size("seq")
-    other = swap(send, "seq", bit)
-    other_sum = total if last else swap(total, "seq", bit)
-    outs = merge(base, bit, last, rate, end, total, other, other_sum, prefix, prefix_sum)
+    got = swap(send, "seq", bit)
+    outs = merge(base, bit, last, rate, end, total, got, prefix, prefix_sum)
     if last:
         return outs[0]
     prefix, prefix_sum, end, send, total = outs

time: 83.1 us -> 75.5 us (0.909)
  Pallas kernels: 32.5 us -> 27.6 us
  waiting for transfers between devices: 15 us -> 12 us
    pallas_call x2, Pallas kernels: 11.4 us -> 7.98 us  [add_carry(): pl.pallas_call(body, grid=(width // WIDTH,), in_specs=specs, out_specs=[p...]
    ppermute x15 -> x11, waiting for transfers between devices: 15 us -> 12 us  [swap(): return lax.ppermute(a, axis, [(i, i ^ bit) for i in range(count)])]
    pallas_call x6, Pallas kernels: 1.71 us -> 0.42 us  [merge(): pl.pallas_call(body, in_specs=in_vmem(6), out_specs=in_vmem(len(outs)), o...]
    ppermute x15 -> x11, starting transfers between devices: 16.9 us -> 17.8 us  [swap(): return lax.ppermute(a, axis, [(i, i ^ bit) for i in range(count)])]
  transfers between devices with their start and end apart: 17 -> 13, of which waited for: 7 -> 6; matrix products, arithmetic and copies ran while one was open for 0% -> 0% of each run, Pallas kernels for 19% -> 17%
where the time goes in v3:
time: 75.5 us; the launch traced here: 75.3 us
  Pallas kernels  27.6 us (37%)
  starting transfers between devices  21.4 us (28%)
  waiting for transfers between devices  12 us (16%)
  blocking collectives  11.9 us (16%)
  local copies, waits for them, and re-layouts  0.9 us (1%)
  between operations  0.8 us (1%)
    ppermute x11, starting transfers between devices, swap(): return lax.ppermute(a, axis, [(i, i ^ bit) for i in range(count)])  17.8 us
    ppermute x11, waiting for transfers between devices, swap(): return lax.ppermute(a, axis, [(i, i ^ bit) for i in range(count)])  12 us
    all_to_all x1, blocking collectives, weight_gradient(): weight = lax.all_to_all(weight, 'seq', 0, 0)  11.9 us
    pallas_call x2, Pallas kernels, local_scan(): pl.pallas_call(body, in_specs=in_vmem(len(ops)), out_specs=in_vmem(6), ou...  11.7 us
    pallas_call x2, Pallas kernels, add_carry(): pl.pallas_call(body, grid=(width // WIDTH,), in_specs=specs, out_specs=[p...  7.98 us
    pallas_call x1, Pallas kernels, conv_project(): pl.pallas_call(conv_kernel, in_specs=in_vmem(6), out_specs=in_vmem(2), ou...  3.8 us
    ppermute x2, starting transfers between devices, on_device(): lax.ppermute(edge, 'seq', [p for i in range(k, count - 1, 2) for p in ((i...  3.62 us
    pallas_call x1, Pallas kernels, fetch(): pl.pallas_call(body, in_specs=[pl.BlockSpec(memory_space=pltpu.HBM)] * co...  2.66 us
  transfers between devices with their start and end apart: 13, of which 6 were waited for; matrix products, arithmetic and copies ran while one was open for 0% of the time, Pallas kernels for 17%

profile of v3, /device:TPU:0, one launch (start us, length us, event | category | flops | bytes accessed | tf_op | source)
XLA Modules:
  0.0 75.3 jit_solution(9561914708303853410)
XLA Ops:
  0.6 0.8 %slice.3 = bf16[8,4096]{1,0:T(8,128)(2,1)S(1)} slice(bf16[128,4096]{1,0:T(8,128)(2,1)} %refs_0_.1), slice={[120:128], [0:4096]} | slice | bytes 131072 | tf_op jit(solution)/shard_map/slice | solution.py:587
  1.5 3.0 %collective-permute-start = (bf16[8,4096]{1,0:T(8,128)(2,1)S(1)}, bf16[8,4096]{1,0:T(8,128)(2,1)S(1)}, u32[]{:S(2)}, u32[]{:S(2)}) collective-permute-start(bf16[8,4096]{1,0:T(8,128)(2,1)S(1)} %slice.3), channel_id=1, source_target_pairs={{0,4},{4,0},{8,12},{12,8},{16,20},{20,16},{24,28},{28,24},{1,5},{5... | collective-permute-start | bytes 196616 | tf_op jit(solution)/shard_map/ppermute | solution.py:589
  4.4 0.7 collective-permute-start.1
  5.1 2.7 %fetch.1 = (bf16[128,4096]{1,0:T(8,128)(2,1)S(1)}, f32[4,4096]{1,0:T(4,128)S(1)}, f32[1,4096]{1,0:T(1,128)S(1)}, bf16[544,4096]{1,0:T(8,128)(2,1)S(1)}) custom-call(bf16[128,4096]{1,0:T(8,128)(2,1)} %refs_0_.1, f32[4,4096]{1,0:T(4,128)} %refs_1_.1, f32[1,4096]{1,0:T(1,128)} %bitcast.13, bf16[544,4096]{1,0:T(8,128)(2,1)} %bitcast.11), custom_call_target="tpu_custom_call" | custom-call | bytes 11173888 | tf_op jit(solution)/shard_map/fetch/pallas_call | solution.py:50
  7.8 0.0 copy-start.4
  7.8 0.0 copy-start
  7.8 0.0 copy-start.1
  7.8 0.0 copy-start.2
  7.8 0.0 copy-start.3
  7.8 0.0 collective-permute-done.odd_ref
  7.8 0.0 collective-permute-done.1.even_ref
  7.9 3.8 %conv_project.1 = (bf16[128,4096]{1,0:T(8,128)(2,1)S(1)}, f32[128,544]{1,0:T(8,128)S(1)}) custom-call(bf16[128,4096]{1,0:T(8,128)(2,1)S(1)} %get-tuple-element.48.x_ref, bf16[8,4096]{1,0:T(8,128)(2,1)S(1)} %collective-permute-done.odd_ref, bf16[8,4096]{1,0:T(8,128)(2,1)S(1)} %collective-permute-done.1.even_ref, f32[4,4096]{1,0:T(4,128)S(1)} %get-tuple-element.49.w_ref, ...), custom_call_target="tpu_custom_call" | custom-call | tf_op jit(solution)/shard_map/conv_project/pallas_call | solution.py:101
  11.7 0.1 collective-permute-start.2
  11.7 1.6 %collective-permute-done.2.b_ref = f32[128,544]{1,0:T(8,128)S(1)} collective-permute-done((f32[128,544]{1,0:T(8,128)S(1)}, f32[128,544]{1,0:T(8,128)S(1)}, u32[]{:S(2)}, u32[]{:S(2)}) %collective-permute-start.2) | collective-permute-done | bytes 278560 | tf_op jit(solution)/shard_map/ppermute | solution.py:21
  13.4 0.1 add_first.1.mine_ref
  13.5 1.6 %collective-permute-start.3 = (bf16[128,576]{1,0:T(8,128)(2,1)S(1)}, bf16[128,576]{1,0:T(8,128)(2,1)S(1)}, u32[]{:S(2)}, u32[]{:S(2)}) collective-permute-start(bf16[128,576]{1,0:T(8,128)(2,1)S(1)} %add_first.1.mine_ref), channel_id=1, source_target_pairs={{0,2},{1,3},{2,0},{3,1},{4,6},{5,7},{6,4},{7,5},{8,10},{9,11},{10,... | collective-permute-start | bytes 442376 | tf_op jit(solution)/shard_map/ppermute | solution.py:21
  15.1 0.0 copy-done.4
  15.1 4.7 %collective-permute-done.3.other_ref = bf16[128,576]{1,0:T(8,128)(2,1)S(1)} collective-permute-done((bf16[128,576]{1,0:T(8,128)(2,1)S(1)}, bf16[128,576]{1,0:T(8,128)(2,1)S(1)}, u32[]{:S(2)}, u32[]{:S(2)}) %collective-permute-start.3) | collective-permute-done | bytes 147488 | tf_op jit(solution)/shard_map/ppermute | solution.py:21
  19.8 0.6 prepare.1
  20.5 5.9 %local_scan.2 = (f32[128,2048]{1,0:T(8,128)S(1)}, f32[128,2048]{1,0:T(8,128)S(1)}, f32[16,2048]{1,0:T(8,128)S(1)}, bf16[16,2304]{1,0:T(8,128)(2,1)S(1)}, f32[1,2048]{1,0:T(1,128)S(1)}, /*index=5*/f32[128,256]{1,0:T(8,128)S(1)}) custom-call(bf16[128,512]{1,0:T(8,128)(2,1)S(1)} %get-tuple-element.54.refs_0_, f32[2048,128]{1,0:T(8,128)S(1)} %get-tuple-element.55.refs_1_, ...), custom_call_target="tpu_custom_call" | custom-call | flops 2516582400 | bytes 4194304 | tf_op jit(solution)/shard_map/local_scan/pallas_call | solution.py:328
  26.3 4.3 %collective-permute-start.7 = (bf16[16,2304]{1,0:T(8,128)(2,1)S(1)}, bf16[16,2304]{1,0:T(8,128)(2,1)S(1)}, u32[]{:S(2)}, u32[]{:S(2)}) collective-permute-start(bf16[16,2304]{1,0:T(8,128)(2,1)S(1)} %get-tuple-element.76), channel_id=1, source_target_pairs={{0,4},{4,0},{8,12},{12,8},{16,20},{20,16},{24,28},{28,24},{1,5},{5... | collective-permute-start | bytes 221192 | tf_op jit(solution)/shard_map/ppermute | solution.py:21
  30.6 5.9 %local_scan.3 = (f32[128,2048]{1,0:T(8,128)S(1)}, f32[128,2048]{1,0:T(8,128)S(1)}, f32[16,2048]{1,0:T(8,128)S(1)}, bf16[16,2304]{1,0:T(8,128)(2,1)S(1)}, f32[1,2048]{1,0:T(1,128)S(1)}, /*index=5*/f32[128,256]{1,0:T(8,128)S(1)}) custom-call(bf16[128,512]{1,0:T(8,128)(2,1)S(1)} %get-tuple-element.54.refs_0_, f32[2048,128]{1,0:T(8,128)S(1)} %get-tuple-element.55.refs_1_, ...), custom_call_target="tpu_custom_call" | custom-call | flops 2516582400 | bytes 4194304 | tf_op jit(solution)/shard_map/local_scan/pallas_call | solution.py:328
  36.5 0.0 collective-permute-start.4
  36.5 0.0 collective-permute-done.7.refs_3_
  36.6 0.1 merge.9
  36.6 3.0 %collective-permute-start.8 = (bf16[16,2304]{1,0:T(8,128)(2,1)S(1)}, bf16[16,2304]{1,0:T(8,128)(2,1)S(1)}, u32[]{:S(2)}, u32[]{:S(2)}) collective-permute-start(bf16[16,2304]{1,0:T(8,128)(2,1)S(1)} %get-tuple-element.79), channel_id=1, source_target_pairs={{0,8},{4,12},{8,0},{12,4},{16,24},{20,28},{24,16},{28,20},{1,9},{5... | collective-permute-start | bytes 221192 | tf_op jit(solution)/shard_map/ppermute | solution.py:21
  39.6 1.2 %collective-permute-done.4.refs_3_ = bf16[16,2304]{1,0:T(8,128)(2,1)S(1)} collective-permute-done((bf16[16,2304]{1,0:T(8,128)(2,1)S(1)}, bf16[16,2304]{1,0:T(8,128)(2,1)S(1)}, u32[]{:S(2)}, u32[]{:S(2)}) %collective-permute-start.4) | collective-permute-done | bytes 73760 | tf_op jit(solution)/shard_map/ppermute | solution.py:21
  40.9 0.1 merge.6
  41.0 1.6 %collective-permute-start.5 = (bf16[16,2304]{1,0:T(8,128)(2,1)S(1)}, bf16[16,2304]{1,0:T(8,128)(2,1)S(1)}, u32[]{:S(2)}, u32[]{:S(2)}) collective-permute-start(bf16[16,2304]{1,0:T(8,128)(2,1)S(1)} %get-tuple-element.64), channel_id=1, source_target_pairs={{0,8},{4,12},{8,0},{12,4},{16,24},{20,28},{24,16},{28,20},{1,9},{5... | collective-permute-start | bytes 221192 | tf_op jit(solution)/shard_map/ppermute | solution.py:21
  42.6 0.0 collective-permute-done.8.refs_3_
  42.6 0.1 merge.10
  42.7 3.2 %collective-permute-start.9 = (bf16[16,2304]{1,0:T(8,128)(2,1)S(1)}, bf16[16,2304]{1,0:T(8,128)(2,1)S(1)}, u32[]{:S(2)}, u32[]{:S(2)}) collective-permute-start(bf16[16,2304]{1,0:T(8,128)(2,1)S(1)} %get-tuple-element.84), channel_id=1, source_target_pairs={{0,16},{4,20},{8,24},{12,28},{16,0},{20,4},{24,8},{28,12},{1,17},{... | collective-permute-start | bytes 221192 | tf_op jit(solution)/shard_map/ppermute | solution.py:21
  45.9 0.0 collective-permute-done.5.refs_3_
  45.9 0.1 merge.7
  46.0 2.1 %collective-permute-start.6 = (bf16[16,2304]{1,0:T(8,128)(2,1)S(1)}, bf16[16,2304]{1,0:T(8,128)(2,1)S(1)}, u32[]{:S(2)}, u32[]{:S(2)}) collective-permute-start(bf16[16,2304]{1,0:T(8,128)(2,1)S(1)} %get-tuple-element.69), channel_id=1, source_target_pairs={{0,16},{4,20},{8,24},{12,28},{16,0},{20,4},{24,8},{28,12},{1,17},{... | collective-permute-start | bytes 221192 | tf_op jit(solution)/shard_map/ppermute | solution.py:21
  48.1 1.7 %collective-permute-done.9.refs_3_ = bf16[16,2304]{1,0:T(8,128)(2,1)S(1)} collective-permute-done((bf16[16,2304]{1,0:T(8,128)(2,1)S(1)}, bf16[16,2304]{1,0:T(8,128)(2,1)S(1)}, u32[]{:S(2)}, u32[]{:S(2)}) %collective-permute-start.9) | collective-permute-done | bytes 73760 | tf_op jit(solution)/shard_map/ppermute | solution.py:21
  49.8 3.9 %add_carry.2 = (bf16[128,4096]{1,0:T(8,128)(2,1)}, f32[16,128]{1,0:T(8,128)S(1)}) custom-call(bf16[128,256]{1,0:T(8,128)(2,1)S(1)} %get-tuple-element.53.refs_0_, f32[16,4096]{1,0:T(8,128)S(1)} %broadcast_multiply_fusion.refs_5_.refs_0_.refs_1_, f32[16,2048]{1,0:T(8,128)S(1)} %merge.11.refs_2_, f32[128,2048]{1,0:T(8,128)S(1)} %get-tuple-element.87.refs_3_, ...), custom_call_target="tpu_custom_call" | custom-call | flops 1258291200 | bytes 4194304 | tf_op jit(solution)/shard_map/add_carry/pallas_call | solution.py:437
  53.8 0.0 collective-permute-done.6.refs_3_
  53.8 4.1 %add_carry.3 = (bf16[128,4096]{1,0:T(8,128)(2,1)}, f32[16,128]{1,0:T(8,128)S(1)}) custom-call(bf16[128,256]{1,0:T(8,128)(2,1)S(1)} %get-tuple-element.53.refs_0_, f32[16,4096]{1,0:T(8,128)S(1)} %broadcast_multiply_fusion.refs_5_.refs_0_.refs_1_, f32[16,2048]{1,0:T(8,128)S(1)} %merge.8.refs_2_, ...), custom_call_target="tpu_custom_call", output_to_operand_aliasing={{0}: (8, {})} | custom-call | flops 1258291200 | bytes 4194304 | tf_op jit(solution)/shard_map/add_carry/pallas_call | solution.py:437
  57.9 0.0 collective-permute-start.10
  57.9 1.5 %collective-permute-start.11 = (f32[16,128]{1,0:T(8,128)S(1)}, f32[16,128]{1,0:T(8,128)S(1)}, u32[]{:S(2)}, u32[]{:S(2)}) collective-permute-start(f32[16,128]{1,0:T(8,128)S(1)} %get-tuple-element.93.refs_0_), channel_id=1, source_target_pairs={{0,2},{1,3},{2,0},{3,1},{4,6},{5,7},{6,4},{7,5},{8,10},{9,11},{10,... | collective-permute-start | bytes 24584 | tf_op jit(solution)/shard_map/ppermute | solution.py:21
  59.4 0.3 collective-permute-start.12
  59.7 0.0 collective-permute-done.10.refs_1_
  59.7 1.8 %collective-permute-done.11.refs_2_ = f32[16,128]{1,0:T(8,128)S(1)} collective-permute-done((f32[16,128]{1,0:T(8,128)S(1)}, f32[16,128]{1,0:T(8,128)S(1)}, u32[]{:S(2)}, u32[]{:S(2)}) %collective-permute-start.11) | collective-permute-done | bytes 8224 | tf_op jit(solution)/shard_map/ppermute | solution.py:21
  61.5 1.0 %collective-permute-done.12.refs_3_ = f32[16,128]{1,0:T(8,128)S(1)} collective-permute-done((f32[16,128]{1,0:T(8,128)S(1)}, f32[16,128]{1,0:T(8,128)S(1)}, u32[]{:S(2)}, u32[]{:S(2)}) %collective-permute-start.12) | collective-permute-done | bytes 8224 | tf_op jit(solution)/shard_map/ppermute | solution.py:21
  62.5 0.2 weight_first.1
  62.7 11.9 %all_to_all.5 = bf16[8,16,512]{2,1,0:T(8,128)(2,1)S(1)} all-to-all(bf16[8,16,512]{2,1,0:T(8,128)(2,1)S(1)} %weight_first.1), channel_id=1, replica_groups=mesh['seq'=8,'tp'=4] {'seq'}, dimensions={0} | all-to-all | bytes 262144 | tf_op jit(solution)/shard_map/all_to_all | solution.py:554
  74.6 0.6 convert_reduce_fusion
  (9 shorter events, 0.1 us)
Async XLA Ops:
  1.5 6.4 %collective-permute-start = (bf16[8,4096]{1,0:T(8,128)(2,1)S(1)}, bf16[8,4096]{1,0:T(8,128)(2,1)S(1)}, u32[]{:S(2)}, u32[]{:S(2)}) collective-permute-start(bf16[8,4096]{1,0:T(8,128)(2,1)S(1)} %slice.3), channel_id=1, source_target_pairs={{0,4},{4,0},{8,12},{12,8},{16,20},{20,16},{24,28},{28,24},{1,5},{5... | collective-permute-start | bytes 196616 | tf_op jit(solution)/shard_map/ppermute | solution.py:589
  4.4 3.4 %collective-permute-start.1 = (bf16[8,4096]{1,0:T(8,128)(2,1)S(1)}, bf16[8,4096]{1,0:T(8,128)(2,1)S(1)}, u32[]{:S(2)}, u32[]{:S(2)}) collective-permute-start(bf16[8,4096]{1,0:T(8,128)(2,1)S(1)} %slice.3), channel_id=1, source_target_pairs={{4,8},{8,4},{12,16},{16,12},{20,24},{24,20},{5,9},{9,5},{13,17},{1... | collective-permute-start | bytes 196616 | tf_op jit(solution)/shard_map/ppermute | solution.py:589
  7.8 7.3 %copy-start.4 = (f32[16,4096]{1,0:T(8,128)S(1)}, f32[16,4096]{1,0:T(8,128)}, u32[]{:S(2)}) copy-start(f32[16,4096]{1,0:T(8,128)} %param.15) | copy-start | bytes 786436
  7.8 12.6 %copy-start = (bf16[512,4096]{1,0:T(8,128)(2,1)S(1)}, bf16[512,4096]{1,0:T(8,128)(2,1)}, u32[]{:S(2)}) copy-start(bf16[512,4096]{1,0:T(8,128)(2,1)} %refs_3_.3) | copy-start | bytes 12582916
  7.8 12.6 %copy-start.1 = (bf16[128,4096]{1,0:T(8,128)(2,1)S(1)}, bf16[128,4096]{1,0:T(8,128)(2,1)}, u32[]{:S(2)}) copy-start(bf16[128,4096]{1,0:T(8,128)(2,1)} %refs_5_.3) | copy-start | bytes 3145732
  7.8 12.6 %copy-start.2 = (f32[4096]{0:T(1024)S(1)}, f32[4096]{0:T(1024)}, u32[]{:S(2)}) copy-start(f32[4096]{0:T(1024)} %param.14) | copy-start | bytes 49156
  7.8 12.6 %copy-start.3 = (f32[4096]{0:T(1024)S(1)}, f32[4096]{0:T(1024)}, u32[]{:S(2)}) copy-start(f32[4096]{0:T(1024)} %param.16) | copy-start | bytes 49156
  11.7 1.7 %collective-permute-start.2 = (f32[128,544]{1,0:T(8,128)S(1)}, f32[128,544]{1,0:T(8,128)S(1)}, u32[]{:S(2)}, u32[]{:S(2)}) collective-permute-start(f32[128,544]{1,0:T(8,128)S(1)} %get-tuple-element.52.a_ref), channel_id=1, source_target_pairs={{0,1},{1,0},{2,3},{3,2},{4,5},{5,4},{6,7},{7,6},{8,9},{9,8},{10,11... | collective-permute-start | bytes 835592 | tf_op jit(solution)/shard_map/ppermute | solution.py:21
  13.5 6.3 %collective-permute-start.3 = (bf16[128,576]{1,0:T(8,128)(2,1)S(1)}, bf16[128,576]{1,0:T(8,128)(2,1)S(1)}, u32[]{:S(2)}, u32[]{:S(2)}) collective-permute-start(bf16[128,576]{1,0:T(8,128)(2,1)S(1)} %add_first.1.mine_ref), channel_id=1, source_target_pairs={{0,2},{1,3},{2,0},{3,1},{4,6},{5,7},{6,4},{7,5},{8,10},{9,11},{10,... | collective-permute-start | bytes 442376 | tf_op jit(solution)/shard_map/ppermute | solution.py:21
  26.3 10.2 %collective-permute-start.7 = (bf16[16,2304]{1,0:T(8,128)(2,1)S(1)}, bf16[16,2304]{1,0:T(8,128)(2,1)S(1)}, u32[]{:S(2)}, u32[]{:S(2)}) collective-permute-start(bf16[16,2304]{1,0:T(8,128)(2,1)S(1)} %get-tuple-element.76), channel_id=1, source_target_pairs={{0,4},{4,0},{8,12},{12,8},{16,20},{20,16},{24,28},{28,24},{1,5},{5... | collective-permute-start | bytes 221192 | tf_op jit(solution)/shard_map/ppermute | solution.py:21
  36.5 4.4 %collective-permute-start.4 = (bf16[16,2304]{1,0:T(8,128)(2,1)S(1)}, bf16[16,2304]{1,0:T(8,128)(2,1)S(1)}, u32[]{:S(2)}, u32[]{:S(2)}) collective-permute-start(bf16[16,2304]{1,0:T(8,128)(2,1)S(1)} %get-tuple-element.61), channel_id=1, source_target_pairs={{0,4},{4,0},{8,12},{12,8},{16,20},{20,16},{24,28},{28,24},{1,5},{5... | collective-permute-start | bytes 221192 | tf_op jit(solution)/shard_map/ppermute | solution.py:21
  36.6 5.9 %collective-permute-start.8 = (bf16[16,2304]{1,0:T(8,128)(2,1)S(1)}, bf16[16,2304]{1,0:T(8,128)(2,1)S(1)}, u32[]{:S(2)}, u32[]{:S(2)}) collective-permute-start(bf16[16,2304]{1,0:T(8,128)(2,1)S(1)} %get-tuple-element.79), channel_id=1, source_target_pairs={{0,8},{4,12},{8,0},{12,4},{16,24},{20,28},{24,16},{28,20},{1,9},{5... | collective-permute-start | bytes 221192 | tf_op jit(solution)/shard_map/ppermute | solution.py:21
  41.0 4.9 %collective-permute-start.5 = (bf16[16,2304]{1,0:T(8,128)(2,1)S(1)}, bf16[16,2304]{1,0:T(8,128)(2,1)S(1)}, u32[]{:S(2)}, u32[]{:S(2)}) collective-permute-start(bf16[16,2304]{1,0:T(8,128)(2,1)S(1)} %get-tuple-element.64), channel_id=1, source_target_pairs={{0,8},{4,12},{8,0},{12,4},{16,24},{20,28},{24,16},{28,20},{1,9},{5... | collective-permute-start | bytes 221192 | tf_op jit(solution)/shard_map/ppermute | solution.py:21
  42.7 7.1 %collective-permute-start.9 = (bf16[16,2304]{1,0:T(8,128)(2,1)S(1)}, bf16[16,2304]{1,0:T(8,128)(2,1)S(1)}, u32[]{:S(2)}, u32[]{:S(2)}) collective-permute-start(bf16[16,2304]{1,0:T(8,128)(2,1)S(1)} %get-tuple-element.84), channel_id=1, source_target_pairs={{0,16},{4,20},{8,24},{12,28},{16,0},{20,4},{24,8},{28,12},{1,17},{... | collective-permute-start | bytes 221192 | tf_op jit(solution)/shard_map/ppermute | solution.py:21
  46.0 7.8 %collective-permute-start.6 = (bf16[16,2304]{1,0:T(8,128)(2,1)S(1)}, bf16[16,2304]{1,0:T(8,128)(2,1)S(1)}, u32[]{:S(2)}, u32[]{:S(2)}) collective-permute-start(bf16[16,2304]{1,0:T(8,128)(2,1)S(1)} %get-tuple-element.69), channel_id=1, source_target_pairs={{0,16},{4,20},{8,24},{12,28},{16,0},{20,4},{24,8},{28,12},{1,17},{... | collective-permute-start | bytes 221192 | tf_op jit(solution)/shard_map/ppermute | solution.py:21
  57.9 1.9 %collective-permute-start.10 = (f32[16,128]{1,0:T(8,128)S(1)}, f32[16,128]{1,0:T(8,128)S(1)}, u32[]{:S(2)}, u32[]{:S(2)}) collective-permute-start(f32[16,128]{1,0:T(8,128)S(1)} %get-tuple-element.93.refs_0_), channel_id=1, source_target_pairs={{0,1},{1,0},{2,3},{3,2},{4,5},{5,4},{6,7},{7,6},{8,9},{9,8},{10,11... | collective-permute-start | bytes 24584 | tf_op jit(solution)/shard_map/ppermute | solution.py:21
  57.9 3.7 %collective-permute-start.11 = (f32[16,128]{1,0:T(8,128)S(1)}, f32[16,128]{1,0:T(8,128)S(1)}, u32[]{:S(2)}, u32[]{:S(2)}) collective-permute-start(f32[16,128]{1,0:T(8,128)S(1)} %get-tuple-element.93.refs_0_), channel_id=1, source_target_pairs={{0,2},{1,3},{2,0},{3,1},{4,6},{5,7},{6,4},{7,5},{8,10},{9,11},{10,... | collective-permute-start | bytes 24584 | tf_op jit(solution)/shard_map/ppermute | solution.py:21
  59.4 3.1 %collective-permute-start.12 = (f32[16,128]{1,0:T(8,128)S(1)}, f32[16,128]{1,0:T(8,128)S(1)}, u32[]{:S(2)}, u32[]{:S(2)}) collective-permute-start(f32[16,128]{1,0:T(8,128)S(1)} %get-tuple-element.93.refs_0_), channel_id=1, source_target_pairs={{0,3},{1,2},{2,1},{3,0},{4,7},{5,6},{6,5},{7,4},{8,11},{9,10},{10,... | collective-permute-start | bytes 24584 | tf_op jit(solution)/shard_map/ppermute | solution.py:21

commit v4 on v3

--- a/solution.py
+++ b/solution.py
@@ -33,41 +33,86 @@
     return pl.BlockSpec((rows, lanes), lambda i: (0, 0))
 
 
-def fetch(*arrays):
-    count = len(arrays)
-
-    def body(*refs):
-        sems = refs[-1]
-        copies = [
-            pltpu.make_async_copy(refs[i], refs[count + i], sems.at[i]) for i in range(count)
-        ]
-        for copy in copies:
-            copy.start()
-        for copy in copies:
-            copy.wait()
-
-    moved = 2 * sum(a.size * a.dtype.itemsize for a in arrays)
-    return pl.pallas_call(
-        body,
-        in_specs=[pl.BlockSpec(memory_space=pltpu.HBM)] * count,
-        out_specs=in_vmem(count),
-        out_shape=[pltpu.VMEM(a.shape, a.dtype) for a in arrays],
-        scratch_shapes=[pltpu.SemaphoreType.DMA((count,))],
-        compiler_params=params(1 << 20),
-        cost_estimate=pl.CostEstimate(flops=0, bytes_accessed=moved, transcendentals=0),
-        name="fetch",
-    )(*[in_hbm(a) for a in arrays])
-
-
 def chunk_at(i, base=0):
     return pl.ds(pl.multiple_of((base + i) * WIDTH, WIDTH), WIDTH)
 
 
-def conv_kernel(x_ref, odd_ref, even_ref, w_ref, bias_ref, proj_ref, out_ref, part_ref, ext):
+def conv_rows(ext, j, weights, bias, tops, base):
+    for top in tops:
+        acc = bias
+        for tap in range(weights.shape[0]):
+            at = base + top + tap
+            acc = acc + weights[tap : tap + 1, :] * ext[j, at : at + BLOCK, :]
+        half = 0.5 * acc
+        yield top, (half + half * jnp.tanh(half)).astype(BF)
+
+
+def conv_body_kernel(
+    x_hbm, w_hbm, bias_hbm, proj_hbm, x_ref, w_ref, bias_ref, proj_ref, out_ref,
+    ext, sems, x_sems,
+):
     rows, channels = x_ref.shape
+    chunks = channels // WIDTH
+
+    def x_copy(i):
+        at = chunk_at(i)
+        return pltpu.make_async_copy(x_hbm.at[:, at], x_ref.at[:, at], x_sems.at[i])
+
+    w_copy = pltpu.make_async_copy(w_hbm, w_ref, sems.at[0])
+    bias_copy = pltpu.make_async_copy(bias_hbm, bias_ref, sems.at[1])
+    proj_copy = pltpu.make_async_copy(proj_hbm, proj_ref, sems.at[2])
+    w_copy.start()
+    bias_copy.start()
+    for i in range(chunks):
+        x_copy(i).start()
+    proj_copy.start()
+    w_copy.wait()
+    bias_copy.wait()
+
+    @pl.loop(0, chunks)
+    def _(i):
+        x_copy(i).wait()
+        for j in range(WIDTH // 128):
+            lanes = pl.ds(pl.multiple_of(i * WIDTH + j * 128, 128), 128)
+            ext[j] = x_ref[:, lanes].astype(F4)
+            base = 1 - w_ref.shape[0]
+            tops = range(BLOCK, rows, BLOCK)
+            for top, out in conv_rows(ext, j, w_ref[:, lanes], bias_ref[:, lanes], tops, base):
+                out_ref[top : top + BLOCK, lanes] = out
+            out_ref[0:BLOCK, lanes] = jnp.zeros((BLOCK, 128), BF)
+
+    proj_copy.wait()
+
+
+def conv_body(conv_in, conv_weight, conv_bias, proj_weight_t):
+    arrays = (conv_in, conv_weight, conv_bias, proj_weight_t)
+    rows, channels = conv_in.shape
+    moved = 2 * sum(a.size * a.dtype.itemsize for a in arrays)
+    return pl.pallas_call(
+        conv_body_kernel,
+        in_specs=[pl.BlockSpec(memory_space=pltpu.HBM)] * 4,
+        out_specs=in_vmem(5),
+        out_shape=[pltpu.VMEM(a.shape, a.dtype) for a in arrays]
+        + [pltpu.VMEM((rows, channels), BF)],
+        scratch_shapes=[
+            pltpu.VMEM((WIDTH // 128, rows, 128), F4),
+            pltpu.SemaphoreType.DMA((3,)),
+            pltpu.SemaphoreType.DMA((channels // WIDTH,)),
+        ],
+        compiler_params=params(),
+        cost_estimate=pl.CostEstimate(
+            flops=20 * rows * channels, bytes_accessed=moved, transcendentals=rows * channels
+        ),
+        name="conv_body",
+    )(*[in_hbm(a) for a in arrays])
+
+
+def conv_kernel(
+    x_ref, odd_ref, even_ref, w_ref, bias_ref, proj_ref, conv_ref, out_ref, part_ref, ext
+):
+    rows, channels = out_ref.shape
     rim = odd_ref.shape[0]
-    taps = w_ref.shape[0]
-    base = rim - (taps - 1)
+    base = rim - (w_ref.shape[0] - 1)
     odd = (lax.axis_index("seq") & 1) != 0
     part_ref[...] = jnp.zeros_like(part_ref)
 
@@ -78,38 +123,32 @@
             ext[j, 0:rim, :] = jnp.where(
                 odd, odd_ref[:, lanes].astype(F4), even_ref[:, lanes].astype(F4)
             )
-            ext[j, rim : rim + rows, :] = x_ref[:, lanes].astype(F4)
-            weights = w_ref[:, lanes]
-            bias = bias_ref[:, lanes]
-            for top in range(0, rows, BLOCK):
-                acc = bias
-                for tap in range(taps):
-                    at = base + top + tap
-                    acc = acc + weights[tap : tap + 1, :] * ext[j, at : at + BLOCK, :]
-                half = 0.5 * acc
-                out_ref[top : top + BLOCK, lanes] = (half + half * jnp.tanh(half)).astype(BF)
+            ext[j, rim:, :] = x_ref[0:BLOCK, lanes].astype(F4)
+            for top, out in conv_rows(ext, j, w_ref[:, lanes], bias_ref[:, lanes], (0,), base):
+                out_ref[0:BLOCK, lanes] = out
         at = chunk_at(i)
         part_ref[...] += lax.dot_general(
             out_ref[:, at], proj_ref[:, at], NT, preferred_element_type=F4
         )
 
 
-def conv_project(conv_in, rims, conv_weight, conv_bias, proj_weight_t):
-    rows, channels = conv_in.shape
+def conv_project(x, rims, w, bias, proj_weight_t, conv_out):
+    rows, channels = conv_out.shape
     wide = proj_weight_t.shape[0]
     rim = rims[0].shape[0]
     return pl.pallas_call(
         conv_kernel,
-        in_specs=in_vmem(6),
+        in_specs=in_vmem(7),
         out_specs=in_vmem(2),
         out_shape=[
             jax.ShapeDtypeStruct((rows, channels), BF),
             jax.ShapeDtypeStruct((rows, wide), F4),
         ],
-        scratch_shapes=[pltpu.VMEM((WIDTH // 128, rows + rim, 128), F4)],
+        scratch_shapes=[pltpu.VMEM((WIDTH // 128, BLOCK + rim, 128), F4)],
+        input_output_aliases={6: 0},
         compiler_params=params(),
         name="conv_project",
-    )(conv_in, *rims, conv_weight, conv_bias, proj_weight_t)
+    )(x, *rims, w, bias, proj_weight_t, conv_out)
 
 
 def in_hbm(a):
@@ -386,9 +425,8 @@
             hist[at, :] = now
             pairs = now * grad
             parts = [pairs[:, k : k + 128] for k in range(0, WIDTH, 128)]
-            while len(parts) > 1:
-                parts = [a + b for a, b in zip(parts[::2], parts[1::2])]
-            sums[n, tokens, :] += parts[0].astype(F4)
+            low = (parts[0] + parts[1]).astype(F4)
+            sums[n, tokens, :] += low + (parts[2] + parts[3]).astype(F4)
         mixed = jnp.dot(alt_ref[tokens, :], hist[...], preferred_element_type=F4)
         out_ref[tokens, :] = (mixed_ref[tokens, here] + mixed).astype(BF)
 
@@ -526,10 +564,13 @@
         grad_c = refs[0][...]
         for r in refs[1:many]:
             grad_c = grad_c + r[...]
-        grad_c = grad_c.astype(BF)
+        high = grad_c.astype(BF)
+        low = (grad_c - high.astype(F4)).astype(BF)
+        both = jnp.concatenate([high, low], axis=0)
         for j in range(count):
             block = conv_ref[:, j * share : (j + 1) * share]
-            out_ref[j] = jnp.dot(grad_c, block, preferred_element_type=F4).astype(BF)
+            out = jnp.dot(both, block, preferred_element_type=F4)
+            out_ref[j] = (out[:states, :] + out[states:, :]).astype(BF)
 
     return pl.pallas_call(
         body,
@@ -589,9 +630,11 @@
         lax.ppermute(edge, "seq", [p for i in range(k, count - 1, 2) for p in ((i, i + 1), (i + 1, i))])
         for k in range(2)
     ]
-    x, w, bias, weight_t = fetch(conv_in, conv_weight, conv_bias[None], proj_weight.T)
+    x, w, bias, weight_t, conv_out = conv_body(
+        conv_in, conv_weight, conv_bias[None], proj_weight.T
+    )
     rate = decay_rate * (-LOG2E)
-    conv_out, part = conv_project(x, rims, w, bias, weight_t)
+    conv_out, part = conv_project(x, rims, w, bias, weight_t, conv_out)
     mine = add_first(part, swap(part, "tp", 1), rank)
     other = swap(mine, "tp", 2)
     bit = 4

time: 75.5 us -> 75.1 us (level)
  transfers between devices with their start and end apart: 13 -> 13, of which waited for: 6 -> 6; matrix products, arithmetic and copies ran while one was open for 0% -> 0% of each run, Pallas kernels for 17% -> 18%
where the time goes in v4:
time: 75.1 us; the launch traced here: 74.9 us
  Pallas kernels  27.4 us (36%)
  starting transfers between devices  21.2 us (28%)
  waiting for transfers between devices  12.2 us (16%)
  blocking collectives  11.7 us (16%)
  local copies, waits for them, and re-layouts  0.9 us (1%)
  between operations  0.8 us (1%)
    ppermute x11, starting transfers between devices, swap(): return lax.ppermute(a, axis, [(i, i ^ bit) for i in range(count)])  17.6 us
    ppermute x11, waiting for transfers between devices, swap(): return lax.ppermute(a, axis, [(i, i ^ bit) for i in range(count)])  12.2 us
    pallas_call x2, Pallas kernels, local_scan(): pl.pallas_call(body, in_specs=in_vmem(len(ops)), out_specs=in_vmem(6), ou...  11.7 us
    all_to_all x1, blocking collectives, weight_gradient(): weight = lax.all_to_all(weight, 'seq', 0, 0)  11.7 us
    pallas_call x2, Pallas kernels, add_carry(): pl.pallas_call(body, grid=(width // WIDTH,), in_specs=specs, out_specs=[p...  8.41 us
    ppermute x2, starting transfers between devices, on_device(): lax.ppermute(edge, 'seq', [p for i in range(k, count - 1, 2) for p in ((i...  3.62 us
    pallas_call x1, Pallas kernels, conv_project(): pl.pallas_call(conv_kernel, in_specs=in_vmem(7), out_specs=in_vmem(2), ou...  2.95 us
    pallas_call x1, Pallas kernels, conv_body(): pl.pallas_call(conv_body_kernel, in_specs=[pl.BlockSpec(memory_space=pltp...  2.85 us
  transfers between devices with their start and end apart: 13, of which 6 were waited for; matrix products, arithmetic and copies ran while one was open for 0% of the time, Pallas kernels for 18%

profile of v4, /device:TPU:0, one launch (start us, length us, event | category | flops | bytes accessed | tf_op | source)
XLA Modules:
  0.0 74.9 jit_solution(8415972323173749924)
XLA Ops:
  0.6 0.8 %slice.3 = bf16[8,4096]{1,0:T(8,128)(2,1)S(1)} slice(bf16[128,4096]{1,0:T(8,128)(2,1)} %x_hbm.1), slice={[120:128], [0:4096]} | slice | bytes 131072 | tf_op jit(solution)/shard_map/slice | solution.py:628
  1.5 3.0 %collective-permute-start = (bf16[8,4096]{1,0:T(8,128)(2,1)S(1)}, bf16[8,4096]{1,0:T(8,128)(2,1)S(1)}, u32[]{:S(2)}, u32[]{:S(2)}) collective-permute-start(bf16[8,4096]{1,0:T(8,128)(2,1)S(1)} %slice.3), channel_id=1, source_target_pairs={{0,4},{4,0},{8,12},{12,8},{16,20},{20,16},{24,28},{28,24},{1,5},{5... | collective-permute-start | bytes 196616 | tf_op jit(solution)/shard_map/ppermute | solution.py:630
  4.4 0.7 collective-permute-start.1
  5.1 2.8 %conv_body.1 = (bf16[128,4096]{1,0:T(8,128)(2,1)S(1)}, f32[4,4096]{1,0:T(4,128)S(1)}, f32[1,4096]{1,0:T(1,128)S(1)}, bf16[544,4096]{1,0:T(8,128)(2,1)S(1)}, bf16[128,4096]{1,0:T(8,128)(2,1)S(1)}) custom-call(bf16[128,4096]{1,0:T(8,128)(2,1)} %x_hbm.1, f32[4,4096]{1,0:T(4,128)} %w_hbm.1, f32[1,4096]{1,0:T(1,128)} %bitcast.13, bf16[544,4096]{1,0:T(8,128)(2,1)} %bitcast.11), custom_call_target="tpu_custom_call" | custom-call | flops 10485760 | bytes 11173888 | tf_op jit(solution)/shard_map/conv_body/pallas_call | solution.py:91
  8.0 0.0 copy-start.4
  8.0 0.0 copy-start
  8.0 0.0 copy-start.1
  8.0 0.0 copy-start.2
  8.0 0.0 copy-start.3
  8.0 0.0 collective-permute-done.odd_ref
  8.0 0.0 collective-permute-done.1.even_ref
  8.0 3.0 %conv_project.1 = (bf16[128,4096]{1,0:T(8,128)(2,1)S(1)}, f32[128,544]{1,0:T(8,128)S(1)}) custom-call(bf16[128,4096]{1,0:T(8,128)(2,1)S(1)} %get-tuple-element.49.x_ref, bf16[8,4096]{1,0:T(8,128)(2,1)S(1)} %collective-permute-done.odd_ref, bf16[8,4096]{1,0:T(8,128)(2,1)S(1)} %collective-permute-done.1.even_ref, ...), custom_call_target="tpu_custom_call", output_to_operand_aliasing={{0}: (6, {})} | custom-call | tf_op jit(solution)/shard_map/conv_project/pallas_call | solution.py:139
  11.0 0.1 collective-permute-start.2
  11.1 1.6 %collective-permute-done.2.b_ref = f32[128,544]{1,0:T(8,128)S(1)} collective-permute-done((f32[128,544]{1,0:T(8,128)S(1)}, f32[128,544]{1,0:T(8,128)S(1)}, u32[]{:S(2)}, u32[]{:S(2)}) %collective-permute-start.2) | collective-permute-done | bytes 278560 | tf_op jit(solution)/shard_map/ppermute | solution.py:21
  12.7 0.1 add_first.1.mine_ref
  12.8 1.6 %collective-permute-start.3 = (bf16[128,576]{1,0:T(8,128)(2,1)S(1)}, bf16[128,576]{1,0:T(8,128)(2,1)S(1)}, u32[]{:S(2)}, u32[]{:S(2)}) collective-permute-start(bf16[128,576]{1,0:T(8,128)(2,1)S(1)} %add_first.1.mine_ref), channel_id=1, source_target_pairs={{0,2},{1,3},{2,0},{3,1},{4,6},{5,7},{6,4},{7,5},{8,10},{9,11},{10,... | collective-permute-start | bytes 442376 | tf_op jit(solution)/shard_map/ppermute | solution.py:21
  14.4 0.0 copy-done.4
  14.4 4.7 %collective-permute-done.3.other_ref = bf16[128,576]{1,0:T(8,128)(2,1)S(1)} collective-permute-done((bf16[128,576]{1,0:T(8,128)(2,1)S(1)}, bf16[128,576]{1,0:T(8,128)(2,1)S(1)}, u32[]{:S(2)}, u32[]{:S(2)}) %collective-permute-start.3) | collective-permute-done | bytes 147488 | tf_op jit(solution)/shard_map/ppermute | solution.py:21
  19.1 0.6 prepare.1
  19.8 5.9 %local_scan.2 = (f32[128,2048]{1,0:T(8,128)S(1)}, f32[128,2048]{1,0:T(8,128)S(1)}, f32[16,2048]{1,0:T(8,128)S(1)}, bf16[16,2304]{1,0:T(8,128)(2,1)S(1)}, f32[1,2048]{1,0:T(1,128)S(1)}, /*index=5*/f32[128,256]{1,0:T(8,128)S(1)}) custom-call(bf16[128,512]{1,0:T(8,128)(2,1)S(1)} %get-tuple-element.56.refs_0_, f32[2048,128]{1,0:T(8,128)S(1)} %get-tuple-element.57.refs_1_, ...), custom_call_target="tpu_custom_call" | custom-call | flops 2516582400 | bytes 4194304 | tf_op jit(solution)/shard_map/local_scan/pallas_call | solution.py:367
  25.7 4.3 %collective-permute-start.7 = (bf16[16,2304]{1,0:T(8,128)(2,1)S(1)}, bf16[16,2304]{1,0:T(8,128)(2,1)S(1)}, u32[]{:S(2)}, u32[]{:S(2)}) collective-permute-start(bf16[16,2304]{1,0:T(8,128)(2,1)S(1)} %get-tuple-element.78), channel_id=1, source_target_pairs={{0,4},{4,0},{8,12},{12,8},{16,20},{20,16},{24,28},{28,24},{1,5},{5... | collective-permute-start | bytes 221192 | tf_op jit(solution)/shard_map/ppermute | solution.py:21
  30.0 5.9 %local_scan.3 = (f32[128,2048]{1,0:T(8,128)S(1)}, f32[128,2048]{1,0:T(8,128)S(1)}, f32[16,2048]{1,0:T(8,128)S(1)}, bf16[16,2304]{1,0:T(8,128)(2,1)S(1)}, f32[1,2048]{1,0:T(1,128)S(1)}, /*index=5*/f32[128,256]{1,0:T(8,128)S(1)}) custom-call(bf16[128,512]{1,0:T(8,128)(2,1)S(1)} %get-tuple-element.56.refs_0_, f32[2048,128]{1,0:T(8,128)S(1)} %get-tuple-element.57.refs_1_, ...), custom_call_target="tpu_custom_call" | custom-call | flops 2516582400 | bytes 4194304 | tf_op jit(solution)/shard_map/local_scan/pallas_call | solution.py:367
  35.8 0.0 collective-permute-start.4
  35.9 0.0 collective-permute-done.7.refs_3_
  35.9 0.1 merge.9
  36.0 2.8 %collective-permute-start.8 = (bf16[16,2304]{1,0:T(8,128)(2,1)S(1)}, bf16[16,2304]{1,0:T(8,128)(2,1)S(1)}, u32[]{:S(2)}, u32[]{:S(2)}) collective-permute-start(bf16[16,2304]{1,0:T(8,128)(2,1)S(1)} %get-tuple-element.81), channel_id=1, source_target_pairs={{0,8},{4,12},{8,0},{12,4},{16,24},{20,28},{24,16},{28,20},{1,9},{5... | collective-permute-start | bytes 221192 | tf_op jit(solution)/shard_map/ppermute | solution.py:21
  38.8 1.4 %collective-permute-done.4.refs_3_ = bf16[16,2304]{1,0:T(8,128)(2,1)S(1)} collective-permute-done((bf16[16,2304]{1,0:T(8,128)(2,1)S(1)}, bf16[16,2304]{1,0:T(8,128)(2,1)S(1)}, u32[]{:S(2)}, u32[]{:S(2)}) %collective-permute-start.4) | collective-permute-done | bytes 73760 | tf_op jit(solution)/shard_map/ppermute | solution.py:21
  40.2 0.1 merge.6
  40.3 1.6 %collective-permute-start.5 = (bf16[16,2304]{1,0:T(8,128)(2,1)S(1)}, bf16[16,2304]{1,0:T(8,128)(2,1)S(1)}, u32[]{:S(2)}, u32[]{:S(2)}) collective-permute-start(bf16[16,2304]{1,0:T(8,128)(2,1)S(1)} %get-tuple-element.66), channel_id=1, source_target_pairs={{0,8},{4,12},{8,0},{12,4},{16,24},{20,28},{24,16},{28,20},{1,9},{5... | collective-permute-start | bytes 221192 | tf_op jit(solution)/shard_map/ppermute | solution.py:21
  41.9 0.0 collective-permute-done.8.refs_3_
  41.9 0.1 merge.10
  42.0 3.1 %collective-permute-start.9 = (bf16[16,2304]{1,0:T(8,128)(2,1)S(1)}, bf16[16,2304]{1,0:T(8,128)(2,1)S(1)}, u32[]{:S(2)}, u32[]{:S(2)}) collective-permute-start(bf16[16,2304]{1,0:T(8,128)(2,1)S(1)} %get-tuple-element.86), channel_id=1, source_target_pairs={{0,16},{4,20},{8,24},{12,28},{16,0},{20,4},{24,8},{28,12},{1,17},{... | collective-permute-start | bytes 221192 | tf_op jit(solution)/shard_map/ppermute | solution.py:21
  45.1 0.0 collective-permute-done.5.refs_3_
  45.1 0.1 merge.7
  45.2 2.3 %collective-permute-start.6 = (bf16[16,2304]{1,0:T(8,128)(2,1)S(1)}, bf16[16,2304]{1,0:T(8,128)(2,1)S(1)}, u32[]{:S(2)}, u32[]{:S(2)}) collective-permute-start(bf16[16,2304]{1,0:T(8,128)(2,1)S(1)} %get-tuple-element.71), channel_id=1, source_target_pairs={{0,16},{4,20},{8,24},{12,28},{16,0},{20,4},{24,8},{28,12},{1,17},{... | collective-permute-start | bytes 221192 | tf_op jit(solution)/shard_map/ppermute | solution.py:21
  47.4 1.8 %collective-permute-done.9.refs_3_ = bf16[16,2304]{1,0:T(8,128)(2,1)S(1)} collective-permute-done((bf16[16,2304]{1,0:T(8,128)(2,1)S(1)}, bf16[16,2304]{1,0:T(8,128)(2,1)S(1)}, u32[]{:S(2)}, u32[]{:S(2)}) %collective-permute-start.9) | collective-permute-done | bytes 73760 | tf_op jit(solution)/shard_map/ppermute | solution.py:21
  49.3 4.1 %add_carry.2 = (bf16[128,4096]{1,0:T(8,128)(2,1)}, f32[16,128]{1,0:T(8,128)S(1)}) custom-call(bf16[128,256]{1,0:T(8,128)(2,1)S(1)} %get-tuple-element.55.refs_0_, f32[16,4096]{1,0:T(8,128)S(1)} %broadcast_multiply_fusion.refs_5_.refs_0_.refs_1_, f32[16,2048]{1,0:T(8,128)S(1)} %merge.11.refs_2_, f32[128,2048]{1,0:T(8,128)S(1)} %get-tuple-element.89.refs_3_, ...), custom_call_target="tpu_custom_call" | custom-call | flops 1258291200 | bytes 4194304 | tf_op jit(solution)/shard_map/add_carry/pallas_call | solution.py:475
  53.4 0.0 collective-permute-done.6.refs_3_
  53.4 4.3 %add_carry.3 = (bf16[128,4096]{1,0:T(8,128)(2,1)}, f32[16,128]{1,0:T(8,128)S(1)}) custom-call(bf16[128,256]{1,0:T(8,128)(2,1)S(1)} %get-tuple-element.55.refs_0_, f32[16,4096]{1,0:T(8,128)S(1)} %broadcast_multiply_fusion.refs_5_.refs_0_.refs_1_, f32[16,2048]{1,0:T(8,128)S(1)} %merge.8.refs_2_, ...), custom_call_target="tpu_custom_call", output_to_operand_aliasing={{0}: (8, {})} | custom-call | flops 1258291200 | bytes 4194304 | tf_op jit(solution)/shard_map/add_carry/pallas_call | solution.py:475
  57.7 0.0 collective-permute-start.10
  57.7 1.5 %collective-permute-start.11 = (f32[16,128]{1,0:T(8,128)S(1)}, f32[16,128]{1,0:T(8,128)S(1)}, u32[]{:S(2)}, u32[]{:S(2)}) collective-permute-start(f32[16,128]{1,0:T(8,128)S(1)} %get-tuple-element.95.refs_0_), channel_id=1, source_target_pairs={{0,2},{1,3},{2,0},{3,1},{4,6},{5,7},{6,4},{7,5},{8,10},{9,11},{10,... | collective-permute-start | bytes 24584 | tf_op jit(solution)/shard_map/ppermute | solution.py:21
  59.2 0.4 collective-permute-start.12
  59.6 0.0 collective-permute-done.10.refs_1_
  59.6 1.8 %collective-permute-done.11.refs_2_ = f32[16,128]{1,0:T(8,128)S(1)} collective-permute-done((f32[16,128]{1,0:T(8,128)S(1)}, f32[16,128]{1,0:T(8,128)S(1)}, u32[]{:S(2)}, u32[]{:S(2)}) %collective-permute-start.11) | collective-permute-done | bytes 8224 | tf_op jit(solution)/shard_map/ppermute | solution.py:21
  61.4 0.9 %collective-permute-done.12.refs_3_ = f32[16,128]{1,0:T(8,128)S(1)} collective-permute-done((f32[16,128]{1,0:T(8,128)S(1)}, f32[16,128]{1,0:T(8,128)S(1)}, u32[]{:S(2)}, u32[]{:S(2)}) %collective-permute-start.12) | collective-permute-done | bytes 8224 | tf_op jit(solution)/shard_map/ppermute | solution.py:21
  62.3 0.3 weight_first.1
  62.6 11.7 %all_to_all.5 = bf16[8,16,512]{2,1,0:T(8,128)(2,1)S(1)} all-to-all(bf16[8,16,512]{2,1,0:T(8,128)(2,1)S(1)} %weight_first.1), channel_id=1, replica_groups=mesh['seq'=8,'tp'=4] {'seq'}, dimensions={0} | all-to-all | bytes 262144 | tf_op jit(solution)/shard_map/all_to_all | solution.py:595
  74.3 0.6 convert_reduce_fusion
  (9 shorter events, 0.1 us)
Async XLA Ops:
  1.5 6.5 %collective-permute-start = (bf16[8,4096]{1,0:T(8,128)(2,1)S(1)}, bf16[8,4096]{1,0:T(8,128)(2,1)S(1)}, u32[]{:S(2)}, u32[]{:S(2)}) collective-permute-start(bf16[8,4096]{1,0:T(8,128)(2,1)S(1)} %slice.3), channel_id=1, source_target_pairs={{0,4},{4,0},{8,12},{12,8},{16,20},{20,16},{24,28},{28,24},{1,5},{5... | collective-permute-start | bytes 196616 | tf_op jit(solution)/shard_map/ppermute | solution.py:630
  4.4 3.6 %collective-permute-start.1 = (bf16[8,4096]{1,0:T(8,128)(2,1)S(1)}, bf16[8,4096]{1,0:T(8,128)(2,1)S(1)}, u32[]{:S(2)}, u32[]{:S(2)}) collective-permute-start(bf16[8,4096]{1,0:T(8,128)(2,1)S(1)} %slice.3), channel_id=1, source_target_pairs={{4,8},{8,4},{12,16},{16,12},{20,24},{24,20},{5,9},{9,5},{13,17},{1... | collective-permute-start | bytes 196616 | tf_op jit(solution)/shard_map/ppermute | solution.py:630
  8.0 6.4 %copy-start.4 = (f32[16,4096]{1,0:T(8,128)S(1)}, f32[16,4096]{1,0:T(8,128)}, u32[]{:S(2)}) copy-start(f32[16,4096]{1,0:T(8,128)} %param.15) | copy-start | bytes 786436
  8.0 11.8 %copy-start = (bf16[512,4096]{1,0:T(8,128)(2,1)S(1)}, bf16[512,4096]{1,0:T(8,128)(2,1)}, u32[]{:S(2)}) copy-start(bf16[512,4096]{1,0:T(8,128)(2,1)} %refs_3_.3) | copy-start | bytes 12582916
  8.0 11.8 %copy-start.1 = (bf16[128,4096]{1,0:T(8,128)(2,1)S(1)}, bf16[128,4096]{1,0:T(8,128)(2,1)}, u32[]{:S(2)}) copy-start(bf16[128,4096]{1,0:T(8,128)(2,1)} %refs_5_.3) | copy-start | bytes 3145732
  8.0 11.8 %copy-start.2 = (f32[4096]{0:T(1024)S(1)}, f32[4096]{0:T(1024)}, u32[]{:S(2)}) copy-start(f32[4096]{0:T(1024)} %param.14) | copy-start | bytes 49156
  8.0 11.8 %copy-start.3 = (f32[4096]{0:T(1024)S(1)}, f32[4096]{0:T(1024)}, u32[]{:S(2)}) copy-start(f32[4096]{0:T(1024)} %param.16) | copy-start | bytes 49156
  11.0 1.7 %collective-permute-start.2 = (f32[128,544]{1,0:T(8,128)S(1)}, f32[128,544]{1,0:T(8,128)S(1)}, u32[]{:S(2)}, u32[]{:S(2)}) collective-permute-start(f32[128,544]{1,0:T(8,128)S(1)} %get-tuple-element.54.a_ref), channel_id=1, source_target_pairs={{0,1},{1,0},{2,3},{3,2},{4,5},{5,4},{6,7},{7,6},{8,9},{9,8},{10,11... | collective-permute-start | bytes 835592 | tf_op jit(solution)/shard_map/ppermute | solution.py:21
  12.8 6.3 %collective-permute-start.3 = (bf16[128,576]{1,0:T(8,128)(2,1)S(1)}, bf16[128,576]{1,0:T(8,128)(2,1)S(1)}, u32[]{:S(2)}, u32[]{:S(2)}) collective-permute-start(bf16[128,576]{1,0:T(8,128)(2,1)S(1)} %add_first.1.mine_ref), channel_id=1, source_target_pairs={{0,2},{1,3},{2,0},{3,1},{4,6},{5,7},{6,4},{7,5},{8,10},{9,11},{10,... | collective-permute-start | bytes 442376 | tf_op jit(solution)/shard_map/ppermute | solution.py:21
  25.7 10.2 %collective-permute-start.7 = (bf16[16,2304]{1,0:T(8,128)(2,1)S(1)}, bf16[16,2304]{1,0:T(8,128)(2,1)S(1)}, u32[]{:S(2)}, u32[]{:S(2)}) collective-permute-start(bf16[16,2304]{1,0:T(8,128)(2,1)S(1)} %get-tuple-element.78), channel_id=1, source_target_pairs={{0,4},{4,0},{8,12},{12,8},{16,20},{20,16},{24,28},{28,24},{1,5},{5... | collective-permute-start | bytes 221192 | tf_op jit(solution)/shard_map/ppermute | solution.py:21
  35.8 4.4 %collective-permute-start.4 = (bf16[16,2304]{1,0:T(8,128)(2,1)S(1)}, bf16[16,2304]{1,0:T(8,128)(2,1)S(1)}, u32[]{:S(2)}, u32[]{:S(2)}) collective-permute-start(bf16[16,2304]{1,0:T(8,128)(2,1)S(1)} %get-tuple-element.63), channel_id=1, source_target_pairs={{0,4},{4,0},{8,12},{12,8},{16,20},{20,16},{24,28},{28,24},{1,5},{5... | collective-permute-start | bytes 221192 | tf_op jit(solution)/shard_map/ppermute | solution.py:21
  36.0 5.9 %collective-permute-start.8 = (bf16[16,2304]{1,0:T(8,128)(2,1)S(1)}, bf16[16,2304]{1,0:T(8,128)(2,1)S(1)}, u32[]{:S(2)}, u32[]{:S(2)}) collective-permute-start(bf16[16,2304]{1,0:T(8,128)(2,1)S(1)} %get-tuple-element.81), channel_id=1, source_target_pairs={{0,8},{4,12},{8,0},{12,4},{16,24},{20,28},{24,16},{28,20},{1,9},{5... | collective-permute-start | bytes 221192 | tf_op jit(solution)/shard_map/ppermute | solution.py:21
  40.3 4.8 %collective-permute-start.5 = (bf16[16,2304]{1,0:T(8,128)(2,1)S(1)}, bf16[16,2304]{1,0:T(8,128)(2,1)S(1)}, u32[]{:S(2)}, u32[]{:S(2)}) collective-permute-start(bf16[16,2304]{1,0:T(8,128)(2,1)S(1)} %get-tuple-element.66), channel_id=1, source_target_pairs={{0,8},{4,12},{8,0},{12,4},{16,24},{20,28},{24,16},{28,20},{1,9},{5... | collective-permute-start | bytes 221192 | tf_op jit(solution)/shard_map/ppermute | solution.py:21
  42.0 7.2 %collective-permute-start.9 = (bf16[16,2304]{1,0:T(8,128)(2,1)S(1)}, bf16[16,2304]{1,0:T(8,128)(2,1)S(1)}, u32[]{:S(2)}, u32[]{:S(2)}) collective-permute-start(bf16[16,2304]{1,0:T(8,128)(2,1)S(1)} %get-tuple-element.86), channel_id=1, source_target_pairs={{0,16},{4,20},{8,24},{12,28},{16,0},{20,4},{24,8},{28,12},{1,17},{... | collective-permute-start | bytes 221192 | tf_op jit(solution)/shard_map/ppermute | solution.py:21
  45.2 8.2 %collective-permute-start.6 = (bf16[16,2304]{1,0:T(8,128)(2,1)S(1)}, bf16[16,2304]{1,0:T(8,128)(2,1)S(1)}, u32[]{:S(2)}, u32[]{:S(2)}) collective-permute-start(bf16[16,2304]{1,0:T(8,128)(2,1)S(1)} %get-tuple-element.71), channel_id=1, source_target_pairs={{0,16},{4,20},{8,24},{12,28},{16,0},{20,4},{24,8},{28,12},{1,17},{... | collective-permute-start | bytes 221192 | tf_op jit(solution)/shard_map/ppermute | solution.py:21
  57.7 1.9 %collective-permute-start.10 = (f32[16,128]{1,0:T(8,128)S(1)}, f32[16,128]{1,0:T(8,128)S(1)}, u32[]{:S(2)}, u32[]{:S(2)}) collective-permute-start(f32[16,128]{1,0:T(8,128)S(1)} %get-tuple-element.95.refs_0_), channel_id=1, source_target_pairs={{0,1},{1,0},{2,3},{3,2},{4,5},{5,4},{6,7},{7,6},{8,9},{9,8},{10,11... | collective-permute-start | bytes 24584 | tf_op jit(solution)/shard_map/ppermute | solution.py:21
  57.7 3.7 %collective-permute-start.11 = (f32[16,128]{1,0:T(8,128)S(1)}, f32[16,128]{1,0:T(8,128)S(1)}, u32[]{:S(2)}, u32[]{:S(2)}) collective-permute-start(f32[16,128]{1,0:T(8,128)S(1)} %get-tuple-element.95.refs_0_), channel_id=1, source_target_pairs={{0,2},{1,3},{2,0},{3,1},{4,6},{5,7},{6,4},{7,5},{8,10},{9,11},{10,... | collective-permute-start | bytes 24584 | tf_op jit(solution)/shard_map/ppermute | solution.py:21
  59.2 3.1 %collective-permute-start.12 = (f32[16,128]{1,0:T(8,128)S(1)}, f32[16,128]{1,0:T(8,128)S(1)}, u32[]{:S(2)}, u32[]{:S(2)}) collective-permute-start(f32[16,128]{1,0:T(8,128)S(1)} %get-tuple-element.95.refs_0_), channel_id=1, source_target_pairs={{0,3},{1,2},{2,1},{3,0},{4,7},{5,6},{6,5},{7,4},{8,11},{9,10},{10,... | collective-permute-start | bytes 24584 | tf_op jit(solution)/shard_map/ppermute | solution.py:21

commit v5 on v4

--- a/solution.py
+++ b/solution.py
@@ -114,7 +114,6 @@
     rim = odd_ref.shape[0]
     base = rim - (w_ref.shape[0] - 1)
     odd = (lax.axis_index("seq") & 1) != 0
-    part_ref[...] = jnp.zeros_like(part_ref)
 
     @pl.loop(0, channels // WIDTH)
     def _(i):
@@ -126,10 +125,10 @@
             ext[j, rim:, :] = x_ref[0:BLOCK, lanes].astype(F4)
             for top, out in conv_rows(ext, j, w_ref[:, lanes], bias_ref[:, lanes], (0,), base):
                 out_ref[0:BLOCK, lanes] = out
-        at = chunk_at(i)
-        part_ref[...] += lax.dot_general(
-            out_ref[:, at], proj_ref[:, at], NT, preferred_element_type=F4
-        )
+
+    part_ref[...] = lax.dot_general(
+        out_ref[...], proj_ref[...], NT, preferred_element_type=F4
+    )
 
 
 def conv_project(x, rims, w, bias, proj_weight_t, conv_out):

time: 75.1 us -> 74.2 us (0.988)
  Pallas kernels: 27.4 us -> 26.5 us
    pallas_call x1, Pallas kernels: 2.95 us -> 2.04 us  [conv_project(): pl.pallas_call(conv_kernel, in_specs=in_vmem(7), out_specs=in_vmem(2), ou...]
where the time goes in v5:
time: 74.2 us; the launch traced here: 74 us
  Pallas kernels  26.5 us (36%)
  starting transfers between devices  21.2 us (29%)
  waiting for transfers between devices  12.2 us (16%)
  blocking collectives  11.7 us (16%)
  local copies, waits for them, and re-layouts  0.9 us (1%)
  between operations  0.8 us (1%)
    ppermute x11, starting transfers between devices, swap(): return lax.ppermute(a, axis, [(i, i ^ bit) for i in range(count)])  17.6 us
    ppermute x11, waiting for transfers between devices, swap(): return lax.ppermute(a, axis, [(i, i ^ bit) for i in range(count)])  12.2 us
    pallas_call x2, Pallas kernels, local_scan(): pl.pallas_call(body, in_specs=in_vmem(len(ops)), out_specs=in_vmem(6), ou...  11.7 us
    all_to_all x1, blocking collectives, weight_gradient(): weight = lax.all_to_all(weight, 'seq', 0, 0)  11.7 us
    pallas_call x2, Pallas kernels, add_carry(): pl.pallas_call(body, grid=(width // WIDTH,), in_specs=specs, out_specs=[p...  8.41 us
    ppermute x2, starting transfers between devices, on_device(): lax.ppermute(edge, 'seq', [p for i in range(k, count - 1, 2) for p in ((i...  3.62 us
    pallas_call x1, Pallas kernels, conv_body(): pl.pallas_call(conv_body_kernel, in_specs=[pl.BlockSpec(memory_space=pltp...  2.85 us
    pallas_call x1, Pallas kernels, conv_project(): pl.pallas_call(conv_kernel, in_specs=in_vmem(7), out_specs=in_vmem(2), ou...  2.04 us
  transfers between devices with their start and end apart: 13, of which 6 were waited for; matrix products, arithmetic and copies ran while one was open for 0% of the time, Pallas kernels for 18%

profile of v5, /device:TPU:0, one launch (start us, length us, event | category | flops | bytes accessed | tf_op | source)
XLA Modules:
  0.0 74.0 jit_solution(5431852175286628388)
XLA Ops:
  0.6 0.8 %slice.3 = bf16[8,4096]{1,0:T(8,128)(2,1)S(1)} slice(bf16[128,4096]{1,0:T(8,128)(2,1)} %x_hbm.1), slice={[120:128], [0:4096]} | slice | bytes 131072 | tf_op jit(solution)/shard_map/slice | solution.py:627
  1.5 3.0 %collective-permute-start = (bf16[8,4096]{1,0:T(8,128)(2,1)S(1)}, bf16[8,4096]{1,0:T(8,128)(2,1)S(1)}, u32[]{:S(2)}, u32[]{:S(2)}) collective-permute-start(bf16[8,4096]{1,0:T(8,128)(2,1)S(1)} %slice.3), channel_id=1, source_target_pairs={{0,4},{4,0},{8,12},{12,8},{16,20},{20,16},{24,28},{28,24},{1,5},{5... | collective-permute-start | bytes 196616 | tf_op jit(solution)/shard_map/ppermute | solution.py:629
  4.4 0.7 collective-permute-start.1
  5.1 2.8 %conv_body.1 = (bf16[128,4096]{1,0:T(8,128)(2,1)S(1)}, f32[4,4096]{1,0:T(4,128)S(1)}, f32[1,4096]{1,0:T(1,128)S(1)}, bf16[544,4096]{1,0:T(8,128)(2,1)S(1)}, bf16[128,4096]{1,0:T(8,128)(2,1)S(1)}) custom-call(bf16[128,4096]{1,0:T(8,128)(2,1)} %x_hbm.1, f32[4,4096]{1,0:T(4,128)} %w_hbm.1, f32[1,4096]{1,0:T(1,128)} %bitcast.13, bf16[544,4096]{1,0:T(8,128)(2,1)} %bitcast.11), custom_call_target="tpu_custom_call" | custom-call | flops 10485760 | bytes 11173888 | tf_op jit(solution)/shard_map/conv_body/pallas_call | solution.py:91
  8.0 0.0 copy-start.4
  8.0 0.0 copy-start
  8.0 0.0 copy-start.1
  8.0 0.0 copy-start.2
  8.0 0.0 copy-start.3
  8.0 0.0 collective-permute-done.odd_ref
  8.0 0.0 collective-permute-done.1.even_ref
  8.0 2.0 %conv_project.1 = (bf16[128,4096]{1,0:T(8,128)(2,1)S(1)}, f32[128,544]{1,0:T(8,128)S(1)}) custom-call(bf16[128,4096]{1,0:T(8,128)(2,1)S(1)} %get-tuple-element.49.x_ref, bf16[8,4096]{1,0:T(8,128)(2,1)S(1)} %collective-permute-done.odd_ref, bf16[8,4096]{1,0:T(8,128)(2,1)S(1)} %collective-permute-done.1.even_ref, ...), custom_call_target="tpu_custom_call", output_to_operand_aliasing={{0}: (6, {})} | custom-call | tf_op jit(solution)/shard_map/conv_project/pallas_call | solution.py:138
  10.1 0.1 collective-permute-start.2
  10.2 1.6 %collective-permute-done.2.b_ref = f32[128,544]{1,0:T(8,128)S(1)} collective-permute-done((f32[128,544]{1,0:T(8,128)S(1)}, f32[128,544]{1,0:T(8,128)S(1)}, u32[]{:S(2)}, u32[]{:S(2)}) %collective-permute-start.2) | collective-permute-done | bytes 278560 | tf_op jit(solution)/shard_map/ppermute | solution.py:21
  11.8 0.1 add_first.1.mine_ref
  11.9 1.6 %collective-permute-start.3 = (bf16[128,576]{1,0:T(8,128)(2,1)S(1)}, bf16[128,576]{1,0:T(8,128)(2,1)S(1)}, u32[]{:S(2)}, u32[]{:S(2)}) collective-permute-start(bf16[128,576]{1,0:T(8,128)(2,1)S(1)} %add_first.1.mine_ref), channel_id=1, source_target_pairs={{0,2},{1,3},{2,0},{3,1},{4,6},{5,7},{6,4},{7,5},{8,10},{9,11},{10,... | collective-permute-start | bytes 442376 | tf_op jit(solution)/shard_map/ppermute | solution.py:21
  13.5 4.7 %collective-permute-done.3.other_ref = bf16[128,576]{1,0:T(8,128)(2,1)S(1)} collective-permute-done((bf16[128,576]{1,0:T(8,128)(2,1)S(1)}, bf16[128,576]{1,0:T(8,128)(2,1)S(1)}, u32[]{:S(2)}, u32[]{:S(2)}) %collective-permute-start.3) | collective-permute-done | bytes 147488 | tf_op jit(solution)/shard_map/ppermute | solution.py:21
  18.2 0.6 prepare.1
  18.9 0.0 copy-done
  18.9 5.9 %local_scan.2 = (f32[128,2048]{1,0:T(8,128)S(1)}, f32[128,2048]{1,0:T(8,128)S(1)}, f32[16,2048]{1,0:T(8,128)S(1)}, bf16[16,2304]{1,0:T(8,128)(2,1)S(1)}, f32[1,2048]{1,0:T(1,128)S(1)}, /*index=5*/f32[128,256]{1,0:T(8,128)S(1)}) custom-call(bf16[128,512]{1,0:T(8,128)(2,1)S(1)} %get-tuple-element.56.refs_0_, f32[2048,128]{1,0:T(8,128)S(1)} %get-tuple-element.57.refs_1_, ...), custom_call_target="tpu_custom_call" | custom-call | flops 2516582400 | bytes 4194304 | tf_op jit(solution)/shard_map/local_scan/pallas_call | solution.py:366
  24.8 4.3 %collective-permute-start.7 = (bf16[16,2304]{1,0:T(8,128)(2,1)S(1)}, bf16[16,2304]{1,0:T(8,128)(2,1)S(1)}, u32[]{:S(2)}, u32[]{:S(2)}) collective-permute-start(bf16[16,2304]{1,0:T(8,128)(2,1)S(1)} %get-tuple-element.78), channel_id=1, source_target_pairs={{0,4},{4,0},{8,12},{12,8},{16,20},{20,16},{24,28},{28,24},{1,5},{5... | collective-permute-start | bytes 221192 | tf_op jit(solution)/shard_map/ppermute | solution.py:21
  29.1 5.9 %local_scan.3 = (f32[128,2048]{1,0:T(8,128)S(1)}, f32[128,2048]{1,0:T(8,128)S(1)}, f32[16,2048]{1,0:T(8,128)S(1)}, bf16[16,2304]{1,0:T(8,128)(2,1)S(1)}, f32[1,2048]{1,0:T(1,128)S(1)}, /*index=5*/f32[128,256]{1,0:T(8,128)S(1)}) custom-call(bf16[128,512]{1,0:T(8,128)(2,1)S(1)} %get-tuple-element.56.refs_0_, f32[2048,128]{1,0:T(8,128)S(1)} %get-tuple-element.57.refs_1_, ...), custom_call_target="tpu_custom_call" | custom-call | flops 2516582400 | bytes 4194304 | tf_op jit(solution)/shard_map/local_scan/pallas_call | solution.py:366
  34.9 0.0 collective-permute-start.4
  34.9 0.0 collective-permute-done.7.refs_3_
  35.0 0.1 merge.9
  35.1 2.8 %collective-permute-start.8 = (bf16[16,2304]{1,0:T(8,128)(2,1)S(1)}, bf16[16,2304]{1,0:T(8,128)(2,1)S(1)}, u32[]{:S(2)}, u32[]{:S(2)}) collective-permute-start(bf16[16,2304]{1,0:T(8,128)(2,1)S(1)} %get-tuple-element.81), channel_id=1, source_target_pairs={{0,8},{4,12},{8,0},{12,4},{16,24},{20,28},{24,16},{28,20},{1,9},{5... | collective-permute-start | bytes 221192 | tf_op jit(solution)/shard_map/ppermute | solution.py:21
  37.9 1.4 %collective-permute-done.4.refs_3_ = bf16[16,2304]{1,0:T(8,128)(2,1)S(1)} collective-permute-done((bf16[16,2304]{1,0:T(8,128)(2,1)S(1)}, bf16[16,2304]{1,0:T(8,128)(2,1)S(1)}, u32[]{:S(2)}, u32[]{:S(2)}) %collective-permute-start.4) | collective-permute-done | bytes 73760 | tf_op jit(solution)/shard_map/ppermute | solution.py:21
  39.3 0.1 merge.6
  39.4 1.6 %collective-permute-start.5 = (bf16[16,2304]{1,0:T(8,128)(2,1)S(1)}, bf16[16,2304]{1,0:T(8,128)(2,1)S(1)}, u32[]{:S(2)}, u32[]{:S(2)}) collective-permute-start(bf16[16,2304]{1,0:T(8,128)(2,1)S(1)} %get-tuple-element.66), channel_id=1, source_target_pairs={{0,8},{4,12},{8,0},{12,4},{16,24},{20,28},{24,16},{28,20},{1,9},{5... | collective-permute-start | bytes 221192 | tf_op jit(solution)/shard_map/ppermute | solution.py:21
  41.0 0.0 collective-permute-done.8.refs_3_
  41.0 0.1 merge.10
  41.1 3.1 %collective-permute-start.9 = (bf16[16,2304]{1,0:T(8,128)(2,1)S(1)}, bf16[16,2304]{1,0:T(8,128)(2,1)S(1)}, u32[]{:S(2)}, u32[]{:S(2)}) collective-permute-start(bf16[16,2304]{1,0:T(8,128)(2,1)S(1)} %get-tuple-element.86), channel_id=1, source_target_pairs={{0,16},{4,20},{8,24},{12,28},{16,0},{20,4},{24,8},{28,12},{1,17},{... | collective-permute-start | bytes 221192 | tf_op jit(solution)/shard_map/ppermute | solution.py:21
  44.2 0.0 collective-permute-done.5.refs_3_
  44.2 0.1 merge.7
  44.3 2.2 %collective-permute-start.6 = (bf16[16,2304]{1,0:T(8,128)(2,1)S(1)}, bf16[16,2304]{1,0:T(8,128)(2,1)S(1)}, u32[]{:S(2)}, u32[]{:S(2)}) collective-permute-start(bf16[16,2304]{1,0:T(8,128)(2,1)S(1)} %get-tuple-element.71), channel_id=1, source_target_pairs={{0,16},{4,20},{8,24},{12,28},{16,0},{20,4},{24,8},{28,12},{1,17},{... | collective-permute-start | bytes 221192 | tf_op jit(solution)/shard_map/ppermute | solution.py:21
  46.5 1.8 %collective-permute-done.9.refs_3_ = bf16[16,2304]{1,0:T(8,128)(2,1)S(1)} collective-permute-done((bf16[16,2304]{1,0:T(8,128)(2,1)S(1)}, bf16[16,2304]{1,0:T(8,128)(2,1)S(1)}, u32[]{:S(2)}, u32[]{:S(2)}) %collective-permute-start.9) | collective-permute-done | bytes 73760 | tf_op jit(solution)/shard_map/ppermute | solution.py:21
  48.4 4.1 %add_carry.2 = (bf16[128,4096]{1,0:T(8,128)(2,1)}, f32[16,128]{1,0:T(8,128)S(1)}) custom-call(bf16[128,256]{1,0:T(8,128)(2,1)S(1)} %get-tuple-element.55.refs_0_, f32[16,4096]{1,0:T(8,128)S(1)} %broadcast_multiply_fusion.refs_5_.refs_0_.refs_1_, f32[16,2048]{1,0:T(8,128)S(1)} %merge.11.refs_2_, f32[128,2048]{1,0:T(8,128)S(1)} %get-tuple-element.89.refs_3_, ...), custom_call_target="tpu_custom_call" | custom-call | flops 1258291200 | bytes 4194304 | tf_op jit(solution)/shard_map/add_carry/pallas_call | solution.py:474
  52.5 0.0 collective-permute-done.6.refs_3_
  52.5 4.3 %add_carry.3 = (bf16[128,4096]{1,0:T(8,128)(2,1)}, f32[16,128]{1,0:T(8,128)S(1)}) custom-call(bf16[128,256]{1,0:T(8,128)(2,1)S(1)} %get-tuple-element.55.refs_0_, f32[16,4096]{1,0:T(8,128)S(1)} %broadcast_multiply_fusion.refs_5_.refs_0_.refs_1_, f32[16,2048]{1,0:T(8,128)S(1)} %merge.8.refs_2_, ...), custom_call_target="tpu_custom_call", output_to_operand_aliasing={{0}: (8, {})} | custom-call | flops 1258291200 | bytes 4194304 | tf_op jit(solution)/shard_map/add_carry/pallas_call | solution.py:474
  56.8 0.0 collective-permute-start.10
  56.8 1.5 %collective-permute-start.11 = (f32[16,128]{1,0:T(8,128)S(1)}, f32[16,128]{1,0:T(8,128)S(1)}, u32[]{:S(2)}, u32[]{:S(2)}) collective-permute-start(f32[16,128]{1,0:T(8,128)S(1)} %get-tuple-element.95.refs_0_), channel_id=1, source_target_pairs={{0,2},{1,3},{2,0},{3,1},{4,6},{5,7},{6,4},{7,5},{8,10},{9,11},{10,... | collective-permute-start | bytes 24584 | tf_op jit(solution)/shard_map/ppermute | solution.py:21
  58.3 0.4 collective-permute-start.12
  58.7 0.0 collective-permute-done.10.refs_1_
  58.7 1.8 %collective-permute-done.11.refs_2_ = f32[16,128]{1,0:T(8,128)S(1)} collective-permute-done((f32[16,128]{1,0:T(8,128)S(1)}, f32[16,128]{1,0:T(8,128)S(1)}, u32[]{:S(2)}, u32[]{:S(2)}) %collective-permute-start.11) | collective-permute-done | bytes 8224 | tf_op jit(solution)/shard_map/ppermute | solution.py:21
  60.5 0.9 %collective-permute-done.12.refs_3_ = f32[16,128]{1,0:T(8,128)S(1)} collective-permute-done((f32[16,128]{1,0:T(8,128)S(1)}, f32[16,128]{1,0:T(8,128)S(1)}, u32[]{:S(2)}, u32[]{:S(2)}) %collective-permute-start.12) | collective-permute-done | bytes 8224 | tf_op jit(solution)/shard_map/ppermute | solution.py:21
  61.4 0.3 weight_first.1
  61.7 11.7 %all_to_all.5 = bf16[8,16,512]{2,1,0:T(8,128)(2,1)S(1)} all-to-all(bf16[8,16,512]{2,1,0:T(8,128)(2,1)S(1)} %weight_first.1), channel_id=1, replica_groups=mesh['seq'=8,'tp'=4] {'seq'}, dimensions={0} | all-to-all | bytes 262144 | tf_op jit(solution)/shard_map/all_to_all | solution.py:594
  73.3 0.6 convert_reduce_fusion
  (9 shorter events, 0.1 us)
Async XLA Ops:
  1.5 6.5 %collective-permute-start = (bf16[8,4096]{1,0:T(8,128)(2,1)S(1)}, bf16[8,4096]{1,0:T(8,128)(2,1)S(1)}, u32[]{:S(2)}, u32[]{:S(2)}) collective-permute-start(bf16[8,4096]{1,0:T(8,128)(2,1)S(1)} %slice.3), channel_id=1, source_target_pairs={{0,4},{4,0},{8,12},{12,8},{16,20},{20,16},{24,28},{28,24},{1,5},{5... | collective-permute-start | bytes 196616 | tf_op jit(solution)/shard_map/ppermute | solution.py:629
  4.4 3.6 %collective-permute-start.1 = (bf16[8,4096]{1,0:T(8,128)(2,1)S(1)}, bf16[8,4096]{1,0:T(8,128)(2,1)S(1)}, u32[]{:S(2)}, u32[]{:S(2)}) collective-permute-start(bf16[8,4096]{1,0:T(8,128)(2,1)S(1)} %slice.3), channel_id=1, source_target_pairs={{4,8},{8,4},{12,16},{16,12},{20,24},{24,20},{5,9},{9,5},{13,17},{1... | collective-permute-start | bytes 196616 | tf_op jit(solution)/shard_map/ppermute | solution.py:629
  8.0 5.5 %copy-start.4 = (f32[16,4096]{1,0:T(8,128)S(1)}, f32[16,4096]{1,0:T(8,128)}, u32[]{:S(2)}) copy-start(f32[16,4096]{1,0:T(8,128)} %param.15) | copy-start | bytes 786436
  8.0 10.9 %copy-start = (bf16[512,4096]{1,0:T(8,128)(2,1)S(1)}, bf16[512,4096]{1,0:T(8,128)(2,1)}, u32[]{:S(2)}) copy-start(bf16[512,4096]{1,0:T(8,128)(2,1)} %refs_3_.3) | copy-start | bytes 12582916
  8.0 10.9 %copy-start.1 = (bf16[128,4096]{1,0:T(8,128)(2,1)S(1)}, bf16[128,4096]{1,0:T(8,128)(2,1)}, u32[]{:S(2)}) copy-start(bf16[128,4096]{1,0:T(8,128)(2,1)} %refs_5_.3) | copy-start | bytes 3145732
  8.0 10.9 %copy-start.2 = (f32[4096]{0:T(1024)S(1)}, f32[4096]{0:T(1024)}, u32[]{:S(2)}) copy-start(f32[4096]{0:T(1024)} %param.14) | copy-start | bytes 49156
  8.0 10.9 %copy-start.3 = (f32[4096]{0:T(1024)S(1)}, f32[4096]{0:T(1024)}, u32[]{:S(2)}) copy-start(f32[4096]{0:T(1024)} %param.16) | copy-start | bytes 49156
  10.1 1.7 %collective-permute-start.2 = (f32[128,544]{1,0:T(8,128)S(1)}, f32[128,544]{1,0:T(8,128)S(1)}, u32[]{:S(2)}, u32[]{:S(2)}) collective-permute-start(f32[128,544]{1,0:T(8,128)S(1)} %get-tuple-element.54.a_ref), channel_id=1, source_target_pairs={{0,1},{1,0},{2,3},{3,2},{4,5},{5,4},{6,7},{7,6},{8,9},{9,8},{10,11... | collective-permute-start | bytes 835592 | tf_op jit(solution)/shard_map/ppermute | solution.py:21
  11.9 6.3 %collective-permute-start.3 = (bf16[128,576]{1,0:T(8,128)(2,1)S(1)}, bf16[128,576]{1,0:T(8,128)(2,1)S(1)}, u32[]{:S(2)}, u32[]{:S(2)}) collective-permute-start(bf16[128,576]{1,0:T(8,128)(2,1)S(1)} %add_first.1.mine_ref), channel_id=1, source_target_pairs={{0,2},{1,3},{2,0},{3,1},{4,6},{5,7},{6,4},{7,5},{8,10},{9,11},{10,... | collective-permute-start | bytes 442376 | tf_op jit(solution)/shard_map/ppermute | solution.py:21
  24.8 10.2 %collective-permute-start.7 = (bf16[16,2304]{1,0:T(8,128)(2,1)S(1)}, bf16[16,2304]{1,0:T(8,128)(2,1)S(1)}, u32[]{:S(2)}, u32[]{:S(2)}) collective-permute-start(bf16[16,2304]{1,0:T(8,128)(2,1)S(1)} %get-tuple-element.78), channel_id=1, source_target_pairs={{0,4},{4,0},{8,12},{12,8},{16,20},{20,16},{24,28},{28,24},{1,5},{5... | collective-permute-start | bytes 221192 | tf_op jit(solution)/shard_map/ppermute | solution.py:21
  34.9 4.4 %collective-permute-start.4 = (bf16[16,2304]{1,0:T(8,128)(2,1)S(1)}, bf16[16,2304]{1,0:T(8,128)(2,1)S(1)}, u32[]{:S(2)}, u32[]{:S(2)}) collective-permute-start(bf16[16,2304]{1,0:T(8,128)(2,1)S(1)} %get-tuple-element.63), channel_id=1, source_target_pairs={{0,4},{4,0},{8,12},{12,8},{16,20},{20,16},{24,28},{28,24},{1,5},{5... | collective-permute-start | bytes 221192 | tf_op jit(solution)/shard_map/ppermute | solution.py:21
  35.1 5.9 %collective-permute-start.8 = (bf16[16,2304]{1,0:T(8,128)(2,1)S(1)}, bf16[16,2304]{1,0:T(8,128)(2,1)S(1)}, u32[]{:S(2)}, u32[]{:S(2)}) collective-permute-start(bf16[16,2304]{1,0:T(8,128)(2,1)S(1)} %get-tuple-element.81), channel_id=1, source_target_pairs={{0,8},{4,12},{8,0},{12,4},{16,24},{20,28},{24,16},{28,20},{1,9},{5... | collective-permute-start | bytes 221192 | tf_op jit(solution)/shard_map/ppermute | solution.py:21
  39.4 4.8 %collective-permute-start.5 = (bf16[16,2304]{1,0:T(8,128)(2,1)S(1)}, bf16[16,2304]{1,0:T(8,128)(2,1)S(1)}, u32[]{:S(2)}, u32[]{:S(2)}) collective-permute-start(bf16[16,2304]{1,0:T(8,128)(2,1)S(1)} %get-tuple-element.66), channel_id=1, source_target_pairs={{0,8},{4,12},{8,0},{12,4},{16,24},{20,28},{24,16},{28,20},{1,9},{5... | collective-permute-start | bytes 221192 | tf_op jit(solution)/shard_map/ppermute | solution.py:21
  41.1 7.2 %collective-permute-start.9 = (bf16[16,2304]{1,0:T(8,128)(2,1)S(1)}, bf16[16,2304]{1,0:T(8,128)(2,1)S(1)}, u32[]{:S(2)}, u32[]{:S(2)}) collective-permute-start(bf16[16,2304]{1,0:T(8,128)(2,1)S(1)} %get-tuple-element.86), channel_id=1, source_target_pairs={{0,16},{4,20},{8,24},{12,28},{16,0},{20,4},{24,8},{28,12},{1,17},{... | collective-permute-start | bytes 221192 | tf_op jit(solution)/shard_map/ppermute | solution.py:21
  44.3 8.2 %collective-permute-start.6 = (bf16[16,2304]{1,0:T(8,128)(2,1)S(1)}, bf16[16,2304]{1,0:T(8,128)(2,1)S(1)}, u32[]{:S(2)}, u32[]{:S(2)}) collective-permute-start(bf16[16,2304]{1,0:T(8,128)(2,1)S(1)} %get-tuple-element.71), channel_id=1, source_target_pairs={{0,16},{4,20},{8,24},{12,28},{16,0},{20,4},{24,8},{28,12},{1,17},{... | collective-permute-start | bytes 221192 | tf_op jit(solution)/shard_map/ppermute | solution.py:21
  56.8 1.9 %collective-permute-start.10 = (f32[16,128]{1,0:T(8,128)S(1)}, f32[16,128]{1,0:T(8,128)S(1)}, u32[]{:S(2)}, u32[]{:S(2)}) collective-permute-start(f32[16,128]{1,0:T(8,128)S(1)} %get-tuple-element.95.refs_0_), channel_id=1, source_target_pairs={{0,1},{1,0},{2,3},{3,2},{4,5},{5,4},{6,7},{7,6},{8,9},{9,8},{10,11... | collective-permute-start | bytes 24584 | tf_op jit(solution)/shard_map/ppermute | solution.py:21
  56.8 3.7 %collective-permute-start.11 = (f32[16,128]{1,0:T(8,128)S(1)}, f32[16,128]{1,0:T(8,128)S(1)}, u32[]{:S(2)}, u32[]{:S(2)}) collective-permute-start(f32[16,128]{1,0:T(8,128)S(1)} %get-tuple-element.95.refs_0_), channel_id=1, source_target_pairs={{0,2},{1,3},{2,0},{3,1},{4,6},{5,7},{6,4},{7,5},{8,10},{9,11},{10,... | collective-permute-start | bytes 24584 | tf_op jit(solution)/shard_map/ppermute | solution.py:21
  58.3 3.1 %collective-permute-start.12 = (f32[16,128]{1,0:T(8,128)S(1)}, f32[16,128]{1,0:T(8,128)S(1)}, u32[]{:S(2)}, u32[]{:S(2)}) collective-permute-start(f32[16,128]{1,0:T(8,128)S(1)} %get-tuple-element.95.refs_0_), channel_id=1, source_target_pairs={{0,3},{1,2},{2,1},{3,0},{4,7},{5,6},{6,5},{7,4},{8,11},{9,10},{10,... | collective-permute-start | bytes 24584 | tf_op jit(solution)/shard_map/ppermute | solution.py:21
